TPU v7x, 32 devices: a whole 2x2x4 slice. The times are simulated.
32 devices in a mesh: wl: 4 (over x, core), gx: 2 (over y), gy: 4 (over z).
Axes of the slice: x: 2, y: 2, z: 4, core: 2. Of those that a mesh axis runs over, the one named last changes fastest.
Arguments:
- forward_efield: float32 [4, 3, 64, 32, 128], P('wl', None, 'gx', 'gy'), may hold values from -6 to 6
- forward_hfield: float32 [4, 3, 64, 32, 128], P('wl', None, 'gx', 'gy'), may hold values from -6 to 6
- adjoint_efield: float32 [4, 3, 64, 32, 128], P('wl', None, 'gx', 'gy'), may hold values from -6 to 6
- adjoint_hfield: float32 [4, 3, 64, 32, 128], P('wl', None, 'gx', 'gy'), may hold values from -6 to 6
- background: float32 [64, 32, 128], P('gx', 'gy'), may hold values from 1 to 4
- design: float32 [8, 64, 32], P('wl', 'gx', 'gy'), may hold values from 1.5 to 6
- source_profile: float32 [4, 64, 32], P('wl', 'gx', 'gy'), may hold values from -24 to 24
- source_layer: int32 [4], P('wl'), may hold values from 4 to 59
- monitor_layer: int32 [4], P('wl'), may hold values from 76 to 123
Outputs:
- final_forward: float32 [4, 3, 64, 32, 128], P('wl', None, 'gx', 'gy')
- final_adjoint: float32 [4, 3, 64, 32, 128], P('wl', None, 'gx', 'gy')
- gradient: float32 [8, 64, 32], P('wl', 'gx', 'gy')
Inputs may be any that keep to these rules, and one draw needn't show every extreme that they name: `source_layer`: a z layer below the design slab. `monitor_layer`: a z layer above the design slab.
All inputs are finite; a program needn't handle non-finite values.
Results may differ from a plain program's by a relative error of at most 0.0001.
Values sent between devices are 32-bit elements; how exact they have to be, the bound alone decides.
No kernel may reach another device: no remote copies, remote signals or barrier semaphores. Data moves between devices by JAX's collectives and lax.ppermute only.
A program may use at most 64 MiB of HBM per device.

v0:
```python
import math

import jax
import jax.numpy as jnp
from jax import lax
from jax.sharding import PartitionSpec as P

Z0 = 64
STEPS = 3


time_step = 0.5


def shifted_2(block, axis, distance):
    devices = range(lax.axis_size(axis))
    route = [(i - distance, i) for i in devices if i - distance in devices]
    return lax.ppermute(block, axis, route)


def neighbours(stacked, upward):
    offset = -1 if upward else 1
    plane_x = stacked[:, :1] if upward else stacked[:, -1:]
    plane_y = stacked[:, :, :1] if upward else stacked[:, :, -1:]
    got_x = shifted_2(plane_x, "gx", offset)
    got_y = shifted_2(plane_y, "gy", offset)
    return (got_x, got_y)


def along(stacked, axis, edge, upward):
    count = stacked.shape[axis]
    if upward:
        shifted = jnp.concatenate([lax.slice_in_dim(stacked, 1, count, axis=axis), edge], axis=axis)
        return shifted - stacked
    shifted = jnp.concatenate([edge, lax.slice_in_dim(stacked, 0, count - 1, axis=axis)], axis=axis)
    return stacked - shifted


def curl(stacked, upward):
    comps, width, height, depth = stacked.shape
    edge_x, edge_y = neighbours(stacked, upward)
    edge_z = jnp.zeros((comps, width, height, 1), jnp.float32)
    along_x = along(stacked, 1, edge_x, upward)
    along_y = along(stacked, 2, edge_y, upward)
    along_z = along(stacked, 3, edge_z, upward)
    return jnp.stack([along_y[2] - along_z[1], along_z[0] - along_x[2], along_x[1] - along_y[0]])


def run_window(efield, hfield, adj_e, adj_h, coef, source_term, omega, monitor_mask, slab_depth):
    slabs = []
    monitors = []
    monitor_pick = monitor_mask[None, None, None, :]
    for turn in range(STEPS):
        hfield = hfield - time_step * curl(efield, True)
        efield = efield + coef * curl(hfield, False)
        signal = jnp.sin(omega * ((turn + 1) * time_step))
        efield = efield.at[0].add(time_step * signal * source_term)
        slabs.append(efield[:, :, :, Z0 : Z0 + slab_depth])
        monitors.append(jnp.sum(efield * monitor_pick, axis=3, keepdims=True))
    total = jnp.zeros((efield.shape[1], efield.shape[2], slab_depth), jnp.float32)
    for turn in range(STEPS):
        adj_h = adj_h - time_step * curl(adj_e, True)
        adj_e = adj_e + coef * curl(adj_h, False)
        adj_e = adj_e + 2.0 * time_step * monitors[STEPS - 1 - turn] * monitor_mask
        total = total + jnp.sum(
            slabs[STEPS - 1 - turn] * adj_e[:, :, :, Z0 : Z0 + slab_depth], axis=0
        )
    return (efield, adj_e, total)


def per_device(
    forward_efield,
    forward_hfield,
    adjoint_efield,
    adjoint_hfield,
    background,
    design,
    source_profile,
    source_layer,
    monitor_layer,
):
    groups = lax.axis_size("wl")
    owned = design.shape[0]
    slab_depth = owned * groups
    depth = background.shape[2]
    tiles = lax.all_gather(design, "wl", axis=0, tiled=True)
    permit = jnp.concatenate(
        [
            background[:, :, :Z0],
            jnp.transpose(tiles, (1, 2, 0)),
            background[:, :, Z0 + slab_depth :],
        ],
        axis=2,
    )
    layers = lax.iota(jnp.int32, depth)
    wave_index = lax.axis_index("wl").astype(jnp.float32)
    omega = jnp.float32(2.0 * math.pi) / (16.0 + 32.0 * wave_index / groups)
    source_mask = (layers == source_layer[0]).astype(jnp.float32)
    monitor_mask = (layers == monitor_layer[0]).astype(jnp.float32)
    source_term = source_profile[0][:, :, None] * source_mask
    coef = time_step / permit
    efield, adj_e, total = run_window(
        forward_efield[0],
        forward_hfield[0],
        adjoint_efield[0],
        adjoint_hfield[0],
        coef,
        source_term,
        omega,
        monitor_mask,
        slab_depth,
    )
    local_grad = jnp.transpose(omega * omega * total, (2, 0, 1))
    summed = lax.psum(local_grad, "wl")
    gradient = lax.dynamic_slice_in_dim(summed, lax.axis_index("wl") * owned, owned, 0)
    return (efield[None], adj_e[None], gradient)


def solution(mesh):
    return jax.shard_map(
        per_device,
        mesh=mesh,
        in_specs=(
            P("wl", None, "gx", "gy", None),
            P("wl", None, "gx", "gy", None),
            P("wl", None, "gx", "gy", None),
            P("wl", None, "gx", "gy", None),
            P("gx", "gy", None),
            P("wl", "gx", "gy"),
            P("wl", "gx", "gy"),
            P("wl"),
            P("wl"),
        ),
        out_specs=(
            P("wl", None, "gx", "gy", None),
            P("wl", None, "gx", "gy", None),
            P("wl", "gx", "gy"),
        ),
        check_vma=False,
    )
```

profile of v0, /device:TPU:0, one launch (start us, length us, event | category | flops | bytes accessed | tf_op | source)
XLA Modules:
  0.0 120.3 jit_solution(9037135590626028653)
XLA Ops:
  1.7 1.3 %collective-permute-start = (f32[3,32,1,128]{3,2,1,0:T(1,128)S(1)}, f32[3,32,1,128]{3,2,1,0:T(1,128)S(1)}, u32[]{:S(2)}, u32[]{:S(2)}) collective-permute-start(f32[3,32,1,128]{3,2,1,0:T(1,128)S(1)} %slice.645), channel_id=1, source_target_pairs={{1,0},{2,1},{3,2},{5,4},{6,5},{7,6},{9,8},{10,9},{11,10},{13,12},{... | collective-permute-start | bytes 147464 | tf_op jit(solution)/shard_map/ppermute | solution.py:18
  3.7 1.3 %collective-permute-start.1 = (f32[3,1,8,128]{3,2,1,0:T(8,128)S(1)}, f32[3,1,8,128]{3,2,1,0:T(8,128)S(1)}, u32[]{:S(2)}, u32[]{:S(2)}) collective-permute-start(f32[3,1,8,128]{3,2,1,0:T(8,128)S(1)} %slice.651), channel_id=1, source_target_pairs={{4,0},{5,1},{6,2},{7,3},{12,8},{13,9},{14,10},{15,11},{20,16},{21,... | collective-permute-start | bytes 36872 | tf_op jit(solution)/shard_map/ppermute | solution.py:18
  6.0 1.4 %collective-permute-start.12 = (f32[3,32,1,128]{3,2,1,0:T(1,128)S(1)}, f32[3,32,1,128]{3,2,1,0:T(1,128)S(1)}, u32[]{:S(2)}, u32[]{:S(2)}) collective-permute-start(f32[3,32,1,128]{3,2,1,0:T(1,128)S(1)} %slice.714), channel_id=1, source_target_pairs={{1,0},{2,1},{3,2},{5,4},{6,5},{7,6},{9,8},{10,9},{11,10},{13,12},{... | collective-permute-start | bytes 147464 | tf_op jit(solution)/shard_map/ppermute | solution.py:18
  8.2 1.3 %collective-permute-start.13 = (f32[3,1,8,128]{3,2,1,0:T(8,128)S(1)}, f32[3,1,8,128]{3,2,1,0:T(8,128)S(1)}, u32[]{:S(2)}, u32[]{:S(2)}) collective-permute-start(f32[3,1,8,128]{3,2,1,0:T(8,128)S(1)} %slice.720), channel_id=1, source_target_pairs={{4,0},{5,1},{6,2},{7,3},{12,8},{13,9},{14,10},{15,11},{20,16},{21,... | collective-permute-start | bytes 36872 | tf_op jit(solution)/shard_map/ppermute | solution.py:18
  9.5 6.2 %all_gather.3 = f32[8,32,8]{1,2,0:T(8,128)S(1)} all-gather(f32[2,32,8]{1,2,0:T(8,128)S(1)} %copy-done.26), channel_id=1, replica_groups=mesh['wl'=4,'gx'=2,'gy'=4] {'wl'}, dimensions={0}, use_global_device_ids=true | all-gather | bytes 10240 | tf_op jit(solution)/shard_map/all_gather | solution.py:86
  21.1 5.2 %collective-permute-start.2 = (f32[3,32,1,128]{3,2,1,0:T(1,128)S(1)}, f32[3,32,1,128]{3,2,1,0:T(1,128)S(1)}, u32[]{:S(2)}, u32[]{:S(2)}) collective-permute-start(f32[3,32,1,128]{3,2,1,0:T(1,128)S(1)} %slice.655), channel_id=1, source_target_pairs={{0,1},{1,2},{2,3},{4,5},{5,6},{6,7},{8,9},{9,10},{10,11},{12,13},{... | collective-permute-start | bytes 147464 | tf_op jit(solution)/shard_map/ppermute | solution.py:18
  26.3 4.5 %collective-permute-start.3 = (f32[3,1,8,128]{3,2,1,0:T(8,128)S(1)}, f32[3,1,8,128]{3,2,1,0:T(8,128)S(1)}, u32[]{:S(2)}, u32[]{:S(2)}) collective-permute-start(f32[3,1,8,128]{3,2,1,0:T(8,128)S(1)} %slice.661), channel_id=1, source_target_pairs={{0,4},{1,5},{2,6},{3,7},{8,12},{9,13},{10,14},{11,15},{16,20},{17,... | collective-permute-start | bytes 36872 | tf_op jit(solution)/shard_map/ppermute | solution.py:18
  32.7 1.3 %collective-permute-start.4 = (f32[3,32,1,128]{3,2,1,0:T(1,128)S(1)}, f32[3,32,1,128]{3,2,1,0:T(1,128)S(1)}, u32[]{:S(2)}, u32[]{:S(2)}) collective-permute-start(f32[3,32,1,128]{3,2,1,0:T(1,128)S(1)} %slice.668), channel_id=1, source_target_pairs={{1,0},{2,1},{3,2},{5,4},{6,5},{7,6},{9,8},{10,9},{11,10},{13,12},{... | collective-permute-start | bytes 147464 | tf_op jit(solution)/shard_map/ppermute | solution.py:18
  34.0 1.3 %collective-permute-start.5 = (f32[3,1,8,128]{3,2,1,0:T(8,128)S(1)}, f32[3,1,8,128]{3,2,1,0:T(8,128)S(1)}, u32[]{:S(2)}, u32[]{:S(2)}) collective-permute-start(f32[3,1,8,128]{3,2,1,0:T(8,128)S(1)} %slice.674), channel_id=1, source_target_pairs={{4,0},{5,1},{6,2},{7,3},{12,8},{13,9},{14,10},{15,11},{20,16},{21,... | collective-permute-start | bytes 36872 | tf_op jit(solution)/shard_map/ppermute | solution.py:18
  35.6 4.0 %collective-permute-done.5 = f32[3,1,8,128]{3,2,1,0:T(8,128)S(1)} collective-permute-done((f32[3,1,8,128]{3,2,1,0:T(8,128)S(1)}, f32[3,1,8,128]{3,2,1,0:T(8,128)S(1)}, u32[]{:S(2)}, u32[]{:S(2)}) %collective-permute-start.5) | collective-permute-done | bytes 12320 | tf_op jit(solution)/shard_map/ppermute | solution.py:18
  40.0 4.6 %collective-permute-start.6 = (f32[3,32,1,128]{3,2,1,0:T(1,128)S(1)}, f32[3,32,1,128]{3,2,1,0:T(1,128)S(1)}, u32[]{:S(2)}, u32[]{:S(2)}) collective-permute-start(f32[3,32,1,128]{3,2,1,0:T(1,128)S(1)} %slice.678), channel_id=1, source_target_pairs={{0,1},{1,2},{2,3},{4,5},{5,6},{6,7},{8,9},{9,10},{10,11},{12,13},{... | collective-permute-start | bytes 147464 | tf_op jit(solution)/shard_map/ppermute | solution.py:18
  44.5 2.7 %collective-permute-start.7 = (f32[3,1,8,128]{3,2,1,0:T(8,128)S(1)}, f32[3,1,8,128]{3,2,1,0:T(8,128)S(1)}, u32[]{:S(2)}, u32[]{:S(2)}) collective-permute-start(f32[3,1,8,128]{3,2,1,0:T(8,128)S(1)} %slice.684), channel_id=1, source_target_pairs={{0,4},{1,5},{2,6},{3,7},{8,12},{9,13},{10,14},{11,15},{16,20},{17,... | collective-permute-start | bytes 36872 | tf_op jit(solution)/shard_map/ppermute | solution.py:18
  47.4 3.9 %collective-permute-start.14 = (f32[3,32,1,128]{3,2,1,0:T(1,128)S(1)}, f32[3,32,1,128]{3,2,1,0:T(1,128)S(1)}, u32[]{:S(2)}, u32[]{:S(2)}) collective-permute-start(f32[3,32,1,128]{3,2,1,0:T(1,128)S(1)} %slice.724), channel_id=1, source_target_pairs={{0,1},{1,2},{2,3},{4,5},{5,6},{6,7},{8,9},{9,10},{10,11},{12,13},{... | collective-permute-start | bytes 147464 | tf_op jit(solution)/shard_map/ppermute | solution.py:18
  51.3 1.3 %collective-permute-start.15 = (f32[3,1,8,128]{3,2,1,0:T(8,128)S(1)}, f32[3,1,8,128]{3,2,1,0:T(8,128)S(1)}, u32[]{:S(2)}, u32[]{:S(2)}) collective-permute-start(f32[3,1,8,128]{3,2,1,0:T(8,128)S(1)} %slice.730), channel_id=1, source_target_pairs={{0,4},{1,5},{2,6},{3,7},{8,12},{9,13},{10,14},{11,15},{16,20},{17,... | collective-permute-start | bytes 36872 | tf_op jit(solution)/shard_map/ppermute | solution.py:18
  53.1 1.3 %collective-permute-start.8 = (f32[3,32,1,128]{3,2,1,0:T(1,128)S(1)}, f32[3,32,1,128]{3,2,1,0:T(1,128)S(1)}, u32[]{:S(2)}, u32[]{:S(2)}) collective-permute-start(f32[3,32,1,128]{3,2,1,0:T(1,128)S(1)} %slice.691), channel_id=1, source_target_pairs={{1,0},{2,1},{3,2},{5,4},{6,5},{7,6},{9,8},{10,9},{11,10},{13,12},{... | collective-permute-start | bytes 147464 | tf_op jit(solution)/shard_map/ppermute | solution.py:18
  54.4 1.3 %collective-permute-start.9 = (f32[3,1,8,128]{3,2,1,0:T(8,128)S(1)}, f32[3,1,8,128]{3,2,1,0:T(8,128)S(1)}, u32[]{:S(2)}, u32[]{:S(2)}) collective-permute-start(f32[3,1,8,128]{3,2,1,0:T(8,128)S(1)} %slice.697), channel_id=1, source_target_pairs={{4,0},{5,1},{6,2},{7,3},{12,8},{13,9},{14,10},{15,11},{20,16},{21,... | collective-permute-start | bytes 36872 | tf_op jit(solution)/shard_map/ppermute | solution.py:18
  56.2 3.8 %collective-permute-done.9 = f32[3,1,8,128]{3,2,1,0:T(8,128)S(1)} collective-permute-done((f32[3,1,8,128]{3,2,1,0:T(8,128)S(1)}, f32[3,1,8,128]{3,2,1,0:T(8,128)S(1)}, u32[]{:S(2)}, u32[]{:S(2)}) %collective-permute-start.9) | collective-permute-done | bytes 12320 | tf_op jit(solution)/shard_map/ppermute | solution.py:18
  60.4 4.5 %collective-permute-start.10 = (f32[3,32,1,128]{3,2,1,0:T(1,128)S(1)}, f32[3,32,1,128]{3,2,1,0:T(1,128)S(1)}, u32[]{:S(2)}, u32[]{:S(2)}) collective-permute-start(f32[3,32,1,128]{3,2,1,0:T(1,128)S(1)} %slice.701), channel_id=1, source_target_pairs={{0,1},{1,2},{2,3},{4,5},{5,6},{6,7},{8,9},{9,10},{10,11},{12,13},{... | collective-permute-start | bytes 147464 | tf_op jit(solution)/shard_map/ppermute | solution.py:18
  64.9 1.6 %collective-permute-start.11 = (f32[3,1,8,128]{3,2,1,0:T(8,128)S(1)}, f32[3,1,8,128]{3,2,1,0:T(8,128)S(1)}, u32[]{:S(2)}, u32[]{:S(2)}) collective-permute-start(f32[3,1,8,128]{3,2,1,0:T(8,128)S(1)} %slice.707), channel_id=1, source_target_pairs={{0,4},{1,5},{2,6},{3,7},{8,12},{9,13},{10,14},{11,15},{16,20},{17,... | collective-permute-start | bytes 36872 | tf_op jit(solution)/shard_map/ppermute | solution.py:18
  66.7 1.3 %collective-permute-done.11 = f32[3,1,8,128]{3,2,1,0:T(8,128)S(1)} collective-permute-done((f32[3,1,8,128]{3,2,1,0:T(8,128)S(1)}, f32[3,1,8,128]{3,2,1,0:T(8,128)S(1)}, u32[]{:S(2)}, u32[]{:S(2)}) %collective-permute-start.11) | collective-permute-done | bytes 12320 | tf_op jit(solution)/shard_map/ppermute | solution.py:18
  69.5 1.3 %collective-permute-start.16 = (f32[3,32,1,128]{3,2,1,0:T(1,128)S(1)}, f32[3,32,1,128]{3,2,1,0:T(1,128)S(1)}, u32[]{:S(2)}, u32[]{:S(2)}) collective-permute-start(f32[3,32,1,128]{3,2,1,0:T(1,128)S(1)} %slice.736), channel_id=1, source_target_pairs={{1,0},{2,1},{3,2},{5,4},{6,5},{7,6},{9,8},{10,9},{11,10},{13,12},{... | collective-permute-start | bytes 147464 | tf_op jit(solution)/shard_map/ppermute | solution.py:18
  70.8 1.3 %collective-permute-start.17 = (f32[3,1,8,128]{3,2,1,0:T(8,128)S(1)}, f32[3,1,8,128]{3,2,1,0:T(8,128)S(1)}, u32[]{:S(2)}, u32[]{:S(2)}) collective-permute-start(f32[3,1,8,128]{3,2,1,0:T(8,128)S(1)} %slice.742), channel_id=1, source_target_pairs={{4,0},{5,1},{6,2},{7,3},{12,8},{13,9},{14,10},{15,11},{20,16},{21,... | collective-permute-start | bytes 36872 | tf_op jit(solution)/shard_map/ppermute | solution.py:18
  72.4 4.0 %collective-permute-done.17 = f32[3,1,8,128]{3,2,1,0:T(8,128)S(1)} collective-permute-done((f32[3,1,8,128]{3,2,1,0:T(8,128)S(1)}, f32[3,1,8,128]{3,2,1,0:T(8,128)S(1)}, u32[]{:S(2)}, u32[]{:S(2)}) %collective-permute-start.17) | collective-permute-done | bytes 12320 | tf_op jit(solution)/shard_map/ppermute | solution.py:18
  76.9 4.5 %collective-permute-start.18 = (f32[3,32,1,128]{3,2,1,0:T(1,128)S(1)}, f32[3,32,1,128]{3,2,1,0:T(1,128)S(1)}, u32[]{:S(2)}, u32[]{:S(2)}) collective-permute-start(f32[3,32,1,128]{3,2,1,0:T(1,128)S(1)} %slice.746), channel_id=1, source_target_pairs={{0,1},{1,2},{2,3},{4,5},{5,6},{6,7},{8,9},{9,10},{10,11},{12,13},{... | collective-permute-start | bytes 147464 | tf_op jit(solution)/shard_map/ppermute | solution.py:18
  81.4 1.6 %collective-permute-start.19 = (f32[3,1,8,128]{3,2,1,0:T(8,128)S(1)}, f32[3,1,8,128]{3,2,1,0:T(8,128)S(1)}, u32[]{:S(2)}, u32[]{:S(2)}) collective-permute-start(f32[3,1,8,128]{3,2,1,0:T(8,128)S(1)} %slice.752), channel_id=1, source_target_pairs={{0,4},{1,5},{2,6},{3,7},{8,12},{9,13},{10,14},{11,15},{16,20},{17,... | collective-permute-start | bytes 36872 | tf_op jit(solution)/shard_map/ppermute | solution.py:18
  83.1 1.4 %collective-permute-done.19 = f32[3,1,8,128]{3,2,1,0:T(8,128)S(1)} collective-permute-done((f32[3,1,8,128]{3,2,1,0:T(8,128)S(1)}, f32[3,1,8,128]{3,2,1,0:T(8,128)S(1)}, u32[]{:S(2)}, u32[]{:S(2)}) %collective-permute-start.19) | collective-permute-done | bytes 12320 | tf_op jit(solution)/shard_map/ppermute | solution.py:18
  86.1 1.3 %collective-permute-start.20 = (f32[3,32,1,128]{3,2,1,0:T(1,128)}, f32[3,32,1,128]{3,2,1,0:T(1,128)}, u32[]{:S(2)}, u32[]{:S(2)}) collective-permute-start(f32[3,32,1,128]{3,2,1,0:T(1,128)} %slice.758), channel_id=1, source_target_pairs={{1,0},{2,1},{3,2},{5,4},{6,5},{7,6},{9,8},{10,9},{11,10},{13,12},{... | collective-permute-start | bytes 147464 | tf_op jit(solution)/shard_map/ppermute | solution.py:18
  87.4 1.3 %collective-permute-start.21 = (f32[3,1,8,128]{3,2,1,0:T(8,128)S(1)}, f32[3,1,8,128]{3,2,1,0:T(8,128)}, u32[]{:S(2)}, u32[]{:S(2)}) collective-permute-start(f32[3,1,8,128]{3,2,1,0:T(8,128)S(1)} %slice.764), channel_id=1, source_target_pairs={{4,0},{5,1},{6,2},{7,3},{12,8},{13,9},{14,10},{15,11},{20,16},{21,... | collective-permute-start | bytes 36872 | tf_op jit(solution)/shard_map/ppermute | solution.py:18
  90.4 2.8 %collective-permute-done.21 = f32[3,1,8,128]{3,2,1,0:T(8,128)} collective-permute-done((f32[3,1,8,128]{3,2,1,0:T(8,128)S(1)}, f32[3,1,8,128]{3,2,1,0:T(8,128)}, u32[]{:S(2)}, u32[]{:S(2)}) %collective-permute-start.21) | collective-permute-done | bytes 12320 | tf_op jit(solution)/shard_map/ppermute | solution.py:18
  95.4 4.5 %collective-permute-start.22 = (f32[3,32,1,128]{3,2,1,0:T(1,128)S(1)}, f32[3,32,1,128]{3,2,1,0:T(1,128)S(1)}, u32[]{:S(2)}, u32[]{:S(2)}) collective-permute-start(f32[3,32,1,128]{3,2,1,0:T(1,128)S(1)} %slice.768), channel_id=1, source_target_pairs={{0,1},{1,2},{2,3},{4,5},{5,6},{6,7},{8,9},{9,10},{10,11},{12,13},{... | collective-permute-start | bytes 147464 | tf_op jit(solution)/shard_map/ppermute | solution.py:18
  100.0 3.3 %collective-permute-start.23 = (f32[3,1,8,128]{3,2,1,0:T(8,128)S(1)}, f32[3,1,8,128]{3,2,1,0:T(8,128)S(1)}, u32[]{:S(2)}, u32[]{:S(2)}) collective-permute-start(f32[3,1,8,128]{3,2,1,0:T(8,128)S(1)} %slice.774), channel_id=1, source_target_pairs={{0,4},{1,5},{2,6},{3,7},{8,12},{9,13},{10,14},{11,15},{16,20},{17,... | collective-permute-start | bytes 36872 | tf_op jit(solution)/shard_map/ppermute | solution.py:18
  106.5 11.6 %psum.7 = f32[8,32,8]{0,2,1:T(8,128)S(1)} all-reduce(f32[8,32,8]{0,2,1:T(8,128)S(1)} %multiply_bitcast_fusion), channel_id=1, replica_groups=mesh['wl'=4,'gx'=2,'gy'=4] {'wl'}, use_global_device_ids=true, to_apply=%region_6.0 | all-reduce | flops 2048 | bytes 16384 | tf_op jit(solution)/shard_map/psum | solution.py:114
  (177 shorter events, 23.8 us)
Async XLA Ops:
  1.7 18.2 %collective-permute-start = (f32[3,32,1,128]{3,2,1,0:T(1,128)S(1)}, f32[3,32,1,128]{3,2,1,0:T(1,128)S(1)}, u32[]{:S(2)}, u32[]{:S(2)}) collective-permute-start(f32[3,32,1,128]{3,2,1,0:T(1,128)S(1)} %slice.645), channel_id=1, source_target_pairs={{1,0},{2,1},{3,2},{5,4},{6,5},{7,6},{9,8},{10,9},{11,10},{13,12},{... | collective-permute-start | bytes 147464 | tf_op jit(solution)/shard_map/ppermute | solution.py:18
  3.7 16.2 %collective-permute-start.1 = (f32[3,1,8,128]{3,2,1,0:T(8,128)S(1)}, f32[3,1,8,128]{3,2,1,0:T(8,128)S(1)}, u32[]{:S(2)}, u32[]{:S(2)}) collective-permute-start(f32[3,1,8,128]{3,2,1,0:T(8,128)S(1)} %slice.651), channel_id=1, source_target_pairs={{4,0},{5,1},{6,2},{7,3},{12,8},{13,9},{14,10},{15,11},{20,16},{21,... | collective-permute-start | bytes 36872 | tf_op jit(solution)/shard_map/ppermute | solution.py:18
  6.0 9.8 %copy-start.24 = (f32[32,8,128]{2,1,0:T(8,128)S(1)}, f32[32,8,128]{2,1,0:T(8,128)}, u32[]{:S(2)}) copy-start(f32[32,8,128]{2,1,0:T(8,128)} %param.19) | copy-start | bytes 393220
  6.0 24.9 %collective-permute-start.12 = (f32[3,32,1,128]{3,2,1,0:T(1,128)S(1)}, f32[3,32,1,128]{3,2,1,0:T(1,128)S(1)}, u32[]{:S(2)}, u32[]{:S(2)}) collective-permute-start(f32[3,32,1,128]{3,2,1,0:T(1,128)S(1)} %slice.714), channel_id=1, source_target_pairs={{1,0},{2,1},{3,2},{5,4},{6,5},{7,6},{9,8},{10,9},{11,10},{13,12},{... | collective-permute-start | bytes 147464 | tf_op jit(solution)/shard_map/ppermute | solution.py:18
  8.2 22.7 %collective-permute-start.13 = (f32[3,1,8,128]{3,2,1,0:T(8,128)S(1)}, f32[3,1,8,128]{3,2,1,0:T(8,128)S(1)}, u32[]{:S(2)}, u32[]{:S(2)}) collective-permute-start(f32[3,1,8,128]{3,2,1,0:T(8,128)S(1)} %slice.720), channel_id=1, source_target_pairs={{4,0},{5,1},{6,2},{7,3},{12,8},{13,9},{14,10},{15,11},{20,16},{21,... | collective-permute-start | bytes 36872 | tf_op jit(solution)/shard_map/ppermute | solution.py:18
  21.1 11.2 %collective-permute-start.2 = (f32[3,32,1,128]{3,2,1,0:T(1,128)S(1)}, f32[3,32,1,128]{3,2,1,0:T(1,128)S(1)}, u32[]{:S(2)}, u32[]{:S(2)}) collective-permute-start(f32[3,32,1,128]{3,2,1,0:T(1,128)S(1)} %slice.655), channel_id=1, source_target_pairs={{0,1},{1,2},{2,3},{4,5},{5,6},{6,7},{8,9},{9,10},{10,11},{12,13},{... | collective-permute-start | bytes 147464 | tf_op jit(solution)/shard_map/ppermute | solution.py:18
  26.3 5.9 %collective-permute-start.3 = (f32[3,1,8,128]{3,2,1,0:T(8,128)S(1)}, f32[3,1,8,128]{3,2,1,0:T(8,128)S(1)}, u32[]{:S(2)}, u32[]{:S(2)}) collective-permute-start(f32[3,1,8,128]{3,2,1,0:T(8,128)S(1)} %slice.661), channel_id=1, source_target_pairs={{0,4},{1,5},{2,6},{3,7},{8,12},{9,13},{10,14},{11,15},{16,20},{17,... | collective-permute-start | bytes 36872 | tf_op jit(solution)/shard_map/ppermute | solution.py:18
  32.7 6.9 %collective-permute-start.4 = (f32[3,32,1,128]{3,2,1,0:T(1,128)S(1)}, f32[3,32,1,128]{3,2,1,0:T(1,128)S(1)}, u32[]{:S(2)}, u32[]{:S(2)}) collective-permute-start(f32[3,32,1,128]{3,2,1,0:T(1,128)S(1)} %slice.668), channel_id=1, source_target_pairs={{1,0},{2,1},{3,2},{5,4},{6,5},{7,6},{9,8},{10,9},{11,10},{13,12},{... | collective-permute-start | bytes 147464 | tf_op jit(solution)/shard_map/ppermute | solution.py:18
  34.0 5.6 %collective-permute-start.5 = (f32[3,1,8,128]{3,2,1,0:T(8,128)S(1)}, f32[3,1,8,128]{3,2,1,0:T(8,128)S(1)}, u32[]{:S(2)}, u32[]{:S(2)}) collective-permute-start(f32[3,1,8,128]{3,2,1,0:T(8,128)S(1)} %slice.674), channel_id=1, source_target_pairs={{4,0},{5,1},{6,2},{7,3},{12,8},{13,9},{14,10},{15,11},{20,16},{21,... | collective-permute-start | bytes 36872 | tf_op jit(solution)/shard_map/ppermute | solution.py:18
  39.8 7.4 %copy-start.2 = (f32[1,3,32,8,128]{4,3,2,1,0:T(8,128)S(1)}, f32[1,3,32,8,128]{4,3,2,1,0:T(8,128)}, u32[]{:S(2)}) copy-start(f32[1,3,32,8,128]{4,3,2,1,0:T(8,128)} %param.18) | copy-start | bytes 1179652
  40.0 12.7 %collective-permute-start.6 = (f32[3,32,1,128]{3,2,1,0:T(1,128)S(1)}, f32[3,32,1,128]{3,2,1,0:T(1,128)S(1)}, u32[]{:S(2)}, u32[]{:S(2)}) collective-permute-start(f32[3,32,1,128]{3,2,1,0:T(1,128)S(1)} %slice.678), channel_id=1, source_target_pairs={{0,1},{1,2},{2,3},{4,5},{5,6},{6,7},{8,9},{9,10},{10,11},{12,13},{... | collective-permute-start | bytes 147464 | tf_op jit(solution)/shard_map/ppermute | solution.py:18
  44.5 8.1 %collective-permute-start.7 = (f32[3,1,8,128]{3,2,1,0:T(8,128)S(1)}, f32[3,1,8,128]{3,2,1,0:T(8,128)S(1)}, u32[]{:S(2)}, u32[]{:S(2)}) collective-permute-start(f32[3,1,8,128]{3,2,1,0:T(8,128)S(1)} %slice.684), channel_id=1, source_target_pairs={{0,4},{1,5},{2,6},{3,7},{8,12},{9,13},{10,14},{11,15},{16,20},{17,... | collective-permute-start | bytes 36872 | tf_op jit(solution)/shard_map/ppermute | solution.py:18
  47.4 8.4 %collective-permute-start.14 = (f32[3,32,1,128]{3,2,1,0:T(1,128)S(1)}, f32[3,32,1,128]{3,2,1,0:T(1,128)S(1)}, u32[]{:S(2)}, u32[]{:S(2)}) collective-permute-start(f32[3,32,1,128]{3,2,1,0:T(1,128)S(1)} %slice.724), channel_id=1, source_target_pairs={{0,1},{1,2},{2,3},{4,5},{5,6},{6,7},{8,9},{9,10},{10,11},{12,13},{... | collective-permute-start | bytes 147464 | tf_op jit(solution)/shard_map/ppermute | solution.py:18
  51.3 4.5 %collective-permute-start.15 = (f32[3,1,8,128]{3,2,1,0:T(8,128)S(1)}, f32[3,1,8,128]{3,2,1,0:T(8,128)S(1)}, u32[]{:S(2)}, u32[]{:S(2)}) collective-permute-start(f32[3,1,8,128]{3,2,1,0:T(8,128)S(1)} %slice.730), channel_id=1, source_target_pairs={{0,4},{1,5},{2,6},{3,7},{8,12},{9,13},{10,14},{11,15},{16,20},{17,... | collective-permute-start | bytes 36872 | tf_op jit(solution)/shard_map/ppermute | solution.py:18
  53.1 6.9 %collective-permute-start.8 = (f32[3,32,1,128]{3,2,1,0:T(1,128)S(1)}, f32[3,32,1,128]{3,2,1,0:T(1,128)S(1)}, u32[]{:S(2)}, u32[]{:S(2)}) collective-permute-start(f32[3,32,1,128]{3,2,1,0:T(1,128)S(1)} %slice.691), channel_id=1, source_target_pairs={{1,0},{2,1},{3,2},{5,4},{6,5},{7,6},{9,8},{10,9},{11,10},{13,12},{... | collective-permute-start | bytes 147464 | tf_op jit(solution)/shard_map/ppermute | solution.py:18
  54.4 5.6 %collective-permute-start.9 = (f32[3,1,8,128]{3,2,1,0:T(8,128)S(1)}, f32[3,1,8,128]{3,2,1,0:T(8,128)S(1)}, u32[]{:S(2)}, u32[]{:S(2)}) collective-permute-start(f32[3,1,8,128]{3,2,1,0:T(8,128)S(1)} %slice.697), channel_id=1, source_target_pairs={{4,0},{5,1},{6,2},{7,3},{12,8},{13,9},{14,10},{15,11},{20,16},{21,... | collective-permute-start | bytes 36872 | tf_op jit(solution)/shard_map/ppermute | solution.py:18
  60.4 7.6 %collective-permute-start.10 = (f32[3,32,1,128]{3,2,1,0:T(1,128)S(1)}, f32[3,32,1,128]{3,2,1,0:T(1,128)S(1)}, u32[]{:S(2)}, u32[]{:S(2)}) collective-permute-start(f32[3,32,1,128]{3,2,1,0:T(1,128)S(1)} %slice.701), channel_id=1, source_target_pairs={{0,1},{1,2},{2,3},{4,5},{5,6},{6,7},{8,9},{9,10},{10,11},{12,13},{... | collective-permute-start | bytes 147464 | tf_op jit(solution)/shard_map/ppermute | solution.py:18
  64.9 3.0 %collective-permute-start.11 = (f32[3,1,8,128]{3,2,1,0:T(8,128)S(1)}, f32[3,1,8,128]{3,2,1,0:T(8,128)S(1)}, u32[]{:S(2)}, u32[]{:S(2)}) collective-permute-start(f32[3,1,8,128]{3,2,1,0:T(8,128)S(1)} %slice.707), channel_id=1, source_target_pairs={{0,4},{1,5},{2,6},{3,7},{8,12},{9,13},{10,14},{11,15},{16,20},{17,... | collective-permute-start | bytes 36872 | tf_op jit(solution)/shard_map/ppermute | solution.py:18
  69.3 15.5 %copy-start.17 = (f32[3,32,8]{2,1,0:T(8,128)}, f32[3,32,8]{2,1,0:T(8,128)S(1)}, u32[]{:S(2)}) copy-start(f32[3,32,8]{2,1,0:T(8,128)S(1)} %get-tuple-element.46) | copy-start | bytes 9220
  69.3 15.5 %copy-start.20 = (f32[3,32,8]{2,1,0:T(8,128)}, f32[3,32,8]{2,1,0:T(8,128)S(1)}, u32[]{:S(2)}) copy-start(f32[3,32,8]{2,1,0:T(8,128)S(1)} %get-tuple-element.45) | copy-start | bytes 9220
  69.5 6.9 %collective-permute-start.16 = (f32[3,32,1,128]{3,2,1,0:T(1,128)S(1)}, f32[3,32,1,128]{3,2,1,0:T(1,128)S(1)}, u32[]{:S(2)}, u32[]{:S(2)}) collective-permute-start(f32[3,32,1,128]{3,2,1,0:T(1,128)S(1)} %slice.736), channel_id=1, source_target_pairs={{1,0},{2,1},{3,2},{5,4},{6,5},{7,6},{9,8},{10,9},{11,10},{13,12},{... | collective-permute-start | bytes 147464 | tf_op jit(solution)/shard_map/ppermute | solution.py:18
  70.8 5.6 %collective-permute-start.17 = (f32[3,1,8,128]{3,2,1,0:T(8,128)S(1)}, f32[3,1,8,128]{3,2,1,0:T(8,128)S(1)}, u32[]{:S(2)}, u32[]{:S(2)}) collective-permute-start(f32[3,1,8,128]{3,2,1,0:T(8,128)S(1)} %slice.742), channel_id=1, source_target_pairs={{4,0},{5,1},{6,2},{7,3},{12,8},{13,9},{14,10},{15,11},{20,16},{21,... | collective-permute-start | bytes 36872 | tf_op jit(solution)/shard_map/ppermute | solution.py:18
  76.7 7.7 %copy-start.6 = (f32[1,32,8,128]{3,2,1,0:T(8,128)}, f32[1,32,8,128]{3,2,1,0:T(8,128)S(1)}, u32[]{:S(2)}) copy-start(f32[1,32,8,128]{3,2,1,0:T(8,128)S(1)} %get-tuple-element.67) | copy-start | bytes 393220
  76.9 7.6 %collective-permute-start.18 = (f32[3,32,1,128]{3,2,1,0:T(1,128)S(1)}, f32[3,32,1,128]{3,2,1,0:T(1,128)S(1)}, u32[]{:S(2)}, u32[]{:S(2)}) collective-permute-start(f32[3,32,1,128]{3,2,1,0:T(1,128)S(1)} %slice.746), channel_id=1, source_target_pairs={{0,1},{1,2},{2,3},{4,5},{5,6},{6,7},{8,9},{9,10},{10,11},{12,13},{... | collective-permute-start | bytes 147464 | tf_op jit(solution)/shard_map/ppermute | solution.py:18
  81.4 3.0 %collective-permute-start.19 = (f32[3,1,8,128]{3,2,1,0:T(8,128)S(1)}, f32[3,1,8,128]{3,2,1,0:T(8,128)S(1)}, u32[]{:S(2)}, u32[]{:S(2)}) collective-permute-start(f32[3,1,8,128]{3,2,1,0:T(8,128)S(1)} %slice.752), channel_id=1, source_target_pairs={{0,4},{1,5},{2,6},{3,7},{8,12},{9,13},{10,14},{11,15},{16,20},{17,... | collective-permute-start | bytes 36872 | tf_op jit(solution)/shard_map/ppermute | solution.py:18
  86.1 7.0 %collective-permute-start.20 = (f32[3,32,1,128]{3,2,1,0:T(1,128)}, f32[3,32,1,128]{3,2,1,0:T(1,128)}, u32[]{:S(2)}, u32[]{:S(2)}) collective-permute-start(f32[3,32,1,128]{3,2,1,0:T(1,128)} %slice.758), channel_id=1, source_target_pairs={{1,0},{2,1},{3,2},{5,4},{6,5},{7,6},{9,8},{10,9},{11,10},{13,12},{... | collective-permute-start | bytes 147464 | tf_op jit(solution)/shard_map/ppermute | solution.py:18
  87.4 5.7 %collective-permute-start.21 = (f32[3,1,8,128]{3,2,1,0:T(8,128)S(1)}, f32[3,1,8,128]{3,2,1,0:T(8,128)}, u32[]{:S(2)}, u32[]{:S(2)}) collective-permute-start(f32[3,1,8,128]{3,2,1,0:T(8,128)S(1)} %slice.764), channel_id=1, source_target_pairs={{4,0},{5,1},{6,2},{7,3},{12,8},{13,9},{14,10},{15,11},{20,16},{21,... | collective-permute-start | bytes 36872 | tf_op jit(solution)/shard_map/ppermute | solution.py:18
  95.2 8.0 %copy-start.5 = (f32[3,32,8,128]{3,2,1,0:T(8,128)S(1)}, f32[3,32,8,128]{3,2,1,0:T(8,128)}, u32[]{:S(2)}) copy-start(f32[3,32,8,128]{3,2,1,0:T(8,128)} %copy-done.4) | copy-start | bytes 1179652
  95.4 9.2 %collective-permute-start.22 = (f32[3,32,1,128]{3,2,1,0:T(1,128)S(1)}, f32[3,32,1,128]{3,2,1,0:T(1,128)S(1)}, u32[]{:S(2)}, u32[]{:S(2)}) collective-permute-start(f32[3,32,1,128]{3,2,1,0:T(1,128)S(1)} %slice.768), channel_id=1, source_target_pairs={{0,1},{1,2},{2,3},{4,5},{5,6},{6,7},{8,9},{9,10},{10,11},{12,13},{... | collective-permute-start | bytes 147464 | tf_op jit(solution)/shard_map/ppermute | solution.py:18
  100.0 4.7 %collective-permute-start.23 = (f32[3,1,8,128]{3,2,1,0:T(8,128)S(1)}, f32[3,1,8,128]{3,2,1,0:T(8,128)S(1)}, u32[]{:S(2)}, u32[]{:S(2)}) collective-permute-start(f32[3,1,8,128]{3,2,1,0:T(8,128)S(1)} %slice.774), channel_id=1, source_target_pairs={{0,4},{1,5},{2,6},{3,7},{8,12},{9,13},{10,14},{11,15},{16,20},{17,... | collective-permute-start | bytes 36872 | tf_op jit(solution)/shard_map/ppermute | solution.py:18
  106.5 12.5 %copy-start.19 = (f32[3,32,8]{2,1,0:T(8,128)S(1)}, f32[3,32,8]{2,1,0:T(8,128)}, u32[]{:S(2)}) copy-start(f32[3,32,8]{2,1,0:T(8,128)} %copy-done.17) | copy-start | bytes 9220
  106.5 12.5 %copy-start.22 = (f32[3,32,8]{2,1,0:T(8,128)S(1)}, f32[3,32,8]{2,1,0:T(8,128)}, u32[]{:S(2)}) copy-start(f32[3,32,8]{2,1,0:T(8,128)} %copy-done.20) | copy-start | bytes 9220
  (21 other events, 32.2 us)
where the time goes:
time: 121 us; the launch traced here: 120 us
  starting transfers between devices  58 us (48%)
  waiting for transfers between devices  19.5 us (16%)
  blocking collectives  17.8 us (15%)
  local copies, waits for them, and re-layouts  13.3 us (11%)
  other arithmetic  8.24 us (7%)
  between operations  3.44 us (3%)
    ppermute x24, starting transfers between devices, shifted_2(): return lax.ppermute(block, axis, route)  58 us
    ppermute x24, waiting for transfers between devices, shifted_2(): return lax.ppermute(block, axis, route)  19.5 us
    psum x1, blocking collectives, per_device(): summed = lax.psum(local_grad, 'wl')  11.6 us
    all_gather x1, blocking collectives, per_device(): tiles = lax.all_gather(design, 'wl', axis=0, tiled=True)  6.17 us
    unnamed x59, local copies, waits for them, and re-layouts  5.58 us
    slice x12, local copies, waits for them, and re-layouts, neighbours(): plane_y = stacked[:, :, :1] if upward else stacked[:, :, -1:]  3.04 us
  transfers between devices with their start and end apart: 24, of which 8 were waited for; matrix products, arithmetic and copies ran while one was open for 6% of the time, Pallas kernels for 0%

commit v1 on v0

v1 whole, which is shorter than its diff:
```python
import math

import jax
import jax.numpy as jnp
import numpy as np
from jax import lax
from jax.experimental import pallas as pl
from jax.experimental.pallas import tpu as pltpu
from jax.sharding import PartitionSpec as P

Z0 = 64
STEPS = 3
DT = 0.5
F32 = jnp.float32
FH = 5
AH = 3
CH = 4


def pair(axis, parity):
    def go(i):
        return (i ^ 1) if parity == 0 else ((i + 1) ^ 1) - 1
    return go


def swap(block, flip_x, parity):
    nx, ny = lax.axis_size("gx"), lax.axis_size("gy")
    go = (lambda i: i) if parity is None else pair("gy", parity)
    route = []
    for a in range(nx):
        for b in range(ny):
            ta, tb = (a ^ 1 if flip_x else a), go(b)
            if 0 <= ta < nx and 0 <= tb < ny:
                route.append((a * ny + b, ta * ny + tb))
    return lax.ppermute(block, ("gx", "gy"), route)


def y_units():
    units = [("fe", c, s) for c in range(3) for s in range(FH)]
    units += [("fh", c, s) for c in range(3) for s in range(FH)]
    units += [("ae", c, s) for c in range(3) for s in range(AH)]
    units += [("ah", c, s) for c in range(3) for s in range(AH)]
    units += [("co", 0, s) for s in range(CH)]
    return units


def x_units(ny):
    units = [(a, c, y) for a in ("fe", "fh", "ae", "ah") for c in range(3) for y in range(ny)]
    return units + [("co", 0, y) for y in range(ny)]


def dims(xl, yl):
    return xl + 8, yl + 2 * FH


def pack_body(fe, fh, ae, ah, bg, dsg, sp, co, pa, pb, px, pda, pdb, *, xl, yl):
    depth = dsg.shape[0]
    gx, gy = lax.axis_index("gx"), lax.axis_index("gy")
    lane = lax.broadcasted_iota(jnp.int32, (xl, 128), 1)
    layers = [dsg[l] for l in range(depth)]
    for y in range(yl):
        perm = bg[pl.ds(y, xl, stride=yl), :]
        for l in range(depth):
            col = jnp.broadcast_to(layers[l][:, y : y + 1], (xl, 128))
            perm = jnp.where(lane == Z0 + l, col, perm)
        co[y] = DT / perm
    refs = dict(fe=fe, fh=fh, ae=ae, ah=ah)
    x0 = pl.multiple_of(jnp.where(gx == 0, xl - 8, 0), 8)
    prof = sp[...]
    zero = jnp.zeros((xl, 128), F32)
    plane = xl * yl
    for dst, dst_d, up in ((pa, pda, gy % 2 == 0), (pb, pdb, gy % 2 == 1)):
        base = dict(fe=FH, fh=FH, ae=AH, ah=AH, co=CH)
        base = {k: jnp.where(up, yl - v, 0) for k, v in base.items()}
        u = 0
        for name, c, s in y_units():
            row = base[name] + s
            if name == "co":
                dst[u] = co[row]
            else:
                dst[u] = refs[name][pl.ds(c * plane + row, xl, stride=yl), :]
            u += 1
        dst[u] = zero
        dst[u, :, 0:FH] = jnp.where(up, prof[:, yl - FH : yl], prof[:, 0:FH])
        for v in range(u + 1):
            dst_d[v] = dst[v, pl.ds(x0, 8), :]
    u = 0
    for name, c, y in x_units(yl):
        if name == "co":
            px[u] = co[y, pl.ds(x0, 8), :]
        else:
            px[u] = refs[name][pl.ds(c * plane + x0 * yl + y, 8, stride=yl), :]
        u += 1
    px[u] = jnp.zeros((8, 128), F32)
    px[u, :, 0:yl] = sp[pl.ds(x0, 8), :]


def main_body(fe, fh, ae, ah, co, sp, ra, rb, rx, rda, rdb, src, mon, out_f, out_a, grad,
              e0, e1, e2, e3, h, a, g, cx, sx, *, xl, yl, nw, signals, omegas):
    xr, yr = dims(xl, yl)
    gx, gy, w = lax.axis_index("gx"), lax.axis_index("gy"), lax.axis_index("wl")
    lane = lax.broadcasted_iota(jnp.int32, (xr, 128), 1)
    sub = lax.broadcasted_iota(jnp.int32, (8, 128), 0)
    src_l, mon_l = src[0], mon[0]
    keep = jnp.where(gx == 0, (sub < FH).astype(F32), (sub >= 8 - FH).astype(F32))
    big = dict(fe=e0, fh=h, ae=a, ah=g)
    plane = xl * yl
    halo = pl.ds(xl, 8)
    own = pl.ds(0, xl)
    for name, ref in (("fe", fe), ("fh", fh), ("ae", ae), ("ah", ah)):
        for c in range(3):
            for y in range(yl):
                big[name][c, FH + y, own, :] = ref[pl.ds(c * plane + y, xl, stride=yl), :]
    for y in range(yl):
        cx[FH + y, own, :] = co[y]
    at_src = lax.broadcasted_iota(jnp.int32, (xl, 128), 1) == src_l
    at_src8 = lax.broadcasted_iota(jnp.int32, (8, 128), 1) == src_l
    zero, zero8 = jnp.zeros((xl, 128), F32), jnp.zeros((8, 128), F32)
    prof = sp[...]
    u = 0
    for name, c, y in x_units(yl):
        tile = rx[u] * keep
        if name == "co":
            cx[FH + y, halo, :] = tile
        else:
            big[name][c, FH + y, halo, :] = tile
        u += 1
    prof_x = rx[u] * keep
    for y in range(yl):
        sx[FH + y, own, :] = jnp.where(at_src, jnp.broadcast_to(prof[:, y : y + 1], (xl, 128)), zero)
        sx[FH + y, halo, :] = jnp.where(at_src8, jnp.broadcast_to(prof_x[:, y : y + 1], (8, 128)), zero8)
    for ref, ref_d, high in ((ra, rda, gy % 2 == 0), (rb, rdb, gy % 2 == 1)):
        first = {}
        for name, deep in (("fe", FH), ("fh", FH), ("ae", AH), ("ah", AH), ("co", CH)):
            first[name] = jnp.where(high, FH + yl, FH - deep)
        u = 0
        for name, c, s in y_units():
            row = first[name] + s
            tile = ref_d[u] * keep
            if name == "co":
                cx[row, own, :] = ref[u]
                cx[row, halo, :] = tile
            else:
                big[name][c, row, own, :] = ref[u]
                big[name][c, row, halo, :] = tile
            u += 1
        prof_y, prof_d = ref[u], ref_d[u] * keep
        for s in range(FH):
            row = first["fe"] + s
            sx[row, own, :] = jnp.where(at_src, jnp.broadcast_to(prof_y[:, s : s + 1], (xl, 128)), zero)
            sx[row, halo, :] = jnp.where(at_src8, jnp.broadcast_to(prof_d[:, s : s + 1], (8, 128)), zero8)

    ring = lax.broadcasted_iota(jnp.int32, (xr, 128), 0)
    inside_low = jnp.where(ring < xl + FH, F32(DT), F32(0.0))
    inside_high = jnp.where((ring < xl) | (ring >= xr - FH), F32(DT), F32(0.0))
    h_in = jnp.where(gx == 0, inside_low, inside_high)
    low = jnp.where(gy == 0, 0.0, 1.0).astype(F32)
    h_low = h_in * low
    z_last = lane == 127
    z_first = lane == 0
    at_mon = lane == mon_l

    def zup(v):
        return jnp.where(z_last, 0.0, pltpu.roll(v, 127, 1)) - v

    def zdn(v):
        return v - jnp.where(z_first, 0.0, pltpu.roll(v, 1, 1))

    def xup(v):
        return pltpu.roll(v, xr - 1, 0) - v

    def xdn(v):
        return v - pltpu.roll(v, 1, 0)

    def step_h(e, hh, y):
        k = h_low if y < FH else h_in
        ex, ey, ez = e[0, y], e[1, y], e[2, y]
        hh[0, y] = hh[0, y] - k * ((e[2, y + 1] - ez) - zup(ey))
        hh[1, y] = hh[1, y] - k * (zup(ex) - xup(ez))
        hh[2, y] = hh[2, y] - k * (xup(ey) - (e[0, y + 1] - ex))

    def curl_e(hh, y):
        hx, hy, hz = hh[0, y], hh[1, y], hh[2, y]
        k = cx[y]
        return (
            k * ((hz - hh[2, y - 1]) - zdn(hy)),
            k * (zdn(hx) - xdn(hz)),
            k * (xdn(hy) - (hx - hh[0, y - 1])),
        )

    def pick(values):
        value = F32(values[0])
        for i in range(1, nw):
            value = jnp.where(w == i, F32(values[i]), value)
        return value

    runs = (e0, e1, e2, e3)
    for k in range(STEPS):
        old, new = runs[k], runs[k + 1]
        signal = pick([signals[i][k] for i in range(nw)])
        for y in range(k, yr - 1 - k):
            step_h(old, h, y)
            if y > k:
                dx, dy, dz = curl_e(h, y)
                new[0, y] = old[0, y] + dx + signal * sx[y]
                new[1, y] = old[1, y] + dy
                new[2, y] = old[2, y] + dz
    total = [None] * yl
    for j in range(STEPS):
        seen = runs[STEPS - j]
        for y in range(FH - AH + j, yr - AH - j):
            step_h(a, g, y)
            if y > FH - AH + j:
                for c, d in enumerate(curl_e(g, y)):
                    f = seen[c, y]
                    v = a[c, y] + d + jnp.where(at_mon, 2.0 * DT * f, 0.0)
                    a[c, y] = v
                    if FH <= y < FH + yl:
                        t = (f * v)[0:xl]
                        i = y - FH
                        total[i] = t if total[i] is None else total[i] + t
    lane_o = lax.broadcasted_iota(jnp.int32, (xl, 128), 1)
    scale = pick([o * o for o in omegas])
    packed = jnp.zeros((xl, 128), F32)
    wide = 128 // yl
    for y in range(yl):
        moved = pltpu.roll(total[y] * scale, (wide * y - Z0) % 128, 1)
        packed = jnp.where((lane_o >= wide * y) & (lane_o < wide * y + wide), moved, packed)
    grad[...] = packed
    for c in range(3):
        for y in range(yl):
            out_f[pl.ds(c * plane + y, xl, stride=yl), :] = e3[c, FH + y, own, :]
            out_a[pl.ds(c * plane + y, xl, stride=yl), :] = a[c, FH + y, own, :]


def sum_body(*refs, owned, yl):
    *parts, out = refs
    w = lax.axis_index("wl")
    acc = parts[0][...]
    for p in parts[1:]:
        acc = acc + p[...]
    acc = pltpu.roll(acc, (128 - owned * w) % 128, 1)
    lane = lax.broadcasted_iota(jnp.int32, acc.shape, 1)
    wide = 128 // yl
    for i in range(owned):
        res = jnp.zeros_like(acc)
        for y in range(yl):
            res = jnp.where(lane == y, pltpu.roll(acc, (y - wide * y - i) % 128, 1), res)
        out[i] = res[:, 0:yl]


def per_device(fe, fh, ae, ah, background, design, source_profile, source_layer, monitor_layer):
    _, _, xl, yl, nz = fe.shape
    nw = lax.axis_size("wl")
    owned = design.shape[0]
    flat = [v.reshape(3 * xl * yl, nz) for v in (fe, fh, ae, ah)]
    bg = background.reshape(xl * yl, nz)
    sp = source_profile[0]
    tiles = lax.all_gather(design, "wl", axis=0, tiled=True)
    xr, yr = dims(xl, yl)
    n_y, n_x = len(y_units()) + 1, len(x_units(yl)) + 1
    shape = lambda *s: jax.ShapeDtypeStruct(s, F32)
    params = pltpu.CompilerParams(vmem_limit_bytes=50 * 1024 * 1024)
    co, pa, pb, px, pda, pdb = pl.pallas_call(
        lambda *r: pack_body(*r, xl=xl, yl=yl),
        out_shape=(shape(yl, xl, nz), shape(n_y, xl, nz), shape(n_y, xl, nz), shape(n_x, 8, nz),
                   shape(n_y, 8, nz), shape(n_y, 8, nz)),
        compiler_params=params,
        name="pack",
    )(*flat, bg, tiles, sp)
    ra = swap(pa, False, 0)
    rb = swap(pb, False, 1)
    rx = swap(px, True, None)
    rda = swap(pda, True, 0)
    rdb = swap(pdb, True, 1)
    f32 = np.float32
    omegas = [f32(2.0 * math.pi) / (f32(16.0) + f32(32.0) * f32(i) / f32(nw)) for i in range(nw)]
    signals = [[f32(DT) * np.sin(f32(o * f32((k + 1) * DT))) for k in range(STEPS)] for o in omegas]
    ext = lambda *s: pltpu.VMEM(s, F32)
    field = ext(3, yr, xr, nz)
    smem = pl.BlockSpec(memory_space=pltpu.SMEM)
    out_f, out_a, grad = pl.pallas_call(
        lambda *r: main_body(*r, xl=xl, yl=yl, nw=nw, signals=signals, omegas=omegas),
        out_shape=(shape(3 * xl * yl, nz), shape(3 * xl * yl, nz), shape(xl, nz)),
        in_specs=[pl.BlockSpec(memory_space=pltpu.VMEM)] * 11 + [smem, smem],
        scratch_shapes=[field] * 7 + [ext(yr, xr, nz), ext(yr, xr, nz)],
        compiler_params=params,
        name="window",
    )(*flat, co, sp, ra, rb, rx, rda, rdb, source_layer, monitor_layer)
    parts = [grad]
    for k in range(1, nw):
        parts.append(lax.ppermute(grad, "wl", [(i, i ^ k) for i in range(nw)]))
    gradient = pl.pallas_call(
        lambda *r: sum_body(*r, owned=owned, yl=yl),
        out_shape=shape(owned, xl, yl),
        compiler_params=params,
        name="gather_sum",
    )(*parts)
    block = (1, 3, xl, yl, nz)
    return (out_f.reshape(block), out_a.reshape(block), gradient)


def solution(mesh):
    field = P("wl", None, "gx", "gy", None)
    return jax.shard_map(
        per_device,
        mesh=mesh,
        in_specs=(field, field, field, field, P("gx", "gy", None), P("wl", "gx", "gy"),
                  P("wl", "gx", "gy"), P("wl"), P("wl")),
        out_specs=(field, field, P("wl", "gx", "gy")),
        check_vma=False,
    )
```

time: 121 us -> 59.7 us (0.49)
  the two profiles are of different devices: /device:TPU:0 before, /device:TPU:9 now
where the time goes in v1:
time: 59.7 us; the launch traced here: 59.3 us
  waiting for transfers between devices  24.7 us (41%)
  starting transfers between devices  10.4 us (17%)
  Pallas kernels  10.2 us (17%)
  local copies, waits for them, and re-layouts  6.44 us (11%)
  blocking collectives  5.66 us (9%)
  between operations  2.01 us (3%)
    ppermute x5, waiting for transfers between devices, swap(): return lax.ppermute(block, ('gx', 'gy'), route)  21.9 us
    pallas_call x1, Pallas kernels, per_device(): pl.pallas_call(lambda *r: main_body(*r, xl=xl, yl=yl, nw=nw, signals=sign...  8.4 us
    ppermute x5, starting transfers between devices, swap(): return lax.ppermute(block, ('gx', 'gy'), route)  7.7 us
    unnamed x16, local copies, waits for them, and re-layouts  6.35 us
    all_gather x1, blocking collectives, per_device(): tiles = lax.all_gather(design, 'wl', axis=0, tiled=True)  5.66 us
    ppermute x3, waiting for transfers between devices, per_device(): parts.append(lax.ppermute(grad, 'wl', [(i, i ^ k) for i in range(nw)]))  2.74 us
    ppermute x3, starting transfers between devices, per_device(): parts.append(lax.ppermute(grad, 'wl', [(i, i ^ k) for i in range(nw)]))  2.69 us
    pallas_call x1, Pallas kernels, per_device(): pl.pallas_call(lambda *r: pack_body(*r, xl=xl, yl=yl), out_shape=(shape(y...  1.59 us
  transfers between devices with their start and end apart: 8, of which 4 were waited for; matrix products, arithmetic and copies ran while one was open for 0% of the time, Pallas kernels for 0%

profile of v1, /device:TPU:9, one launch (start us, length us, event | category | flops | bytes accessed | tf_op | source)
XLA Modules:
  0.0 59.3 jit_solution(17214720718079798882)
XLA Ops:
  0.6 0.0 copy-start.6
  0.6 0.0 copy-start.4
  0.7 0.8 %copy.15 = f32[1,32,8]{2,1,0:T(8,128)S(1)} copy(f32[1,32,8]{1,2,0:T(8,128)} %param.15) | data formatting | bytes 2048 | tf_op args[6]
  1.4 0.0 copy-done.6
  1.5 5.7 %all_gather.3 = f32[8,32,8]{1,2,0:T(8,128)S(1)} all-gather(f32[2,32,8]{1,2,0:T(8,128)S(1)} %copy-done.6), channel_id=1, replica_groups=mesh['wl'=4,'gx'=2,'gy'=4] {'wl'}, dimensions={0}, use_global_device_ids=true | all-gather | bytes 10240 | tf_op jit(solution)/shard_map/all_gather | solution.py:259
  7.1 0.1 copy.16.r_5_
  7.2 0.0 copy-start
  7.2 1.0 %copy-done = f32[1,3,32,8,128]{4,3,2,1,0:T(8,128)S(1)} copy-done((f32[1,3,32,8,128]{4,3,2,1,0:T(8,128)S(1)}, f32[1,3,32,8,128]{4,3,2,1,0:T(8,128)}, u32[]{:S(2)}) %copy-start) | copy-done | bytes 393240
  8.2 1.0 %copy-done.1 = f32[1,3,32,8,128]{4,3,2,1,0:T(8,128)S(1)} copy-done((f32[1,3,32,8,128]{4,3,2,1,0:T(8,128)S(1)}, f32[1,3,32,8,128]{4,3,2,1,0:T(8,128)}, u32[]{:S(2)}) %copy-start.1) | copy-done | bytes 393240
  9.2 1.0 %copy-done.2 = f32[1,3,32,8,128]{4,3,2,1,0:T(8,128)S(1)} copy-done((f32[1,3,32,8,128]{4,3,2,1,0:T(8,128)S(1)}, f32[1,3,32,8,128]{4,3,2,1,0:T(8,128)}, u32[]{:S(2)}) %copy-start.2) | copy-done | bytes 393240
  10.2 1.0 %copy-done.3 = f32[1,3,32,8,128]{4,3,2,1,0:T(8,128)S(1)} copy-done((f32[1,3,32,8,128]{4,3,2,1,0:T(8,128)S(1)}, f32[1,3,32,8,128]{4,3,2,1,0:T(8,128)}, u32[]{:S(2)}) %copy-start.3) | copy-done | bytes 393240
  11.2 1.6 %pack.1 = (f32[8,32,128]{2,1,0:T(8,128)S(1)}, f32[53,32,128]{2,1,0:T(8,128)S(1)}, f32[53,32,128]{2,1,0:T(8,128)}, f32[105,8,128]{2,1,0:T(8,128)S(1)}, f32[53,8,1...) custom-call(f32[768,128]{1,0:T(8,128)S(1)} %bitcast.8, f32[768,128]{1,0:T(8,128)S(1)} %bitcast.10, f32[768,128]{1,0:T(8,128)S(1)} %bitcast.12, ...), custom_call_target="tpu_custom_call" | custom-call | tf_op jit(solution)/shard_map/pack/pallas_call | solution.py:264
  12.8 0.0 collective-permute-start
  12.8 4.5 %collective-permute-start.1 = (f32[53,32,128]{2,1,0:T(8,128)}, f32[53,32,128]{2,1,0:T(8,128)S(1)}, u32[]{:S(2)}, u32[]{:S(2)}) collective-permute-start(f32[53,32,128]{2,1,0:T(8,128)} %get-tuple-element.14), channel_id=1, source_target_pairs={{1,2},{2,1},{5,6},{6,5},{9,10},{10,9},{13,14},{14,13},{17,18},{18,... | collective-permute-start | bytes 2605064 | tf_op jit(solution)/shard_map/ppermute | solution.py:35
  17.3 1.3 %collective-permute-start.2 = (f32[105,8,128]{2,1,0:T(8,128)S(1)}, f32[105,8,128]{2,1,0:T(8,128)S(1)}, u32[]{:S(2)}, u32[]{:S(2)}) collective-permute-start(f32[105,8,128]{2,1,0:T(8,128)S(1)} %get-tuple-element.15), channel_id=1, source_target_pairs={{0,4},{1,5},{2,6},{3,7},{4,0},{5,1},{6,2},{7,3},{8,12},{9,13},{10,... | collective-permute-start | bytes 1290248 | tf_op jit(solution)/shard_map/ppermute | solution.py:35
  18.6 0.0 collective-permute-start.3
  18.6 1.9 %collective-permute-start.4 = (f32[53,8,128]{2,1,0:T(8,128)S(1)}, f32[53,8,128]{2,1,0:T(8,128)S(1)}, u32[]{:S(2)}, u32[]{:S(2)}) collective-permute-start(f32[53,8,128]{2,1,0:T(8,128)S(1)} %get-tuple-element.17), channel_id=1, source_target_pairs={{1,6},{2,5},{5,2},{6,1},{9,14},{10,13},{13,10},{14,9},{17,22},{18,... | collective-permute-start | bytes 651272 | tf_op jit(solution)/shard_map/ppermute | solution.py:35
  21.8 18.0 %collective-permute-done.3.r_9_ = f32[53,8,128]{2,1,0:T(8,128)S(1)} collective-permute-done((f32[53,8,128]{2,1,0:T(8,128)S(1)}, f32[53,8,128]{2,1,0:T(8,128)S(1)}, u32[]{:S(2)}, u32[]{:S(2)}) %collective-permute-start.3) | collective-permute-done | bytes 217120 | tf_op jit(solution)/shard_map/ppermute | solution.py:35
  39.8 3.9 %collective-permute-done.4.r_10_ = f32[53,8,128]{2,1,0:T(8,128)S(1)} collective-permute-done((f32[53,8,128]{2,1,0:T(8,128)S(1)}, f32[53,8,128]{2,1,0:T(8,128)S(1)}, u32[]{:S(2)}, u32[]{:S(2)}) %collective-permute-start.4) | collective-permute-done | bytes 217120 | tf_op jit(solution)/shard_map/ppermute | solution.py:35
  43.7 0.0 collective-permute-done.2.r_8_
  43.7 0.0 collective-permute-done.r_6_
  43.7 0.0 collective-permute-done.1.r_7_
  43.7 0.9 %copy-done.5 = f32[53,32,128]{2,1,0:T(8,128)} copy-done((f32[53,32,128]{2,1,0:T(8,128)}, f32[53,32,128]{2,1,0:T(8,128)S(1)}, u32[]{:S(2)}) %copy-start.5) | copy-done | bytes 868376
  44.6 8.4 %window.1 = (f32[768,128]{1,0:T(8,128)}, f32[768,128]{1,0:T(8,128)}, f32[32,128]{1,0:T(8,128)S(1)}) custom-call(f32[768,128]{1,0:T(8,128)S(1)} %bitcast.9, f32[768,128]{1,0:T(8,128)S(1)} %bitcast.11, f32[768,128]{1,0:T(8,128)S(1)} %bitcast.13, f32[768,128]{1,0:T(8,128)S(1)} %bitcast.15, f32[8,32,128]{2,1,0:T(8,128)S(1)} %get-tuple-element.12.r_4_, ...), custom_call_target="tpu_custom_call" | custom-call | tf_op jit(solution)/shard_map/window/pallas_call | solution.py:282
  53.0 1.1 %collective-permute-start.5 = (f32[32,128]{1,0:T(8,128)S(1)}, f32[32,128]{1,0:T(8,128)S(1)}, u32[]{:S(2)}, u32[]{:S(2)}) collective-permute-start(f32[32,128]{1,0:T(8,128)S(1)} %get-tuple-element.20.r_0_), channel_id=1, source_target_pairs={{0,8},{8,0},{16,24},{24,16},{1,9},{9,1},{17,25},{25,17},{2,10},{10... | collective-permute-start | bytes 49160 | tf_op jit(solution)/shard_map/ppermute | solution.py:292
  54.1 1.2 %collective-permute-start.6 = (f32[32,128]{1,0:T(8,128)S(1)}, f32[32,128]{1,0:T(8,128)S(1)}, u32[]{:S(2)}, u32[]{:S(2)}) collective-permute-start(f32[32,128]{1,0:T(8,128)S(1)} %get-tuple-element.20.r_0_), channel_id=1, source_target_pairs={{0,16},{8,24},{16,0},{24,8},{1,17},{9,25},{17,1},{25,9},{2,18},{10... | collective-permute-start | bytes 49160 | tf_op jit(solution)/shard_map/ppermute | solution.py:292
  55.3 0.4 collective-permute-start.7
  55.7 0.0 collective-permute-done.5.r_1_
  55.7 1.0 %collective-permute-done.6.r_2_ = f32[32,128]{1,0:T(8,128)S(1)} collective-permute-done((f32[32,128]{1,0:T(8,128)S(1)}, f32[32,128]{1,0:T(8,128)S(1)}, u32[]{:S(2)}, u32[]{:S(2)}) %collective-permute-start.6) | collective-permute-done | bytes 16416 | tf_op jit(solution)/shard_map/ppermute | solution.py:292
  56.7 1.8 %collective-permute-done.7.r_3_ = f32[32,128]{1,0:T(8,128)S(1)} collective-permute-done((f32[32,128]{1,0:T(8,128)S(1)}, f32[32,128]{1,0:T(8,128)S(1)}, u32[]{:S(2)}, u32[]{:S(2)}) %collective-permute-start.7) | collective-permute-done | bytes 16416 | tf_op jit(solution)/shard_map/ppermute | solution.py:292
  58.5 0.2 gather_sum.1
  58.7 0.7 %copy.17 = f32[2,32,8]{1,2,0:T(8,128)} copy(f32[2,32,8]{2,1,0:T(8,128)S(1)} %gather_sum.1) | data formatting | bytes 4096
  (5 shorter events, 0.0 us)
Async XLA Ops:
  0.6 0.8 %copy-start.6 = (f32[2,32,8]{1,2,0:T(8,128)S(1)}, f32[2,32,8]{1,2,0:T(8,128)}, u32[]{:S(2)}) copy-start(f32[2,32,8]{1,2,0:T(8,128)} %param.14) | copy-start | bytes 6148
  0.6 6.6 %copy-start.4 = (f32[32,8,128]{2,1,0:T(8,128)S(1)}, f32[32,8,128]{2,1,0:T(8,128)}, u32[]{:S(2)}) copy-start(f32[32,8,128]{2,1,0:T(8,128)} %param.13) | copy-start | bytes 393220
  7.2 1.0 %copy-start = (f32[1,3,32,8,128]{4,3,2,1,0:T(8,128)S(1)}, f32[1,3,32,8,128]{4,3,2,1,0:T(8,128)}, u32[]{:S(2)}) copy-start(f32[1,3,32,8,128]{4,3,2,1,0:T(8,128)} %param.9) | copy-start | bytes 1179652
  8.2 1.0 %copy-start.1 = (f32[1,3,32,8,128]{4,3,2,1,0:T(8,128)S(1)}, f32[1,3,32,8,128]{4,3,2,1,0:T(8,128)}, u32[]{:S(2)}) copy-start(f32[1,3,32,8,128]{4,3,2,1,0:T(8,128)} %param.10) | copy-start | bytes 1179652
  9.2 1.0 %copy-start.2 = (f32[1,3,32,8,128]{4,3,2,1,0:T(8,128)S(1)}, f32[1,3,32,8,128]{4,3,2,1,0:T(8,128)}, u32[]{:S(2)}) copy-start(f32[1,3,32,8,128]{4,3,2,1,0:T(8,128)} %param.11) | copy-start | bytes 1179652
  10.2 1.0 %copy-start.3 = (f32[1,3,32,8,128]{4,3,2,1,0:T(8,128)S(1)}, f32[1,3,32,8,128]{4,3,2,1,0:T(8,128)}, u32[]{:S(2)}) copy-start(f32[1,3,32,8,128]{4,3,2,1,0:T(8,128)} %param.12) | copy-start | bytes 1179652
  12.8 30.9 %collective-permute-start = (f32[53,32,128]{2,1,0:T(8,128)S(1)}, f32[53,32,128]{2,1,0:T(8,128)S(1)}, u32[]{:S(2)}, u32[]{:S(2)}) collective-permute-start(f32[53,32,128]{2,1,0:T(8,128)S(1)} %get-tuple-element.13), channel_id=1, source_target_pairs={{0,1},{1,0},{2,3},{3,2},{4,5},{5,4},{6,7},{7,6},{8,9},{9,8},{10,11... | collective-permute-start | bytes 2605064 | tf_op jit(solution)/shard_map/ppermute | solution.py:35
  12.8 30.9 %collective-permute-start.1 = (f32[53,32,128]{2,1,0:T(8,128)}, f32[53,32,128]{2,1,0:T(8,128)S(1)}, u32[]{:S(2)}, u32[]{:S(2)}) collective-permute-start(f32[53,32,128]{2,1,0:T(8,128)} %get-tuple-element.14), channel_id=1, source_target_pairs={{1,2},{2,1},{5,6},{6,5},{9,10},{10,9},{13,14},{14,13},{17,18},{18,... | collective-permute-start | bytes 2605064 | tf_op jit(solution)/shard_map/ppermute | solution.py:35
  17.3 26.4 %collective-permute-start.2 = (f32[105,8,128]{2,1,0:T(8,128)S(1)}, f32[105,8,128]{2,1,0:T(8,128)S(1)}, u32[]{:S(2)}, u32[]{:S(2)}) collective-permute-start(f32[105,8,128]{2,1,0:T(8,128)S(1)} %get-tuple-element.15), channel_id=1, source_target_pairs={{0,4},{1,5},{2,6},{3,7},{4,0},{5,1},{6,2},{7,3},{8,12},{9,13},{10,... | collective-permute-start | bytes 1290248 | tf_op jit(solution)/shard_map/ppermute | solution.py:35
  18.6 21.2 %collective-permute-start.3 = (f32[53,8,128]{2,1,0:T(8,128)S(1)}, f32[53,8,128]{2,1,0:T(8,128)S(1)}, u32[]{:S(2)}, u32[]{:S(2)}) collective-permute-start(f32[53,8,128]{2,1,0:T(8,128)S(1)} %get-tuple-element.16), channel_id=1, source_target_pairs={{0,5},{1,4},{2,7},{3,6},{4,1},{5,0},{6,3},{7,2},{8,13},{9,12},{10,... | collective-permute-start | bytes 651272 | tf_op jit(solution)/shard_map/ppermute | solution.py:35
  18.6 25.1 %collective-permute-start.4 = (f32[53,8,128]{2,1,0:T(8,128)S(1)}, f32[53,8,128]{2,1,0:T(8,128)S(1)}, u32[]{:S(2)}, u32[]{:S(2)}) collective-permute-start(f32[53,8,128]{2,1,0:T(8,128)S(1)} %get-tuple-element.17), channel_id=1, source_target_pairs={{1,6},{2,5},{5,2},{6,1},{9,14},{10,13},{13,10},{14,9},{17,22},{18,... | collective-permute-start | bytes 651272 | tf_op jit(solution)/shard_map/ppermute | solution.py:35
  43.7 0.9 %copy-start.5 = (f32[53,32,128]{2,1,0:T(8,128)}, f32[53,32,128]{2,1,0:T(8,128)S(1)}, u32[]{:S(2)}) copy-start(f32[53,32,128]{2,1,0:T(8,128)S(1)} %collective-permute-done.1.r_7_) | copy-start | bytes 2605060
  53.0 2.7 %collective-permute-start.5 = (f32[32,128]{1,0:T(8,128)S(1)}, f32[32,128]{1,0:T(8,128)S(1)}, u32[]{:S(2)}, u32[]{:S(2)}) collective-permute-start(f32[32,128]{1,0:T(8,128)S(1)} %get-tuple-element.20.r_0_), channel_id=1, source_target_pairs={{0,8},{8,0},{16,24},{24,16},{1,9},{9,1},{17,25},{25,17},{2,10},{10... | collective-permute-start | bytes 49160 | tf_op jit(solution)/shard_map/ppermute | solution.py:292
  54.1 2.6 %collective-permute-start.6 = (f32[32,128]{1,0:T(8,128)S(1)}, f32[32,128]{1,0:T(8,128)S(1)}, u32[]{:S(2)}, u32[]{:S(2)}) collective-permute-start(f32[32,128]{1,0:T(8,128)S(1)} %get-tuple-element.20.r_0_), channel_id=1, source_target_pairs={{0,16},{8,24},{16,0},{24,8},{1,17},{9,25},{17,1},{25,9},{2,18},{10... | collective-permute-start | bytes 49160 | tf_op jit(solution)/shard_map/ppermute | solution.py:292
  55.3 3.2 %collective-permute-start.7 = (f32[32,128]{1,0:T(8,128)S(1)}, f32[32,128]{1,0:T(8,128)S(1)}, u32[]{:S(2)}, u32[]{:S(2)}) collective-permute-start(f32[32,128]{1,0:T(8,128)S(1)} %get-tuple-element.20.r_0_), channel_id=1, source_target_pairs={{0,24},{8,16},{16,8},{24,0},{1,25},{9,17},{17,9},{25,1},{2,26},{10... | collective-permute-start | bytes 49160 | tf_op jit(solution)/shard_map/ppermute | solution.py:292

commit v2 on v0

v2 whole, which is shorter than its diff:
```python
import math

import jax
import jax.numpy as jnp
import numpy as np
from jax import lax
from jax.experimental import pallas as pl
from jax.experimental.pallas import tpu as pltpu
from jax.sharding import PartitionSpec as P

Z0 = 64
STEPS = 3
DT = 0.5
F32 = jnp.float32
BF16 = jnp.bfloat16
FH = 5
AH = 3
WIN = 16
PER = 128 // WIN
PROF = 112


def swap(block, flip_x, parity):
    nx, ny = lax.axis_size("gx"), lax.axis_size("gy")
    route = []
    for a in range(nx):
        for b in range(ny):
            ta = a ^ 1 if flip_x else a
            tb = b if parity is None else ((b + parity) ^ 1) - parity
            if 0 <= ta < nx and 0 <= tb < ny:
                route.append((a * ny + b, ta * ny + tb))
    return lax.ppermute(block, ("gx", "gy"), route)


FWD, ADJ = ("fe", "fh"), ("ae", "ah")
F_RAW = [(n, c, i) for n in FWD for c in range(3) for i in range(AH)] + [("co", 0, i) for i in range(2)]
A_RAW = [(n, c, i) for n in ADJ for c in range(3) for i in range(AH)]
F_WIN = [(n, c, i) for n in FWD for c in range(3) for i in range(AH, FH)] + [("co", 0, i) for i in (2, 3)]
C_RAW = [(n, c, i) for n in FWD + ADJ for c in range(3) for i in range(AH)] + [("co", 0, i) for i in range(2)]
C_WIN = [(n, c, i) for n in FWD for c in range(3) for i in range(FH)] + [("co", 0, i) for i in range(4)]


def x_parts(yl):
    raw = [(n, c, y) for n in FWD + ADJ for c in range(3) for y in range(yl)]
    win = [(n, c, y) for n in FWD for c in range(3) for y in range(yl)]
    co = [("co", 0, y) for y in range(yl)]
    return raw + co, win + co


def ceil(a, b):
    return -(-a // b)


def fetch_body(*refs):
    n = len(refs) // 2
    ins, outs, sems = refs[:n], refs[n : 2 * n], refs[2 * n]
    copies = [pltpu.make_async_copy(s, d, sems.at[i]) for i, (s, d) in enumerate(zip(ins, outs))]
    for c in copies:
        c.start()
    for c in copies:
        c.wait()


def send_body(mon, fe, fh, ae, ah, bg, sp, *rest, xl, yl, nw, owned):
    parts, (co, prof_t, fa, fb, aa, ab, px, da, db, turn) = rest[:nw], rest[nw:]
    gx, gy, w = lax.axis_index("gx"), lax.axis_index("gy"), lax.axis_index("wl")
    plane = xl * yl
    depth = nw * owned
    lane = lax.broadcasted_iota(jnp.int32, (xl, 128), 1)
    lane8 = lane[0:8]
    first = WIN // 2 - mon[0] + 256
    refs = dict(fe=fe, fh=fh, ae=ae, ah=ah)
    turn[...] = jnp.zeros((128, 128), F32)
    for k in range(nw):
        for i in range(owned):
            turn[pl.ds(owned * (w ^ k) + i, yl, stride=depth), 0:xl] = parts[k][i]
    layers = jnp.transpose(turn[...])[0:xl]
    for y in range(yl):
        moved = pltpu.roll(layers, (Z0 - depth * y) % 128, 1)
        perm = jnp.where((lane >= Z0) & (lane < Z0 + depth), moved, bg[pl.ds(y, xl, stride=yl), :])
        co[y] = DT / perm
    turn[0:yl, 0:xl] = sp[...]
    prof_t[...] = jnp.transpose(turn[...])[0:xl]
    low_x = gx == 0
    x8 = pl.multiple_of(jnp.where(low_x, xl - 8, 0), 8)
    x4 = jnp.where(low_x, xl - 4, 0)

    def rows(name, c, r, x, count):
        if name == "co":
            return co[r, pl.ds(x, count), :]
        return refs[name][pl.ds(c * plane + x * yl + r, count, stride=yl), :]

    def windows(parts, x, count, where):
        out = []
        here = lax.broadcasted_iota(jnp.int32, (count, 128), 1)
        for t in range(ceil(len(parts), PER)):
            acc = jnp.zeros((count, 128), F32)
            for q, (name, c, i) in enumerate(parts[t * PER : (t + 1) * PER]):
                moved = pltpu.roll(rows(name, c, where(i), x, count), (WIN * q + first) % 128, 1)
                acc = jnp.where((here >= WIN * q) & (here < WIN * (q + 1)), moved, acc)
            out.append(acc)
        return out

    def tiles(dst, raw, win, where):
        for n, (name, c, i) in enumerate(raw):
            if name == "co":
                part = pltpu.roll(rows(name, c, where(i), x8, 8), jnp.where(low_x, 4, 0), 0)[0:4]
            else:
                part = rows(name, c, where(i), x4, 4)
            dst[n // 2, 4 * (n % 2) : 4 * (n % 2) + 4, :] = part
        at = ceil(len(raw), 2)
        for tile in windows(win, x8, 8, where):
            dst[at] = tile
            at += 1
        return at

    for dst, dst_a, corner, up in ((fa, aa, da, gy % 2 == 0), (fb, ab, db, gy % 2 == 1)):
        where = lambda i, up=up: jnp.where(up, yl - 1 - i, i)
        for u, (name, c, i) in enumerate(F_RAW):
            dst[u] = rows(name, c, where(i), 0, xl)
        for u, (name, c, i) in enumerate(A_RAW):
            dst_a[u] = rows(name, c, where(i), 0, xl)
        at = len(F_RAW)
        for unit in windows(F_WIN, 0, xl, where):
            dst[at] = unit
            at += 1
        mix = dst[at - 1]
        prof = prof_t[...]
        for i in range(FH):
            col = jnp.where(up, prof[:, yl - 1 - i : yl - i], prof[:, i : i + 1])
            mix = jnp.where(lane == PROF + i, jnp.broadcast_to(col, (xl, 128)), mix)
        dst[at - 1] = mix
        last = tiles(corner, C_RAW, C_WIN, where)
        src8 = dst[at - 1, pl.ds(x8, 8), :]
        corner[last - 1] = jnp.where((lane8 >= PROF) & (lane8 < PROF + FH), src8, corner[last - 1])
    raw, win = x_parts(yl)
    last = tiles(px, raw, win, lambda y: y)
    px[last] = prof_t[pl.ds(x8, 8), :]


class Halo:
    def __init__(self, mon, xl, yl, put):
        self.xl, self.yl, self.put = xl, yl, put
        self.gx, self.gy = lax.axis_index("gx"), lax.axis_index("gy")
        self.back = mon - WIN // 2 + 256
        sub = lax.broadcasted_iota(jnp.int32, (8, 128), 0)
        low = self.gx == 0
        mask = lambda lo, hi: jnp.where(low, lo.astype(F32), hi.astype(F32))
        self.keep = mask(sub < FH, sub >= 8 - FH)
        self.near = mask(sub < 4, sub >= 4) > 0.5
        self.far = mask((sub >= 4) & (sub < FH), (sub < 4) & (sub >= 8 - FH)) > 0.5
        self.shift = [jnp.where(low, 0, 4), jnp.where(low, 4, 0)]

    def row(self, i, high):
        return jnp.where(high, FH + self.yl + i, FH - 1 - i)

    def unroll(self, tile, q):
        return pltpu.roll(tile, (self.back - WIN * q) % 128, 1)

    def side(self, ref, raw, win, high):
        own = pl.ds(0, self.xl)
        for u, (name, c, i) in enumerate(raw):
            self.put(name, c, self.row(i, high), own, ref[u])
        for s, (name, c, i) in enumerate(win):
            self.put(name, c, self.row(i, high), own, self.unroll(ref[len(raw) + s // PER], s % PER))

    def tiles(self, ref, raw, win, names, where):
        halo = pl.ds(self.xl, 8)
        seats = {part: s for s, part in enumerate(win)}
        at = ceil(len(raw), 2)
        for n, part in enumerate(raw):
            if part[0] not in names:
                continue
            value = jnp.where(self.near, pltpu.roll(ref[n // 2], self.shift[n % 2], 0), 0.0)
            if part in seats:
                s = seats.pop(part)
                value = jnp.where(self.far, self.unroll(ref[at + s // PER], s % PER), value)
            self.put(part[0], part[1], where(part[2]), halo, value)
        for part, s in seats.items():
            if part[0] in names:
                self.put(part[0], part[1], where(part[2]), halo, self.unroll(ref[at + s // PER], s % PER) * self.keep)


class Stepper:
    def __init__(self, xl, yl, cx):
        self.xr = xr = xl + 8
        self.cx = cx
        gx, gy = lax.axis_index("gx"), lax.axis_index("gy")
        self.lane = lax.broadcasted_iota(jnp.int32, (xr, 128), 1)
        ring = lax.broadcasted_iota(jnp.int32, (xr, 128), 0)
        inside_low = jnp.where(ring < xl + FH, F32(DT), F32(0.0))
        inside_high = jnp.where((ring < xl) | (ring >= xr - FH), F32(DT), F32(0.0))
        self.h_in = jnp.where(gx == 0, inside_low, inside_high)
        self.h_low = self.h_in * jnp.where(gy == 0, 0.0, 1.0).astype(F32)
        self.z_last = self.lane == 127
        ri = lax.broadcasted_iota(jnp.int32, (128, 128), 0)
        ci = lax.broadcasted_iota(jnp.int32, (128, 128), 1)
        diff = jnp.where(ri == ci, F32(1.0), F32(0.0)) - jnp.where(ri == ci - 1, F32(1.0), F32(0.0))
        self.diff = jnp.concatenate([diff] * 3, 0).astype(BF16)

    def zdn(self, p, q):
        v = jnp.concatenate([p, q], 0)
        hi = v.astype(BF16)
        rest = v - hi.astype(F32)
        mid = rest.astype(BF16)
        low = (rest - mid.astype(F32)).astype(BF16)
        out = lax.dot_general(jnp.concatenate([hi, mid, low], 1), self.diff, (((1,), (0,)), ((), ())),
                              preferred_element_type=F32)
        return out[0 : self.xr], out[self.xr :]

    def zup(self, v):
        return jnp.where(self.z_last, 0.0, pltpu.roll(v, 127, 1)) - v

    def xup(self, v):
        return pltpu.roll(v, self.xr - 1, 0) - v

    def xdn(self, v):
        return v - pltpu.roll(v, 1, 0)

    def rows(self, e, h, start, stop):
        load = lambda ref, y: (ref[0, y], ref[1, y], ref[2, y])
        cur, now = load(e, start), None
        for y in range(start, stop):
            up = load(e, y + 1)
            below = now
            k = self.h_low if y < FH else self.h_in
            ex, ey, ez = cur
            now = (
                h[0, y] - k * ((up[2] - ez) - self.zup(ey)),
                h[1, y] - k * (self.zup(ex) - self.xup(ez)),
                h[2, y] - k * (self.xup(ey) - (up[0] - ex)),
            )
            for c in range(3):
                h[c, y] = now[c]
            if y > start:
                hx, hy, hz = now
                k = self.cx[y]
                zy, zx = self.zdn(hy, hx)
                yield y, cur, (
                    k * ((hz - below[2]) - zy),
                    k * (zx - self.xdn(hz)),
                    k * (self.xdn(hy) - (hx - below[0])),
                )
            cur = up


def pick(values):
    w = lax.axis_index("wl")
    value = F32(values[0])
    for i in range(1, len(values)):
        value = jnp.where(w == i, F32(values[i]), value)
    return value


def fill_own(refs, bigs, xl, yl):
    for ref, big in zip(refs, bigs):
        for c in range(3):
            for y in range(yl):
                big[c, FH + y, 0:xl, :] = ref[pl.ds(c * xl * yl + y, xl, stride=yl), :]


def put_out(big, out, xl, yl):
    for c in range(3):
        for y in range(yl):
            out[pl.ds(c * xl * yl + y, xl, stride=yl), :] = big[c, FH + y, 0:xl, :]


def forward_body(src, mon, fe, fh, co, prof_t, ra, rb, rx, rda, rdb, out, cx, e1, e2, e3, e0, h, sx, *, xl, yl, signals):
    xr, yr = xl + 8, yl + 2 * FH
    gy = lax.axis_index("gy")
    src_l = src[0]
    own, halo = pl.ds(0, xl), pl.ds(xl, 8)

    def put(name, c, row, cols, value):
        if name == "co":
            cx[row, cols, :] = value
        else:
            (e0 if name == "fe" else h)[c, row, cols, :] = value

    to = Halo(mon[0], xl, yl, put)
    fill_own((fe, fh), (e0, h), xl, yl)
    for y in range(yl):
        cx[FH + y, own, :] = co[y]
    names = FWD + ("co",)
    raw, win = x_parts(yl)
    to.tiles(rx, raw, win, names, lambda y: FH + y)
    at_src = lax.broadcasted_iota(jnp.int32, (xl, 128), 1) == src_l
    at_src8 = lax.broadcasted_iota(jnp.int32, (8, 128), 1) == src_l

    def source(row, wide, tile, lane):
        sx[row, own, :] = jnp.where(at_src, jnp.broadcast_to(wide[:, lane : lane + 1], (xl, 128)), 0.0)
        sx[row, halo, :] = jnp.where(at_src8, jnp.broadcast_to(tile[:, lane : lane + 1], (8, 128)), 0.0)

    prof, prof_x = prof_t[...], rx[rx.shape[0] - 1] * to.keep
    for y in range(yl):
        source(FH + y, prof, prof_x, y)
    for ref, ref_d, high in ((ra, rda, gy % 2 == 0), (rb, rdb, gy % 2 == 1)):
        to.side(ref, F_RAW, F_WIN, high)
        to.tiles(ref_d, C_RAW, C_WIN, names, lambda i, high=high: to.row(i, high))
        prof_y, prof_d = ref[ref.shape[0] - 1], ref_d[ref_d.shape[0] - 1] * to.keep
        for i in range(FH):
            source(to.row(i, high), prof_y, prof_d, PROF + i)
    step = Stepper(xl, yl, cx)
    runs = (e0, e1, e2, e3)
    for k in range(STEPS):
        new = runs[k + 1]
        signal = pick([s[k] for s in signals])
        for y, cur, inc in step.rows(runs[k], h, k, yr - 1 - k):
            new[0, y] = cur[0] + inc[0] + signal * sx[y]
            new[1, y] = cur[1] + inc[1]
            new[2, y] = cur[2] + inc[2]
    put_out(e3, out, xl, yl)


def adjoint_body(mon, ae, ah, cx, e1, e2, e3, ra, rb, rx, rda, rdb, out, grad, a, g, *, xl, yl, omegas):
    yr = yl + 2 * FH
    gy = lax.axis_index("gy")

    def put(name, c, row, cols, value):
        (a if name == "ae" else g)[c, row, cols, :] = value

    to = Halo(mon[0], xl, yl, put)
    fill_own((ae, ah), (a, g), xl, yl)
    raw, win = x_parts(yl)
    to.tiles(rx, raw, win, ADJ, lambda y: FH + y)
    for ref, ref_d, high in ((ra, rda, gy % 2 == 0), (rb, rdb, gy % 2 == 1)):
        to.side(ref, A_RAW, [], high)
        to.tiles(ref_d, C_RAW, C_WIN, ADJ, lambda i, high=high: to.row(i, high))
    step = Stepper(xl, yl, cx)
    at_mon = step.lane == mon[0]
    total = [None] * yl
    for j in range(STEPS):
        seen = (e3, e2, e1)[j]
        for y, cur, inc in step.rows(a, g, FH - AH + j, yr - AH - j):
            for c in range(3):
                f = seen[c, y]
                v = cur[c] + inc[c] + jnp.where(at_mon, 2.0 * DT * f, 0.0)
                a[c, y] = v
                if FH <= y < FH + yl:
                    t = (f * v)[0:xl]
                    i = y - FH
                    total[i] = t if total[i] is None else total[i] + t
    scale = pick([o * o for o in omegas])
    lane = step.lane[0:xl]
    packed = jnp.zeros((xl, 128), F32)
    wide = 128 // yl
    for y in range(yl):
        moved = pltpu.roll(total[y] * scale, (wide * y - Z0) % 128, 1)
        packed = jnp.where((lane >= wide * y) & (lane < wide * (y + 1)), moved, packed)
    grad[...] = packed
    put_out(a, out, xl, yl)


def sum_body(*refs, owned, xl, yl):
    *parts, out, turn = refs
    w = lax.axis_index("wl")
    acc = parts[0][...]
    for p in parts[1:]:
        acc = acc + p[...]
    turn[...] = jnp.transpose(acc)
    for i in range(owned):
        out[i] = turn[pl.ds(owned * w + i, yl, stride=128 // yl), :]


def per_device(fe, fh, ae, ah, background, design, source_profile, source_layer, monitor_layer):
    _, _, xl, yl, nz = fe.shape
    nw = lax.axis_size("wl")
    owned = design.shape[0]
    xr, yr = xl + 8, yl + 2 * FH
    flat = [v.reshape(3 * xl * yl, nz) for v in (fe, fh, ae, ah)] + [background.reshape(xl * yl, nz)]
    sp = jnp.transpose(source_profile[0])
    shape = lambda *s: jax.ShapeDtypeStruct(s, F32)
    smem = pl.BlockSpec(memory_space=pltpu.SMEM)
    vmem = pl.BlockSpec(memory_space=pltpu.VMEM)
    hbm = pl.BlockSpec(memory_space=pltpu.HBM)
    ext = lambda *s: pltpu.VMEM(s, F32)
    field = (3, yr, xr, nz)

    def call(body, name, out, specs, scratch=()):
        return pl.pallas_call(
            body, out_shape=tuple(shape(*s) for s in out), in_specs=specs, out_specs=(vmem,) * len(out),
            scratch_shapes=list(scratch), name=name,
            compiler_params=pltpu.CompilerParams(vmem_limit_bytes=20 * 1024 * 1024),
        )

    def over_wl(v):
        return [v] + [lax.ppermute(v, "wl", [(i, i ^ k) for i in range(nw)]) for k in range(1, nw)]

    raw, win = x_parts(yl)
    f_side = (len(F_RAW) + ceil(len(F_WIN), PER), xl, nz)
    a_side = (len(A_RAW), xl, nz)
    corner = (ceil(len(C_RAW), 2) + ceil(len(C_WIN), PER), 8, nz)
    beside = (ceil(len(raw), 2) + ceil(len(win), PER) + 1, 8, nz)

    layers = over_wl(jnp.transpose(design, (0, 2, 1)))
    held = call(fetch_body, "fetch", [v.shape for v in flat], [hbm] * 5, [pltpu.SemaphoreType.DMA((5,))])(
        *[pltpu.with_memory_space_constraint(v, pltpu.HBM) for v in flat])
    co, prof_t, fa, fb, aa, ab, px, da, db = call(
        lambda *r: send_body(*r, xl=xl, yl=yl, nw=nw, owned=owned), "send",
        [(yl, xl, nz), (xl, nz), f_side, f_side, a_side, a_side, beside, corner, corner],
        [smem] + [vmem] * (6 + nw), [ext(128, 128)],
    )(monitor_layer, *held, sp, *layers)
    rfa, rfb = swap(fa, False, 0), swap(fb, False, 1)
    rx = swap(px, True, None)
    rda, rdb = swap(da, True, 0), swap(db, True, 1)
    raa, rab = swap(aa, False, 0), swap(ab, False, 1)
    f32 = np.float32
    omegas = [f32(2.0 * math.pi) / (f32(16.0) + f32(32.0) * f32(i) / f32(nw)) for i in range(nw)]
    signals = [[f32(DT) * np.sin(f32(o * f32((k + 1) * DT))) for k in range(STEPS)] for o in omegas]
    out_f, cx, e1, e2, e3 = call(
        lambda *r: forward_body(*r, xl=xl, yl=yl, signals=signals), "forward",
        [flat[0].shape, (yr, xr, nz), field, field, field], [smem, smem] + [vmem] * 9,
        [ext(*field), ext(*field), ext(yr, xr, nz)],
    )(source_layer, monitor_layer, held[0], held[1], co, prof_t, rfa, rfb, rx, rda, rdb)
    out_a, grad = call(
        lambda *r: adjoint_body(*r, xl=xl, yl=yl, omegas=omegas), "adjoint",
        [flat[0].shape, (xl, nz)], [smem] + [vmem] * 11, [ext(*field), ext(*field)],
    )(monitor_layer, held[2], held[3], cx, e1, e2, e3, raa, rab, rx, rda, rdb)
    (gradient,) = call(
        lambda *r: sum_body(*r, owned=owned, xl=xl, yl=yl), "gather_sum",
        [(owned, yl, xl)], [vmem] * nw, [ext(128, xl)],
    )(*over_wl(grad))
    block = (1, 3, xl, yl, nz)
    return (out_f.reshape(block), out_a.reshape(block), jnp.transpose(gradient, (0, 2, 1)))


def solution(mesh):
    field = P("wl", None, "gx", "gy", None)
    return jax.shard_map(
        per_device,
        mesh=mesh,
        in_specs=(field, field, field, field, P("gx", "gy", None), P("wl", "gx", "gy"),
                  P("wl", "gx", "gy"), P("wl"), P("wl")),
        out_specs=(field, field, P("wl", "gx", "gy")),
        check_vma=False,
    )
```

time: 121 us -> 41.8 us (0.35)
  the two profiles are of different devices: /device:TPU:0 before, /device:TPU:9 now
where the time goes in v2:
time: 41.8 us; the launch traced here: 41.3 us
  starting transfers between devices  20.7 us (50%)
  waiting for transfers between devices  9.47 us (23%)
  Pallas kernels  9.13 us (22%)
  between operations  2.03 us (5%)
    ppermute x7, starting transfers between devices, swap(): return lax.ppermute(block, ('gx', 'gy'), route)  12.2 us
    ppermute x6, starting transfers between devices, over_wl(): lax.ppermute(v, 'wl', [(i, i ^ k) for i in range(nw)])  8.49 us
    ppermute x7, waiting for transfers between devices, swap(): return lax.ppermute(block, ('gx', 'gy'), route)  7.8 us
    pallas_call x1, Pallas kernels, per_device(): call(lambda *r: forward_body(*r, xl=xl, yl=yl, signals=signals), 'forward...  3.16 us
    pallas_call x1, Pallas kernels, per_device(): call(lambda *r: adjoint_body(*r, xl=xl, yl=yl, omegas=omegas), 'adjoint',...  2.45 us
    ppermute x6, waiting for transfers between devices, over_wl(): lax.ppermute(v, 'wl', [(i, i ^ k) for i in range(nw)])  1.67 us
    pallas_call x1, Pallas kernels, per_device(): call(fetch_body, 'fetch', [v.shape for v in flat], [hbm] * 5, [pltpu.Sema...  1.42 us
    pallas_call x1, Pallas kernels, per_device(): call(lambda *r: send_body(*r, xl=xl, yl=yl, nw=nw, owned=owned), 'send',...  1.39 us
  transfers between devices with their start and end apart: 13, of which 5 were waited for; matrix products, arithmetic and copies ran while one was open for 0% of the time, Pallas kernels for 11%

profile of v2, /device:TPU:9, one launch (start us, length us, event | category | flops | bytes accessed | tf_op | source)
XLA Modules:
  0.0 41.3 jit_solution(11162170010305850360)
XLA Ops:
  0.7 1.8 %collective-permute-start.2 = (f32[2,8,32]{2,1,0:T(8,128)}, f32[2,8,32]{2,1,0:T(8,128)S(1)}, u32[]{:S(2)}, u32[]{:S(2)}) collective-permute-start(f32[2,8,32]{2,1,0:T(8,128)} %bitcast.12), channel_id=1, source_target_pairs={{0,24},{8,16},{16,8},{24,0},{1,25},{9,17},{17,9},{25,1},{2,26},{10... | collective-permute-start | bytes 6152 | tf_op jit(solution)/shard_map/ppermute | solution.py:387
  2.5 0.3 collective-permute-start.1
  2.7 0.2 collective-permute-start
  3.6 1.4 %fetch.1 = (f32[768,128]{1,0:T(8,128)S(1)}, f32[768,128]{1,0:T(8,128)S(1)}, f32[768,128]{1,0:T(8,128)S(1)}, f32[768,128]{1,0:T(8,128)S(1)}, f32[256,128]{1,0:T(8,128)S(1)}) custom-call(f32[768,128]{1,0:T(8,128)} %bitcast.17, f32[768,128]{1,0:T(8,128)} %bitcast.18, f32[768,128]{1,0:T(8,128)} %bitcast.19, f32[768,128]{1,0:T(8,128)} %bitcast.20, ...), custom_call_target="tpu_custom_call" | custom-call | tf_op jit(solution)/shard_map/fetch/pallas_call | solution.py:396
  5.0 0.0 collective-permute-done.2.r_10_
  5.1 0.1 collective-permute-done.1.r_9_
  5.2 0.0 collective-permute-done.r_8_
  5.2 0.0 copy-done.1
  5.2 1.4 %send.1 = (f32[8,32,128]{2,1,0:T(8,128)S(1)}, f32[32,128]{1,0:T(8,128)S(1)}, f32[22,32,128]{2,1,0:T(8,128)S(1)}, f32[22,32,128]{2,1,0:T(8,128)S(1)}, f32[18,32,1...) custom-call(s32[1]{0:T(128)S(6)} %copy.13.r_0_.r_1_, ...), custom_call_target="tpu_custom_call" | custom-call | tf_op jit(solution)/shard_map/send/pallas_call | solution.py:398
  6.6 1.2 %collective-permute-start.6 = (f32[24,8,128]{2,1,0:T(8,128)S(1)}, f32[24,8,128]{2,1,0:T(8,128)S(1)}, u32[]{:S(2)}, u32[]{:S(2)}) collective-permute-start(f32[24,8,128]{2,1,0:T(8,128)S(1)} %get-tuple-element.34), channel_id=1, source_target_pairs={{0,5},{1,4},{2,7},{3,6},{4,1},{5,0},{6,3},{7,2},{8,13},{9,12},{10,... | collective-permute-start | bytes 294920 | tf_op jit(solution)/shard_map/ppermute | solution.py:32
  7.8 1.3 %collective-permute-start.3 = (f32[22,32,128]{2,1,0:T(8,128)S(1)}, f32[22,32,128]{2,1,0:T(8,128)S(1)}, u32[]{:S(2)}, u32[]{:S(2)}) collective-permute-start(f32[22,32,128]{2,1,0:T(8,128)S(1)} %get-tuple-element.31), channel_id=1, source_target_pairs={{0,1},{1,0},{2,3},{3,2},{4,5},{5,4},{6,7},{7,6},{8,9},{9,8},{10,11... | collective-permute-start | bytes 1081352 | tf_op jit(solution)/shard_map/ppermute | solution.py:32
  9.1 3.2 %collective-permute-start.4 = (f32[22,32,128]{2,1,0:T(8,128)S(1)}, f32[22,32,128]{2,1,0:T(8,128)S(1)}, u32[]{:S(2)}, u32[]{:S(2)}) collective-permute-start(f32[22,32,128]{2,1,0:T(8,128)S(1)} %get-tuple-element.32), channel_id=1, source_target_pairs={{1,2},{2,1},{5,6},{6,5},{9,10},{10,9},{13,14},{14,13},{17,18},{18,... | collective-permute-start | bytes 1081352 | tf_op jit(solution)/shard_map/ppermute | solution.py:32
  12.3 2.0 %collective-permute-start.7 = (f32[24,8,128]{2,1,0:T(8,128)S(1)}, f32[24,8,128]{2,1,0:T(8,128)S(1)}, u32[]{:S(2)}, u32[]{:S(2)}) collective-permute-start(f32[24,8,128]{2,1,0:T(8,128)S(1)} %get-tuple-element.35), channel_id=1, source_target_pairs={{1,6},{2,5},{5,2},{6,1},{9,14},{10,13},{13,10},{14,9},{17,22},{18,... | collective-permute-start | bytes 294920 | tf_op jit(solution)/shard_map/ppermute | solution.py:32
  14.3 0.1 collective-permute-start.8
  14.4 0.0 collective-permute-done.6.r_9_.r_10_
  14.4 3.2 %collective-permute-start.9 = (f32[18,32,128]{2,1,0:T(8,128)S(1)}, f32[18,32,128]{2,1,0:T(8,128)S(1)}, u32[]{:S(2)}, u32[]{:S(2)}) collective-permute-start(f32[18,32,128]{2,1,0:T(8,128)S(1)} %get-tuple-element.42), channel_id=1, source_target_pairs={{1,2},{2,1},{5,6},{6,5},{9,10},{10,9},{13,14},{14,13},{17,18},{18,... | collective-permute-start | bytes 884744 | tf_op jit(solution)/shard_map/ppermute | solution.py:32
  17.6 3.5 %collective-permute-done.7.r_10_.r_11_ = f32[24,8,128]{2,1,0:T(8,128)S(1)} collective-permute-done((f32[24,8,128]{2,1,0:T(8,128)S(1)}, f32[24,8,128]{2,1,0:T(8,128)S(1)}, u32[]{:S(2)}, u32[]{:S(2)}) %collective-permute-start.7) | collective-permute-done | bytes 98336 | tf_op jit(solution)/shard_map/ppermute | solution.py:32
  21.1 1.2 %collective-permute-start.5 = (f32[60,8,128]{2,1,0:T(8,128)S(1)}, f32[60,8,128]{2,1,0:T(8,128)S(1)}, u32[]{:S(2)}, u32[]{:S(2)}) collective-permute-start(f32[60,8,128]{2,1,0:T(8,128)S(1)} %get-tuple-element.33), channel_id=1, source_target_pairs={{0,4},{1,5},{2,6},{3,7},{4,0},{5,1},{6,2},{7,3},{8,12},{9,13},{10,... | collective-permute-start | bytes 737288 | tf_op jit(solution)/shard_map/ppermute | solution.py:32
  23.0 4.3 %collective-permute-done.5.r_8_.r_9_ = f32[60,8,128]{2,1,0:T(8,128)S(1)} collective-permute-done((f32[60,8,128]{2,1,0:T(8,128)S(1)}, f32[60,8,128]{2,1,0:T(8,128)S(1)}, u32[]{:S(2)}, u32[]{:S(2)}) %collective-permute-start.5) | collective-permute-done | bytes 245792 | tf_op jit(solution)/shard_map/ppermute | solution.py:32
  27.3 0.0 collective-permute-done.3.r_6_
  27.3 0.0 collective-permute-done.4.r_7_
  27.3 3.2 %forward.1 = (f32[768,128]{1,0:T(8,128)}, f32[18,40,128]{2,1,0:T(8,128)S(1)}, f32[3,18,40,128]{3,2,1,0:T(8,128)S(1)}, f32[3,18,40,128]{3,2,1,0:T(8,128)S(1)}, f32[3,18,40,128]{3,2,1,0:T(8,128)S(1)}) custom-call(s32[1]{0:T(128)S(6)} %copy.12.r_0_, s32[1]{0:T(128)S(6)} %copy.13.r_0_.r_1_, f32[768,128]{1,0:T(8,128)S(1)} %get-tuple-element.24.r_1_.r_2_, ...), custom_call_target="tpu_custom_call" | custom-call | tf_op jit(solution)/shard_map/forward/pallas_call | solution.py:410
  30.5 0.0 collective-permute-done.8.r_7_
  30.5 0.0 collective-permute-done.9.r_8_
  30.5 2.5 %adjoint.1 = (f32[768,128]{1,0:T(8,128)}, f32[32,128]{1,0:T(8,128)S(1)}) custom-call(s32[1]{0:T(128)S(6)} %copy.13.r_0_.r_1_, f32[768,128]{1,0:T(8,128)S(1)} %get-tuple-element.26.r_3_.r_1_, f32[768,128]{1,0:T(8,128)S(1)} %get-tuple-element.27.r_4_.r_2_, f32[18,40,128]{2,1,0:T(8,128)S(1)} %get-tuple-element.37.r_3_, ...), custom_call_target="tpu_custom_call" | custom-call | tf_op jit(solution)/shard_map/adjoint/pallas_call | solution.py:415
  32.9 5.1 %collective-permute-start.12 = (f32[32,128]{1,0:T(8,128)S(1)}, f32[32,128]{1,0:T(8,128)S(1)}, u32[]{:S(2)}, u32[]{:S(2)}) collective-permute-start(f32[32,128]{1,0:T(8,128)S(1)} %get-tuple-element.44.r_0_), channel_id=1, source_target_pairs={{0,24},{8,16},{16,8},{24,0},{1,25},{9,17},{17,9},{25,1},{2,26},{10... | collective-permute-start | bytes 49160 | tf_op jit(solution)/shard_map/ppermute | solution.py:387
  38.0 1.1 %collective-permute-start.11 = (f32[32,128]{1,0:T(8,128)S(1)}, f32[32,128]{1,0:T(8,128)S(1)}, u32[]{:S(2)}, u32[]{:S(2)}) collective-permute-start(f32[32,128]{1,0:T(8,128)S(1)} %get-tuple-element.44.r_0_), channel_id=1, source_target_pairs={{0,16},{8,24},{16,0},{24,8},{1,17},{9,25},{17,1},{25,9},{2,18},{10... | collective-permute-start | bytes 49160 | tf_op jit(solution)/shard_map/ppermute | solution.py:387
  39.1 0.0 collective-permute-start.10
  39.1 0.3 collective-permute-done.12.r_3_
  39.5 1.2 %collective-permute-done.11.r_2_ = f32[32,128]{1,0:T(8,128)S(1)} collective-permute-done((f32[32,128]{1,0:T(8,128)S(1)}, f32[32,128]{1,0:T(8,128)S(1)}, u32[]{:S(2)}, u32[]{:S(2)}) %collective-permute-start.11) | collective-permute-done | bytes 16416 | tf_op jit(solution)/shard_map/ppermute | solution.py:387
  40.6 0.0 collective-permute-done.10.r_1_
  40.6 0.7 %gather_sum.1 = f32[2,8,32]{2,1,0:T(8,128)} custom-call(f32[32,128]{1,0:T(8,128)S(1)} %get-tuple-element.44.r_0_, f32[32,128]{1,0:T(8,128)S(1)} %collective-permute-done.10.r_1_, f32[32,128]{1,0:T(8,128)S(1)} %collective-permute-done.11.r_2_, f32[32,128]{1,0:T(8,128)S(1)} %collective-permute-done.12.r_3_), custom_call_target="tpu_custom_call" | custom-call | tf_op jit(solution)/shard_map/gather_sum/pallas_call | solution.py:419
  (3 shorter events, 0.0 us)
Async XLA Ops:
  0.6 4.6 %copy-start = (f32[2,32,8]{1,2,0:T(8,128)S(1)}, f32[2,32,8]{1,2,0:T(8,128)}, u32[]{:S(2)}) copy-start(f32[2,32,8]{1,2,0:T(8,128)} %param.14) | copy-start | bytes 6148
  0.6 4.6 %copy-start.1 = (f32[1,32,8]{1,2,0:T(8,128)S(1)}, f32[1,32,8]{1,2,0:T(8,128)}, u32[]{:S(2)}) copy-start(f32[1,32,8]{1,2,0:T(8,128)} %param.15) | copy-start | bytes 3076
  0.7 4.4 %collective-permute-start.2 = (f32[2,8,32]{2,1,0:T(8,128)}, f32[2,8,32]{2,1,0:T(8,128)S(1)}, u32[]{:S(2)}, u32[]{:S(2)}) collective-permute-start(f32[2,8,32]{2,1,0:T(8,128)} %bitcast.12), channel_id=1, source_target_pairs={{0,24},{8,16},{16,8},{24,0},{1,25},{9,17},{17,9},{25,1},{2,26},{10... | collective-permute-start | bytes 6152 | tf_op jit(solution)/shard_map/ppermute | solution.py:387
  2.5 2.7 %collective-permute-start.1 = (f32[2,8,32]{2,1,0:T(8,128)}, f32[2,8,32]{2,1,0:T(8,128)S(1)}, u32[]{:S(2)}, u32[]{:S(2)}) collective-permute-start(f32[2,8,32]{2,1,0:T(8,128)} %bitcast.13), channel_id=1, source_target_pairs={{0,16},{8,24},{16,0},{24,8},{1,17},{9,25},{17,1},{25,9},{2,18},{10... | collective-permute-start | bytes 6152 | tf_op jit(solution)/shard_map/ppermute | solution.py:387
  2.7 2.5 %collective-permute-start = (f32[2,8,32]{2,1,0:T(8,128)}, f32[2,8,32]{2,1,0:T(8,128)S(1)}, u32[]{:S(2)}, u32[]{:S(2)}) collective-permute-start(f32[2,8,32]{2,1,0:T(8,128)} %bitcast.14), channel_id=1, source_target_pairs={{0,8},{8,0},{16,24},{24,16},{1,9},{9,1},{17,25},{25,17},{2,10},{10... | collective-permute-start | bytes 6152 | tf_op jit(solution)/shard_map/ppermute | solution.py:387
  6.6 7.8 %collective-permute-start.6 = (f32[24,8,128]{2,1,0:T(8,128)S(1)}, f32[24,8,128]{2,1,0:T(8,128)S(1)}, u32[]{:S(2)}, u32[]{:S(2)}) collective-permute-start(f32[24,8,128]{2,1,0:T(8,128)S(1)} %get-tuple-element.34), channel_id=1, source_target_pairs={{0,5},{1,4},{2,7},{3,6},{4,1},{5,0},{6,3},{7,2},{8,13},{9,12},{10,... | collective-permute-start | bytes 294920 | tf_op jit(solution)/shard_map/ppermute | solution.py:32
  7.8 19.5 %collective-permute-start.3 = (f32[22,32,128]{2,1,0:T(8,128)S(1)}, f32[22,32,128]{2,1,0:T(8,128)S(1)}, u32[]{:S(2)}, u32[]{:S(2)}) collective-permute-start(f32[22,32,128]{2,1,0:T(8,128)S(1)} %get-tuple-element.31), channel_id=1, source_target_pairs={{0,1},{1,0},{2,3},{3,2},{4,5},{5,4},{6,7},{7,6},{8,9},{9,8},{10,11... | collective-permute-start | bytes 1081352 | tf_op jit(solution)/shard_map/ppermute | solution.py:32
  9.1 18.2 %collective-permute-start.4 = (f32[22,32,128]{2,1,0:T(8,128)S(1)}, f32[22,32,128]{2,1,0:T(8,128)S(1)}, u32[]{:S(2)}, u32[]{:S(2)}) collective-permute-start(f32[22,32,128]{2,1,0:T(8,128)S(1)} %get-tuple-element.32), channel_id=1, source_target_pairs={{1,2},{2,1},{5,6},{6,5},{9,10},{10,9},{13,14},{14,13},{17,18},{18,... | collective-permute-start | bytes 1081352 | tf_op jit(solution)/shard_map/ppermute | solution.py:32
  12.3 8.8 %collective-permute-start.7 = (f32[24,8,128]{2,1,0:T(8,128)S(1)}, f32[24,8,128]{2,1,0:T(8,128)S(1)}, u32[]{:S(2)}, u32[]{:S(2)}) collective-permute-start(f32[24,8,128]{2,1,0:T(8,128)S(1)} %get-tuple-element.35), channel_id=1, source_target_pairs={{1,6},{2,5},{5,2},{6,1},{9,14},{10,13},{13,10},{14,9},{17,22},{18,... | collective-permute-start | bytes 294920 | tf_op jit(solution)/shard_map/ppermute | solution.py:32
  14.3 16.1 %collective-permute-start.8 = (f32[18,32,128]{2,1,0:T(8,128)S(1)}, f32[18,32,128]{2,1,0:T(8,128)S(1)}, u32[]{:S(2)}, u32[]{:S(2)}) collective-permute-start(f32[18,32,128]{2,1,0:T(8,128)S(1)} %get-tuple-element.41), channel_id=1, source_target_pairs={{0,1},{1,0},{2,3},{3,2},{4,5},{5,4},{6,7},{7,6},{8,9},{9,8},{10,11... | collective-permute-start | bytes 884744 | tf_op jit(solution)/shard_map/ppermute | solution.py:32
  14.4 16.1 %collective-permute-start.9 = (f32[18,32,128]{2,1,0:T(8,128)S(1)}, f32[18,32,128]{2,1,0:T(8,128)S(1)}, u32[]{:S(2)}, u32[]{:S(2)}) collective-permute-start(f32[18,32,128]{2,1,0:T(8,128)S(1)} %get-tuple-element.42), channel_id=1, source_target_pairs={{1,2},{2,1},{5,6},{6,5},{9,10},{10,9},{13,14},{14,13},{17,18},{18,... | collective-permute-start | bytes 884744 | tf_op jit(solution)/shard_map/ppermute | solution.py:32
  21.1 6.2 %collective-permute-start.5 = (f32[60,8,128]{2,1,0:T(8,128)S(1)}, f32[60,8,128]{2,1,0:T(8,128)S(1)}, u32[]{:S(2)}, u32[]{:S(2)}) collective-permute-start(f32[60,8,128]{2,1,0:T(8,128)S(1)} %get-tuple-element.33), channel_id=1, source_target_pairs={{0,4},{1,5},{2,6},{3,7},{4,0},{5,1},{6,2},{7,3},{8,12},{9,13},{10,... | collective-permute-start | bytes 737288 | tf_op jit(solution)/shard_map/ppermute | solution.py:32
  32.9 6.5 %collective-permute-start.12 = (f32[32,128]{1,0:T(8,128)S(1)}, f32[32,128]{1,0:T(8,128)S(1)}, u32[]{:S(2)}, u32[]{:S(2)}) collective-permute-start(f32[32,128]{1,0:T(8,128)S(1)} %get-tuple-element.44.r_0_), channel_id=1, source_target_pairs={{0,24},{8,16},{16,8},{24,0},{1,25},{9,17},{17,9},{25,1},{2,26},{10... | collective-permute-start | bytes 49160 | tf_op jit(solution)/shard_map/ppermute | solution.py:387
  38.0 2.6 %collective-permute-start.11 = (f32[32,128]{1,0:T(8,128)S(1)}, f32[32,128]{1,0:T(8,128)S(1)}, u32[]{:S(2)}, u32[]{:S(2)}) collective-permute-start(f32[32,128]{1,0:T(8,128)S(1)} %get-tuple-element.44.r_0_), channel_id=1, source_target_pairs={{0,16},{8,24},{16,0},{24,8},{1,17},{9,25},{17,1},{25,9},{2,18},{10... | collective-permute-start | bytes 49160 | tf_op jit(solution)/shard_map/ppermute | solution.py:387
  39.1 1.5 %collective-permute-start.10 = (f32[32,128]{1,0:T(8,128)S(1)}, f32[32,128]{1,0:T(8,128)S(1)}, u32[]{:S(2)}, u32[]{:S(2)}) collective-permute-start(f32[32,128]{1,0:T(8,128)S(1)} %get-tuple-element.44.r_0_), channel_id=1, source_target_pairs={{0,8},{8,0},{16,24},{24,16},{1,9},{9,1},{17,25},{25,17},{2,10},{10... | collective-permute-start | bytes 49160 | tf_op jit(solution)/shard_map/ppermute | solution.py:387

commit v3 on v2

--- a/solution.py
+++ b/solution.py
@@ -33,11 +33,17 @@
 
 
 FWD, ADJ = ("fe", "fh"), ("ae", "ah")
-F_RAW = [(n, c, i) for n in FWD for c in range(3) for i in range(AH)] + [("co", 0, i) for i in range(2)]
-A_RAW = [(n, c, i) for n in ADJ for c in range(3) for i in range(AH)]
-F_WIN = [(n, c, i) for n in FWD for c in range(3) for i in range(AH, FH)] + [("co", 0, i) for i in (2, 3)]
-C_RAW = [(n, c, i) for n in FWD + ADJ for c in range(3) for i in range(AH)] + [("co", 0, i) for i in range(2)]
-C_WIN = [(n, c, i) for n in FWD for c in range(3) for i in range(FH)] + [("co", 0, i) for i in range(4)]
+def side_parts(e, h):
+    return [(e, c, i) for c in range(3) for i in range(2)] + [(h, c, i) for c in range(3) for i in range(2)] + [(h, 0, 2), (h, 2, 2)]
+
+
+CO_RAW, CO_WIN = [("co", 0, i) for i in (0, 1)], [("co", 0, i) for i in (2, 3)]
+F_RAW = side_parts(*FWD) + CO_RAW
+A_RAW = side_parts(*ADJ)
+F_WIN = [("fe", c, i) for c in range(3) for i in (2, 3, 4)] + [("fh", 1, 2)]
+F_WIN += [("fh", c, i) for c in range(3) for i in (3, 4)] + CO_WIN
+C_RAW = side_parts(*FWD) + [("fe", 1, 2)] + A_RAW + [("ae", 1, 2)] + CO_RAW
+C_WIN = [(n, c, i) for n in FWD for c in range(3) for i in range(FH)] + CO_RAW + CO_WIN
 
 
 def x_parts(yl):
@@ -51,18 +57,56 @@
     return -(-a // b)
 
 
-def fetch_body(*refs):
-    n = len(refs) // 2
-    ins, outs, sems = refs[:n], refs[n : 2 * n], refs[2 * n]
-    copies = [pltpu.make_async_copy(s, d, sems.at[i]) for i, (s, d) in enumerate(zip(ins, outs))]
+def stepped(e, h, out, xl, yl):
+    sub = lax.broadcasted_iota(jnp.int32, (xl, 128), 0)
+    x_last = sub == xl - 1
+    z_last = lax.broadcasted_iota(jnp.int32, (xl, 128), 1) == 127
+    zup = lambda v: jnp.where(z_last, 0.0, pltpu.roll(v, 127, 1)) - v
+    xup = lambda v: jnp.where(x_last, 0.0, pltpu.roll(v, xl - 1, 0)) - v
+    row = lambda ref, c, y: ref[pl.ds(c * xl * yl + y, xl, stride=yl), :]
+    cur = [row(e, c, 0) for c in range(3)]
+    for y in range(yl - 1):
+        up = [row(e, c, y + 1) for c in range(3)]
+        ex, ey, ez = cur
+        out[0, y] = row(h, 0, y) - DT * ((up[2] - ez) - zup(ey))
+        out[1, y] = row(h, 1, y) - DT * (zup(ex) - xup(ez))
+        out[2, y] = row(h, 2, y) - DT * (xup(ey) - (up[0] - ex))
+        cur = up
+
+
+def edge_row(e, h, h1, is_h, c, i, up, x, count, xl, yl):
+    here = jnp.where(up, yl - 1 - i, i)
+    flat = lambda ref, r: ref[pl.ds(c * xl * yl + x * yl + r, count, stride=yl), :]
+    if not is_h:
+        return flat(e, here)
+    if i in (1, 2):
+        return h1[c, here, pl.ds(x, count), :]
+    return jnp.where(up, flat(h, yl - 1 - i), h1[c, i, pl.ds(x, count), :])
+
+
+def fetch_body(ae, ah, fe, fh, bg, *rest, xl, yl):
+    outs, (h1, aa, ab, sems) = rest[:5], rest[5:]
+    copies = [pltpu.make_async_copy(s, d, sems.at[i]) for i, (s, d) in enumerate(zip((ae, ah, fe, fh, bg), outs))]
     for c in copies:
         c.start()
-    for c in copies:
+    copies[0].wait()
+    copies[1].wait()
+    e, h = outs[0], outs[1]
+    gy = lax.axis_index("gy")
+    stepped(e, h, h1, xl, yl)
+    for u, (name, c, i) in enumerate(A_RAW):
+        for dst, up in ((aa, gy % 2 == 0), (ab, gy % 2 == 1)):
+            dst[u] = edge_row(e, h, h1, name == "ah", c, i, up, 0, xl, xl, yl)
+    for c in copies[2:]:
         c.wait()
 
 
-def send_body(mon, fe, fh, ae, ah, bg, sp, *rest, xl, yl, nw, owned):
-    parts, (co, prof_t, fa, fb, aa, ab, px, da, db, turn) = rest[:nw], rest[nw:]
+def first_body(fe, fh, h1, *, xl, yl):
+    stepped(fe, fh, h1, xl, yl)
+
+
+def send_body(mon, fe, fh, ae, ah, bg, fh1, ah1, sp, *rest, xl, yl, nw, owned):
+    parts, (co, prof_t, fa, fb, px, da, db, turn) = rest[:nw], rest[nw:]
     gx, gy, w = lax.axis_index("gx"), lax.axis_index("gy"), lax.axis_index("wl")
     plane = xl * yl
     depth = nw * owned
@@ -83,45 +127,47 @@
     prof_t[...] = jnp.transpose(turn[...])[0:xl]
     low_x = gx == 0
     x8 = pl.multiple_of(jnp.where(low_x, xl - 8, 0), 8)
-    x4 = jnp.where(low_x, xl - 4, 0)
-
-    def rows(name, c, r, x, count):
+
+    def beside(name, c, y, x, count):
         if name == "co":
-            return co[r, pl.ds(x, count), :]
-        return refs[name][pl.ds(c * plane + x * yl + r, count, stride=yl), :]
-
-    def windows(parts, x, count, where):
+            return co[y, pl.ds(x, count), :]
+        return refs[name][pl.ds(c * plane + x * yl + y, count, stride=yl), :]
+
+    def beyond(up):
+        def rows(name, c, i, x, count):
+            if name == "co":
+                return co[jnp.where(up, yl - 1 - i, i), pl.ds(x, count), :]
+            e, h, h1 = (fe, fh, fh1) if name in FWD else (ae, ah, ah1)
+            return edge_row(e, h, h1, name in ("fh", "ah"), c, i, up, x, count, xl, yl)
+        return rows
+
+    def windows(parts, x, count, rows):
         out = []
         here = lax.broadcasted_iota(jnp.int32, (count, 128), 1)
         for t in range(ceil(len(parts), PER)):
             acc = jnp.zeros((count, 128), F32)
             for q, (name, c, i) in enumerate(parts[t * PER : (t + 1) * PER]):
-                moved = pltpu.roll(rows(name, c, where(i), x, count), (WIN * q + first) % 128, 1)
+                moved = pltpu.roll(rows(name, c, i, x, count), (WIN * q + first) % 128, 1)
                 acc = jnp.where((here >= WIN * q) & (here < WIN * (q + 1)), moved, acc)
             out.append(acc)
         return out
 
-    def tiles(dst, raw, win, where):
+    def tiles(dst, raw, win, rows):
         for n, (name, c, i) in enumerate(raw):
-            if name == "co":
-                part = pltpu.roll(rows(name, c, where(i), x8, 8), jnp.where(low_x, 4, 0), 0)[0:4]
-            else:
-                part = rows(name, c, where(i), x4, 4)
-            dst[n // 2, 4 * (n % 2) : 4 * (n % 2) + 4, :] = part
+            half = pltpu.roll(rows(name, c, i, x8, 8), jnp.where(low_x, 4, 0), 0)[0:4]
+            dst[n // 2, 4 * (n % 2) : 4 * (n % 2) + 4, :] = half
         at = ceil(len(raw), 2)
-        for tile in windows(win, x8, 8, where):
+        for tile in windows(win, x8, 8, rows):
             dst[at] = tile
             at += 1
         return at
 
-    for dst, dst_a, corner, up in ((fa, aa, da, gy % 2 == 0), (fb, ab, db, gy % 2 == 1)):
-        where = lambda i, up=up: jnp.where(up, yl - 1 - i, i)
+    for dst, corner, up in ((fa, da, gy % 2 == 0), (fb, db, gy % 2 == 1)):
+        rows = beyond(up)
         for u, (name, c, i) in enumerate(F_RAW):
-            dst[u] = rows(name, c, where(i), 0, xl)
-        for u, (name, c, i) in enumerate(A_RAW):
-            dst_a[u] = rows(name, c, where(i), 0, xl)
+            dst[u] = rows(name, c, i, 0, xl)
         at = len(F_RAW)
-        for unit in windows(F_WIN, 0, xl, where):
+        for unit in windows(F_WIN, 0, xl, rows):
             dst[at] = unit
             at += 1
         mix = dst[at - 1]
@@ -130,11 +176,11 @@
             col = jnp.where(up, prof[:, yl - 1 - i : yl - i], prof[:, i : i + 1])
             mix = jnp.where(lane == PROF + i, jnp.broadcast_to(col, (xl, 128)), mix)
         dst[at - 1] = mix
-        last = tiles(corner, C_RAW, C_WIN, where)
+        last = tiles(corner, C_RAW, C_WIN, rows)
         src8 = dst[at - 1, pl.ds(x8, 8), :]
         corner[last - 1] = jnp.where((lane8 >= PROF) & (lane8 < PROF + FH), src8, corner[last - 1])
     raw, win = x_parts(yl)
-    last = tiles(px, raw, win, lambda y: y)
+    last = tiles(px, raw, win, beside)
     px[last] = prof_t[pl.ds(x8, 8), :]
 
 
@@ -192,6 +238,8 @@
         inside_high = jnp.where((ring < xl) | (ring >= xr - FH), F32(DT), F32(0.0))
         self.h_in = jnp.where(gx == 0, inside_low, inside_high)
         self.h_low = self.h_in * jnp.where(gy == 0, 0.0, 1.0).astype(F32)
+        edge = ((ring == xl - 1) | (ring == xr - 1)).astype(F32)
+        self.h_edge = self.h_in * edge
         self.z_last = self.lane == 127
         ri = lax.broadcasted_iota(jnp.int32, (128, 128), 0)
         ci = lax.broadcasted_iota(jnp.int32, (128, 128), 1)
@@ -217,7 +265,7 @@
     def xdn(self, v):
         return v - pltpu.roll(v, 1, 0)
 
-    def rows(self, e, h, start, stop):
+    def rows(self, e, h, start, stop, given=()):
         load = lambda ref, y: (ref[0, y], ref[1, y], ref[2, y])
         cur, now = load(e, start), None
         for y in range(start, stop):
@@ -225,11 +273,19 @@
             below = now
             k = self.h_low if y < FH else self.h_in
             ex, ey, ez = cur
-            now = (
-                h[0, y] - k * ((up[2] - ez) - self.zup(ey)),
-                h[1, y] - k * (self.zup(ex) - self.xup(ez)),
-                h[2, y] - k * (self.xup(ey) - (up[0] - ex)),
-            )
+            if y in given:
+                k = self.h_edge
+                now = (
+                    h[0, y],
+                    h[1, y] + k * pltpu.roll(ez, self.xr - 1, 0),
+                    h[2, y] - k * pltpu.roll(ey, self.xr - 1, 0),
+                )
+            else:
+                now = (
+                    h[0, y] - k * ((up[2] - ez) - self.zup(ey)),
+                    h[1, y] - k * (self.zup(ex) - self.xup(ez)),
+                    h[2, y] - k * (self.xup(ey) - (up[0] - ex)),
+                )
             for c in range(3):
                 h[c, y] = now[c]
             if y > start:
@@ -242,6 +298,10 @@
                     k * (self.xdn(hy) - (hx - below[0])),
                 )
             cur = up
+
+
+def given_rows(yl):
+    return {FH - 3, FH - 2, *range(FH + yl, yl + 2 * FH)}
 
 
 def pick(values):
@@ -305,7 +365,7 @@
     for k in range(STEPS):
         new = runs[k + 1]
         signal = pick([s[k] for s in signals])
-        for y, cur, inc in step.rows(runs[k], h, k, yr - 1 - k):
+        for y, cur, inc in step.rows(runs[k], h, k, yr - 1 - k, given_rows(yl) if k == 0 else ()):
             new[0, y] = cur[0] + inc[0] + signal * sx[y]
             new[1, y] = cur[1] + inc[1]
             new[2, y] = cur[2] + inc[2]
@@ -320,6 +380,8 @@
         (a if name == "ae" else g)[c, row, cols, :] = value
 
     to = Halo(mon[0], xl, yl, put)
+    for c in range(3):
+        a[c, FH - AH] = jnp.zeros((xl + 8, 128), F32)
     fill_own((ae, ah), (a, g), xl, yl)
     raw, win = x_parts(yl)
     to.tiles(rx, raw, win, ADJ, lambda y: FH + y)
@@ -331,7 +393,7 @@
     total = [None] * yl
     for j in range(STEPS):
         seen = (e3, e2, e1)[j]
-        for y, cur, inc in step.rows(a, g, FH - AH + j, yr - AH - j):
+        for y, cur, inc in step.rows(a, g, FH - AH + j, yr - AH - j, given_rows(yl) if j == 0 else ()):
             for c in range(3):
                 f = seen[c, y]
                 v = cur[c] + inc[c] + jnp.where(at_mon, 2.0 * DT * f, 0.0)
@@ -393,17 +455,22 @@
     beside = (ceil(len(raw), 2) + ceil(len(win), PER) + 1, 8, nz)
 
     layers = over_wl(jnp.transpose(design, (0, 2, 1)))
-    held = call(fetch_body, "fetch", [v.shape for v in flat], [hbm] * 5, [pltpu.SemaphoreType.DMA((5,))])(
-        *[pltpu.with_memory_space_constraint(v, pltpu.HBM) for v in flat])
-    co, prof_t, fa, fb, aa, ab, px, da, db = call(
+    fe, fh, ae, ah, bg = flat
+    h1 = (3, yl, xl, nz)
+    ae, ah, fe, fh, bg, ah1, aa, ab = call(
+        lambda *r: fetch_body(*r, xl=xl, yl=yl), "fetch",
+        [ae.shape] * 4 + [bg.shape, h1, a_side, a_side], [hbm] * 5, [pltpu.SemaphoreType.DMA((5,))],
+    )(*[pltpu.with_memory_space_constraint(v, pltpu.HBM) for v in (ae, ah, fe, fh, bg)])
+    raa, rab = swap(aa, False, 0), swap(ab, False, 1)
+    (fh1,) = call(lambda *r: first_body(*r, xl=xl, yl=yl), "first", [h1], [vmem] * 2)(fe, fh)
+    co, prof_t, fa, fb, px, da, db = call(
         lambda *r: send_body(*r, xl=xl, yl=yl, nw=nw, owned=owned), "send",
-        [(yl, xl, nz), (xl, nz), f_side, f_side, a_side, a_side, beside, corner, corner],
-        [smem] + [vmem] * (6 + nw), [ext(128, 128)],
-    )(monitor_layer, *held, sp, *layers)
+        [(yl, xl, nz), (xl, nz), f_side, f_side, beside, corner, corner],
+        [smem] + [vmem] * (8 + nw), [ext(128, 128)],
+    )(monitor_layer, fe, fh, ae, ah, bg, fh1, ah1, sp, *layers)
     rfa, rfb = swap(fa, False, 0), swap(fb, False, 1)
     rx = swap(px, True, None)
     rda, rdb = swap(da, True, 0), swap(db, True, 1)
-    raa, rab = swap(aa, False, 0), swap(ab, False, 1)
     f32 = np.float32
     omegas = [f32(2.0 * math.pi) / (f32(16.0) + f32(32.0) * f32(i) / f32(nw)) for i in range(nw)]
     signals = [[f32(DT) * np.sin(f32(o * f32((k + 1) * DT))) for k in range(STEPS)] for o in omegas]
@@ -411,11 +478,11 @@
         lambda *r: forward_body(*r, xl=xl, yl=yl, signals=signals), "forward",
         [flat[0].shape, (yr, xr, nz), field, field, field], [smem, smem] + [vmem] * 9,
         [ext(*field), ext(*field), ext(yr, xr, nz)],
-    )(source_layer, monitor_layer, held[0], held[1], co, prof_t, rfa, rfb, rx, rda, rdb)
+    )(source_layer, monitor_layer, fe, fh, co, prof_t, rfa, rfb, rx, rda, rdb)
     out_a, grad = call(
         lambda *r: adjoint_body(*r, xl=xl, yl=yl, omegas=omegas), "adjoint",
         [flat[0].shape, (xl, nz)], [smem] + [vmem] * 11, [ext(*field), ext(*field)],
-    )(monitor_layer, held[2], held[3], cx, e1, e2, e3, raa, rab, rx, rda, rdb)
+    )(monitor_layer, ae, ah, cx, e1, e2, e3, raa, rab, rx, rda, rdb)
     (gradient,) = call(
         lambda *r: sum_body(*r, owned=owned, xl=xl, yl=yl), "gather_sum",
         [(owned, yl, xl)], [vmem] * nw, [ext(128, xl)],

time: 41.8 us -> 35.7 us (0.85)
  waiting for transfers between devices: 9.47 us -> 5.8 us
  starting transfers between devices: 20.7 us -> 18.4 us
    ppermute x7, waiting for transfers between devices: 7.8 us -> 3.77 us  [swap(): return lax.ppermute(block, ('gx', 'gy'), route)]
    ppermute x6, starting transfers between devices: 8.49 us -> 6.32 us  [over_wl(): lax.ppermute(v, 'wl', [(i, i ^ k) for i in range(nw)])]
    pallas_call x1 -> x2, Pallas kernels: 1.42 us -> 1.58 us  [the longest x1 1.43 us: per_device(): call(lambda *r: fetch_body(*r, xl=xl, yl=yl), 'fetch', [ae.shape] * 4 + [...]
  transfers between devices with their start and end apart: 13 -> 13, of which waited for: 5 -> 5; matrix products, arithmetic and copies ran while one was open for 0% -> 0% of each run, Pallas kernels for 11% -> 13%
where the time goes in v3:
time: 35.7 us; the launch traced here: 35.5 us
  starting transfers between devices  18.4 us (52%)
  Pallas kernels  9.24 us (26%)
  waiting for transfers between devices  5.8 us (16%)
  between operations  2.05 us (6%)
    ppermute x7, starting transfers between devices, swap(): return lax.ppermute(block, ('gx', 'gy'), route)  12.1 us
    ppermute x6, starting transfers between devices, over_wl(): lax.ppermute(v, 'wl', [(i, i ^ k) for i in range(nw)])  6.32 us
    ppermute x7, waiting for transfers between devices, swap(): return lax.ppermute(block, ('gx', 'gy'), route)  3.77 us
    pallas_call x1, Pallas kernels, per_device(): call(lambda *r: forward_body(*r, xl=xl, yl=yl, signals=signals), 'forward...  3.16 us
    pallas_call x1, Pallas kernels, per_device(): call(lambda *r: adjoint_body(*r, xl=xl, yl=yl, omegas=omegas), 'adjoint',...  2.45 us
    ppermute x6, waiting for transfers between devices, over_wl(): lax.ppermute(v, 'wl', [(i, i ^ k) for i in range(nw)])  2.03 us
    pallas_call x1, Pallas kernels, per_device(): call(lambda *r: fetch_body(*r, xl=xl, yl=yl), 'fetch', [ae.shape] * 4 + [...  1.43 us
    pallas_call x1, Pallas kernels, per_device(): call(lambda *r: send_body(*r, xl=xl, yl=yl, nw=nw, owned=owned), 'send',...  1.34 us
  transfers between devices with their start and end apart: 13, of which 5 were waited for; matrix products, arithmetic and copies ran while one was open for 0% of the time, Pallas kernels for 13%

profile of v3, /device:TPU:9, one launch (start us, length us, event | category | flops | bytes accessed | tf_op | source)
XLA Modules:
  0.0 35.5 jit_solution(17716497220345502140)
XLA Ops:
  0.6 1.8 %collective-permute-start.2 = (f32[2,8,32]{2,1,0:T(8,128)}, f32[2,8,32]{2,1,0:T(8,128)S(1)}, u32[]{:S(2)}, u32[]{:S(2)}) collective-permute-start(f32[2,8,32]{2,1,0:T(8,128)} %bitcast.12), channel_id=1, source_target_pairs={{0,24},{8,16},{16,8},{24,0},{1,25},{9,17},{17,9},{25,1},{2,26},{10... | collective-permute-start | bytes 6152 | tf_op jit(solution)/shard_map/ppermute | solution.py:449
  2.5 0.3 collective-permute-start.1
  2.7 0.2 collective-permute-start
  3.6 1.4 %fetch.1 = (f32[768,128]{1,0:T(8,128)S(1)}, f32[768,128]{1,0:T(8,128)S(1)}, f32[768,128]{1,0:T(8,128)S(1)}, f32[768,128]{1,0:T(8,128)S(1)}, f32[256,128]{1,0:T(8...) custom-call(f32[768,128]{1,0:T(8,128)} %bitcast.17, ...), custom_call_target="tpu_custom_call" | custom-call | tf_op jit(solution)/shard_map/fetch/pallas_call | solution.py:460
  5.1 0.1 first.1.r_6_
  5.2 0.0 collective-permute-done.2.r_12_
  5.2 0.0 collective-permute-done.1.r_11_
  5.2 0.0 collective-permute-done.r_10_
  5.3 1.3 %send.1 = (f32[8,32,128]{2,1,0:T(8,128)S(1)}, f32[32,128]{1,0:T(8,128)S(1)}, f32[19,32,128]{2,1,0:T(8,128)S(1)}, f32[19,32,128]{2,1,0:T(8,128)S(1)}, f32[60,8,12...) custom-call(s32[1]{0:T(128)S(6)} %copy.13.r_0_.r_1_, ...), custom_call_target="tpu_custom_call" | custom-call | tf_op jit(solution)/shard_map/send/pallas_call | solution.py:466
  6.6 1.2 %collective-permute-start.6 = (f32[21,8,128]{2,1,0:T(8,128)S(1)}, f32[21,8,128]{2,1,0:T(8,128)S(1)}, u32[]{:S(2)}, u32[]{:S(2)}) collective-permute-start(f32[21,8,128]{2,1,0:T(8,128)S(1)} %get-tuple-element.36), channel_id=1, source_target_pairs={{0,5},{1,4},{2,7},{3,6},{4,1},{5,0},{6,3},{7,2},{8,13},{9,12},{10,... | collective-permute-start | bytes 258056 | tf_op jit(solution)/shard_map/ppermute | solution.py:32
  7.8 4.3 %collective-permute-start.7 = (f32[21,8,128]{2,1,0:T(8,128)S(1)}, f32[21,8,128]{2,1,0:T(8,128)S(1)}, u32[]{:S(2)}, u32[]{:S(2)}) collective-permute-start(f32[21,8,128]{2,1,0:T(8,128)S(1)} %get-tuple-element.37), channel_id=1, source_target_pairs={{1,6},{2,5},{5,2},{6,1},{9,14},{10,13},{13,10},{14,9},{17,22},{18,... | collective-permute-start | bytes 258056 | tf_op jit(solution)/shard_map/ppermute | solution.py:32
  12.1 0.1 collective-permute-start.3
  12.1 2.0 %collective-permute-start.4 = (f32[19,32,128]{2,1,0:T(8,128)S(1)}, f32[19,32,128]{2,1,0:T(8,128)S(1)}, u32[]{:S(2)}, u32[]{:S(2)}) collective-permute-start(f32[19,32,128]{2,1,0:T(8,128)S(1)} %get-tuple-element.34), channel_id=1, source_target_pairs={{1,2},{2,1},{5,6},{6,5},{9,10},{10,9},{13,14},{14,13},{17,18},{18,... | collective-permute-start | bytes 933896 | tf_op jit(solution)/shard_map/ppermute | solution.py:32
  14.1 1.2 %collective-permute-start.5 = (f32[60,8,128]{2,1,0:T(8,128)S(1)}, f32[60,8,128]{2,1,0:T(8,128)S(1)}, u32[]{:S(2)}, u32[]{:S(2)}) collective-permute-start(f32[60,8,128]{2,1,0:T(8,128)S(1)} %get-tuple-element.35), channel_id=1, source_target_pairs={{0,4},{1,5},{2,6},{3,7},{4,0},{5,1},{6,2},{7,3},{8,12},{9,13},{10,... | collective-permute-start | bytes 737288 | tf_op jit(solution)/shard_map/ppermute | solution.py:32
  15.4 0.0 collective-permute-done.6.r_9_.r_10_
  15.4 0.2 collective-permute-start.8
  15.6 0.0 collective-permute-done.7.r_10_.r_11_
  15.6 3.2 %collective-permute-start.9 = (f32[14,32,128]{2,1,0:T(8,128)S(1)}, f32[14,32,128]{2,1,0:T(8,128)S(1)}, u32[]{:S(2)}, u32[]{:S(2)}) collective-permute-start(f32[14,32,128]{2,1,0:T(8,128)S(1)} %get-tuple-element.44), channel_id=1, source_target_pairs={{1,2},{2,1},{5,6},{6,5},{9,10},{10,9},{13,14},{14,13},{17,18},{18,... | collective-permute-start | bytes 688136 | tf_op jit(solution)/shard_map/ppermute | solution.py:32
  19.4 0.8 %collective-permute-done.5.r_8_.r_9_ = f32[60,8,128]{2,1,0:T(8,128)S(1)} collective-permute-done((f32[60,8,128]{2,1,0:T(8,128)S(1)}, f32[60,8,128]{2,1,0:T(8,128)S(1)}, u32[]{:S(2)}, u32[]{:S(2)}) %collective-permute-start.5) | collective-permute-done | bytes 245792 | tf_op jit(solution)/shard_map/ppermute | solution.py:32
  20.2 0.0 collective-permute-done.3.r_6_
  20.2 1.2 %collective-permute-done.4.r_7_ = f32[19,32,128]{2,1,0:T(8,128)S(1)} collective-permute-done((f32[19,32,128]{2,1,0:T(8,128)S(1)}, f32[19,32,128]{2,1,0:T(8,128)S(1)}, u32[]{:S(2)}, u32[]{:S(2)}) %collective-permute-start.4) | collective-permute-done | bytes 311328 | tf_op jit(solution)/shard_map/ppermute | solution.py:32
  21.4 3.2 %forward.1 = (f32[768,128]{1,0:T(8,128)}, f32[18,40,128]{2,1,0:T(8,128)S(1)}, f32[3,18,40,128]{3,2,1,0:T(8,128)S(1)}, f32[3,18,40,128]{3,2,1,0:T(8,128)S(1)}, f32[3,18,40,128]{3,2,1,0:T(8,128)S(1)}) custom-call(s32[1]{0:T(128)S(6)} %copy.12.r_0_, s32[1]{0:T(128)S(6)} %copy.13.r_0_.r_1_, f32[768,128]{1,0:T(8,128)S(1)} %get-tuple-element.25.r_0_.r_1_.r_2_, ...), custom_call_target="tpu_custom_call" | custom-call | tf_op jit(solution)/shard_map/forward/pallas_call | solution.py:477
  24.6 0.0 collective-permute-done.8.r_7_
  24.6 1.7 %collective-permute-done.9.r_8_ = f32[14,32,128]{2,1,0:T(8,128)S(1)} collective-permute-done((f32[14,32,128]{2,1,0:T(8,128)S(1)}, f32[14,32,128]{2,1,0:T(8,128)S(1)}, u32[]{:S(2)}, u32[]{:S(2)}) %collective-permute-start.9) | collective-permute-done | bytes 229408 | tf_op jit(solution)/shard_map/ppermute | solution.py:32
  26.3 2.5 %adjoint.1 = (f32[768,128]{1,0:T(8,128)}, f32[32,128]{1,0:T(8,128)S(1)}) custom-call(s32[1]{0:T(128)S(6)} %copy.13.r_0_.r_1_, f32[768,128]{1,0:T(8,128)S(1)} %get-tuple-element.27.r_3_.r_1_, f32[768,128]{1,0:T(8,128)S(1)} %get-tuple-element.28.r_4_.r_2_, f32[18,40,128]{2,1,0:T(8,128)S(1)} %get-tuple-element.39.r_3_, ...), custom_call_target="tpu_custom_call" | custom-call | tf_op jit(solution)/shard_map/adjoint/pallas_call | solution.py:482
  28.8 3.4 %collective-permute-start.12 = (f32[32,128]{1,0:T(8,128)S(1)}, f32[32,128]{1,0:T(8,128)S(1)}, u32[]{:S(2)}, u32[]{:S(2)}) collective-permute-start(f32[32,128]{1,0:T(8,128)S(1)} %get-tuple-element.46.r_0_), channel_id=1, source_target_pairs={{0,24},{8,16},{16,8},{24,0},{1,25},{9,17},{17,9},{25,1},{2,26},{10... | collective-permute-start | bytes 49160 | tf_op jit(solution)/shard_map/ppermute | solution.py:449
  32.2 0.6 %collective-permute-start.11 = (f32[32,128]{1,0:T(8,128)S(1)}, f32[32,128]{1,0:T(8,128)S(1)}, u32[]{:S(2)}, u32[]{:S(2)}) collective-permute-start(f32[32,128]{1,0:T(8,128)S(1)} %get-tuple-element.46.r_0_), channel_id=1, source_target_pairs={{0,16},{8,24},{16,0},{24,8},{1,17},{9,25},{17,1},{25,9},{2,18},{10... | collective-permute-start | bytes 49160 | tf_op jit(solution)/shard_map/ppermute | solution.py:449
  32.8 0.0 collective-permute-start.10
  32.8 0.8 %collective-permute-done.12.r_3_ = f32[32,128]{1,0:T(8,128)S(1)} collective-permute-done((f32[32,128]{1,0:T(8,128)S(1)}, f32[32,128]{1,0:T(8,128)S(1)}, u32[]{:S(2)}, u32[]{:S(2)}) %collective-permute-start.12) | collective-permute-done | bytes 16416 | tf_op jit(solution)/shard_map/ppermute | solution.py:449
  33.6 1.2 %collective-permute-done.11.r_2_ = f32[32,128]{1,0:T(8,128)S(1)} collective-permute-done((f32[32,128]{1,0:T(8,128)S(1)}, f32[32,128]{1,0:T(8,128)S(1)}, u32[]{:S(2)}, u32[]{:S(2)}) %collective-permute-start.11) | collective-permute-done | bytes 16416 | tf_op jit(solution)/shard_map/ppermute | solution.py:449
  34.8 0.0 collective-permute-done.10.r_1_
  34.8 0.7 %gather_sum.1 = f32[2,8,32]{2,1,0:T(8,128)} custom-call(f32[32,128]{1,0:T(8,128)S(1)} %get-tuple-element.46.r_0_, f32[32,128]{1,0:T(8,128)S(1)} %collective-permute-done.10.r_1_, f32[32,128]{1,0:T(8,128)S(1)} %collective-permute-done.11.r_2_, f32[32,128]{1,0:T(8,128)S(1)} %collective-permute-done.12.r_3_), custom_call_target="tpu_custom_call" | custom-call | tf_op jit(solution)/shard_map/gather_sum/pallas_call | solution.py:486
  (4 shorter events, 0.0 us)
Async XLA Ops:
  0.6 4.6 %collective-permute-start.2 = (f32[2,8,32]{2,1,0:T(8,128)}, f32[2,8,32]{2,1,0:T(8,128)S(1)}, u32[]{:S(2)}, u32[]{:S(2)}) collective-permute-start(f32[2,8,32]{2,1,0:T(8,128)} %bitcast.12), channel_id=1, source_target_pairs={{0,24},{8,16},{16,8},{24,0},{1,25},{9,17},{17,9},{25,1},{2,26},{10... | collective-permute-start | bytes 6152 | tf_op jit(solution)/shard_map/ppermute | solution.py:449
  2.5 2.8 %collective-permute-start.1 = (f32[2,8,32]{2,1,0:T(8,128)}, f32[2,8,32]{2,1,0:T(8,128)S(1)}, u32[]{:S(2)}, u32[]{:S(2)}) collective-permute-start(f32[2,8,32]{2,1,0:T(8,128)} %bitcast.13), channel_id=1, source_target_pairs={{0,16},{8,24},{16,0},{24,8},{1,17},{9,25},{17,1},{25,9},{2,18},{10... | collective-permute-start | bytes 6152 | tf_op jit(solution)/shard_map/ppermute | solution.py:449
  2.7 2.5 %collective-permute-start = (f32[2,8,32]{2,1,0:T(8,128)}, f32[2,8,32]{2,1,0:T(8,128)S(1)}, u32[]{:S(2)}, u32[]{:S(2)}) collective-permute-start(f32[2,8,32]{2,1,0:T(8,128)} %bitcast.14), channel_id=1, source_target_pairs={{0,8},{8,0},{16,24},{24,16},{1,9},{9,1},{17,25},{25,17},{2,10},{10... | collective-permute-start | bytes 6152 | tf_op jit(solution)/shard_map/ppermute | solution.py:449
  3.6 1.6 %copy-start = (f32[2,32,8]{1,2,0:T(8,128)S(1)}, f32[2,32,8]{1,2,0:T(8,128)}, u32[]{:S(2)}) copy-start(f32[2,32,8]{1,2,0:T(8,128)} %param.14) | copy-start | bytes 6148
  3.6 1.6 %copy-start.1 = (f32[1,32,8]{1,2,0:T(8,128)S(1)}, f32[1,32,8]{1,2,0:T(8,128)}, u32[]{:S(2)}) copy-start(f32[1,32,8]{1,2,0:T(8,128)} %param.15) | copy-start | bytes 3076
  6.6 8.8 %collective-permute-start.6 = (f32[21,8,128]{2,1,0:T(8,128)S(1)}, f32[21,8,128]{2,1,0:T(8,128)S(1)}, u32[]{:S(2)}, u32[]{:S(2)}) collective-permute-start(f32[21,8,128]{2,1,0:T(8,128)S(1)} %get-tuple-element.36), channel_id=1, source_target_pairs={{0,5},{1,4},{2,7},{3,6},{4,1},{5,0},{6,3},{7,2},{8,13},{9,12},{10,... | collective-permute-start | bytes 258056 | tf_op jit(solution)/shard_map/ppermute | solution.py:32
  7.8 7.8 %collective-permute-start.7 = (f32[21,8,128]{2,1,0:T(8,128)S(1)}, f32[21,8,128]{2,1,0:T(8,128)S(1)}, u32[]{:S(2)}, u32[]{:S(2)}) collective-permute-start(f32[21,8,128]{2,1,0:T(8,128)S(1)} %get-tuple-element.37), channel_id=1, source_target_pairs={{1,6},{2,5},{5,2},{6,1},{9,14},{10,13},{13,10},{14,9},{17,22},{18,... | collective-permute-start | bytes 258056 | tf_op jit(solution)/shard_map/ppermute | solution.py:32
  12.1 8.1 %collective-permute-start.3 = (f32[19,32,128]{2,1,0:T(8,128)S(1)}, f32[19,32,128]{2,1,0:T(8,128)S(1)}, u32[]{:S(2)}, u32[]{:S(2)}) collective-permute-start(f32[19,32,128]{2,1,0:T(8,128)S(1)} %get-tuple-element.33), channel_id=1, source_target_pairs={{0,1},{1,0},{2,3},{3,2},{4,5},{5,4},{6,7},{7,6},{8,9},{9,8},{10,11... | collective-permute-start | bytes 933896 | tf_op jit(solution)/shard_map/ppermute | solution.py:32
  12.1 9.3 %collective-permute-start.4 = (f32[19,32,128]{2,1,0:T(8,128)S(1)}, f32[19,32,128]{2,1,0:T(8,128)S(1)}, u32[]{:S(2)}, u32[]{:S(2)}) collective-permute-start(f32[19,32,128]{2,1,0:T(8,128)S(1)} %get-tuple-element.34), channel_id=1, source_target_pairs={{1,2},{2,1},{5,6},{6,5},{9,10},{10,9},{13,14},{14,13},{17,18},{18,... | collective-permute-start | bytes 933896 | tf_op jit(solution)/shard_map/ppermute | solution.py:32
  14.1 6.0 %collective-permute-start.5 = (f32[60,8,128]{2,1,0:T(8,128)S(1)}, f32[60,8,128]{2,1,0:T(8,128)S(1)}, u32[]{:S(2)}, u32[]{:S(2)}) collective-permute-start(f32[60,8,128]{2,1,0:T(8,128)S(1)} %get-tuple-element.35), channel_id=1, source_target_pairs={{0,4},{1,5},{2,6},{3,7},{4,0},{5,1},{6,2},{7,3},{8,12},{9,13},{10,... | collective-permute-start | bytes 737288 | tf_op jit(solution)/shard_map/ppermute | solution.py:32
  15.4 9.2 %collective-permute-start.8 = (f32[14,32,128]{2,1,0:T(8,128)S(1)}, f32[14,32,128]{2,1,0:T(8,128)S(1)}, u32[]{:S(2)}, u32[]{:S(2)}) collective-permute-start(f32[14,32,128]{2,1,0:T(8,128)S(1)} %get-tuple-element.43), channel_id=1, source_target_pairs={{0,1},{1,0},{2,3},{3,2},{4,5},{5,4},{6,7},{7,6},{8,9},{9,8},{10,11... | collective-permute-start | bytes 688136 | tf_op jit(solution)/shard_map/ppermute | solution.py:32
  15.6 10.7 %collective-permute-start.9 = (f32[14,32,128]{2,1,0:T(8,128)S(1)}, f32[14,32,128]{2,1,0:T(8,128)S(1)}, u32[]{:S(2)}, u32[]{:S(2)}) collective-permute-start(f32[14,32,128]{2,1,0:T(8,128)S(1)} %get-tuple-element.44), channel_id=1, source_target_pairs={{1,2},{2,1},{5,6},{6,5},{9,10},{10,9},{13,14},{14,13},{17,18},{18,... | collective-permute-start | bytes 688136 | tf_op jit(solution)/shard_map/ppermute | solution.py:32
  28.8 4.8 %collective-permute-start.12 = (f32[32,128]{1,0:T(8,128)S(1)}, f32[32,128]{1,0:T(8,128)S(1)}, u32[]{:S(2)}, u32[]{:S(2)}) collective-permute-start(f32[32,128]{1,0:T(8,128)S(1)} %get-tuple-element.46.r_0_), channel_id=1, source_target_pairs={{0,24},{8,16},{16,8},{24,0},{1,25},{9,17},{17,9},{25,1},{2,26},{10... | collective-permute-start | bytes 49160 | tf_op jit(solution)/shard_map/ppermute | solution.py:449
  32.2 2.6 %collective-permute-start.11 = (f32[32,128]{1,0:T(8,128)S(1)}, f32[32,128]{1,0:T(8,128)S(1)}, u32[]{:S(2)}, u32[]{:S(2)}) collective-permute-start(f32[32,128]{1,0:T(8,128)S(1)} %get-tuple-element.46.r_0_), channel_id=1, source_target_pairs={{0,16},{8,24},{16,0},{24,8},{1,17},{9,25},{17,1},{25,9},{2,18},{10... | collective-permute-start | bytes 49160 | tf_op jit(solution)/shard_map/ppermute | solution.py:449
  32.8 2.0 %collective-permute-start.10 = (f32[32,128]{1,0:T(8,128)S(1)}, f32[32,128]{1,0:T(8,128)S(1)}, u32[]{:S(2)}, u32[]{:S(2)}) collective-permute-start(f32[32,128]{1,0:T(8,128)S(1)} %get-tuple-element.46.r_0_), channel_id=1, source_target_pairs={{0,8},{8,0},{16,24},{24,16},{1,9},{9,1},{17,25},{25,17},{2,10},{10... | collective-permute-start | bytes 49160 | tf_op jit(solution)/shard_map/ppermute | solution.py:449

commit v4 on v3

--- a/solution.py
+++ b/solution.py
@@ -325,7 +325,12 @@
             out[pl.ds(c * xl * yl + y, xl, stride=yl), :] = big[c, FH + y, 0:xl, :]
 
 
-def forward_body(src, mon, fe, fh, co, prof_t, ra, rb, rx, rda, rdb, out, cx, e1, e2, e3, e0, h, sx, *, xl, yl, signals):
+def store_body(e3, a, out_f, out_a, *, xl, yl):
+    put_out(e3, out_f, xl, yl)
+    put_out(a, out_a, xl, yl)
+
+
+def forward_body(src, mon, fe, fh, co, prof_t, ra, rb, rx, rda, rdb, cx, e1, e2, e3, e0, h, sx, *, xl, yl, signals):
     xr, yr = xl + 8, yl + 2 * FH
     gy = lax.axis_index("gy")
     src_l = src[0]
@@ -369,10 +374,9 @@
             new[0, y] = cur[0] + inc[0] + signal * sx[y]
             new[1, y] = cur[1] + inc[1]
             new[2, y] = cur[2] + inc[2]
-    put_out(e3, out, xl, yl)
-
-
-def adjoint_body(mon, ae, ah, cx, e1, e2, e3, ra, rb, rx, rda, rdb, out, grad, a, g, *, xl, yl, omegas):
+
+
+def adjoint_body(mon, ae, ah, cx, e1, e2, e3, ra, rb, rx, rda, rdb, a, grad, g, *, xl, yl, omegas):
     yr = yl + 2 * FH
     gy = lax.axis_index("gy")
 
@@ -410,7 +414,6 @@
         moved = pltpu.roll(total[y] * scale, (wide * y - Z0) % 128, 1)
         packed = jnp.where((lane >= wide * y) & (lane < wide * (y + 1)), moved, packed)
     grad[...] = packed
-    put_out(a, out, xl, yl)
 
 
 def sum_body(*refs, owned, xl, yl):
@@ -474,19 +477,22 @@
     f32 = np.float32
     omegas = [f32(2.0 * math.pi) / (f32(16.0) + f32(32.0) * f32(i) / f32(nw)) for i in range(nw)]
     signals = [[f32(DT) * np.sin(f32(o * f32((k + 1) * DT))) for k in range(STEPS)] for o in omegas]
-    out_f, cx, e1, e2, e3 = call(
+    cx, e1, e2, e3 = call(
         lambda *r: forward_body(*r, xl=xl, yl=yl, signals=signals), "forward",
-        [flat[0].shape, (yr, xr, nz), field, field, field], [smem, smem] + [vmem] * 9,
+        [(yr, xr, nz), field, field, field], [smem, smem] + [vmem] * 9,
         [ext(*field), ext(*field), ext(yr, xr, nz)],
     )(source_layer, monitor_layer, fe, fh, co, prof_t, rfa, rfb, rx, rda, rdb)
-    out_a, grad = call(
+    last_a, grad = call(
         lambda *r: adjoint_body(*r, xl=xl, yl=yl, omegas=omegas), "adjoint",
-        [flat[0].shape, (xl, nz)], [smem] + [vmem] * 11, [ext(*field), ext(*field)],
+        [field, (xl, nz)], [smem] + [vmem] * 11, [ext(*field)],
     )(monitor_layer, ae, ah, cx, e1, e2, e3, raa, rab, rx, rda, rdb)
+    terms = over_wl(grad)
+    out_f, out_a = call(
+        lambda *r: store_body(*r, xl=xl, yl=yl), "store", [flat[0].shape] * 2, [vmem] * 2)(e3, last_a)
     (gradient,) = call(
         lambda *r: sum_body(*r, owned=owned, xl=xl, yl=yl), "gather_sum",
         [(owned, yl, xl)], [vmem] * nw, [ext(128, xl)],
-    )(*over_wl(grad))
+    )(*terms)
     block = (1, 3, xl, yl, nz)
     return (out_f.reshape(block), out_a.reshape(block), jnp.transpose(gradient, (0, 2, 1)))
 

time: 35.7 us -> 35.1 us (0.983)
    pallas_call x0 -> x1, Pallas kernels: none -> 1.01 us  [per_device(): call(lambda *r: store_body(*r, xl=xl, yl=yl), 'store', [flat[0].shape] *...]
    ppermute x6, waiting for transfers between devices: 2.03 us -> 1.11 us  [over_wl(): lax.ppermute(v, 'wl', [(i, i ^ k) for i in range(nw)])]
    pallas_call x1, Pallas kernels: 3.16 us -> 2.47 us  [per_device(): call(lambda *r: forward_body(*r, xl=xl, yl=yl, signals=signals), 'forward...]
    ppermute x7, waiting for transfers between devices: 3.77 us -> 4.45 us  [swap(): return lax.ppermute(block, ('gx', 'gy'), route)]
    pallas_call x1, Pallas kernels: 2.45 us -> 1.81 us  [per_device(): call(lambda *r: adjoint_body(*r, xl=xl, yl=yl, omegas=omegas), 'adjoint',...]
  transfers between devices with their start and end apart: 13 -> 13, of which waited for: 5 -> 6; matrix products, arithmetic and copies ran while one was open for 0% -> 0% of each run, Pallas kernels for 13% -> 14%
where the time goes in v4:
time: 35.1 us; the launch traced here: 34.9 us
  starting transfers between devices  18.3 us (52%)
  Pallas kernels  8.91 us (25%)
  waiting for transfers between devices  5.57 us (16%)
  between operations  2.06 us (6%)
    ppermute x7, starting transfers between devices, swap(): return lax.ppermute(block, ('gx', 'gy'), route)  12.1 us
    ppermute x6, starting transfers between devices, over_wl(): lax.ppermute(v, 'wl', [(i, i ^ k) for i in range(nw)])  6.2 us
    ppermute x7, waiting for transfers between devices, swap(): return lax.ppermute(block, ('gx', 'gy'), route)  4.45 us
    pallas_call x1, Pallas kernels, per_device(): call(lambda *r: forward_body(*r, xl=xl, yl=yl, signals=signals), 'forward...  2.47 us
    pallas_call x1, Pallas kernels, per_device(): call(lambda *r: adjoint_body(*r, xl=xl, yl=yl, omegas=omegas), 'adjoint',...  1.81 us
    pallas_call x1, Pallas kernels, per_device(): call(lambda *r: fetch_body(*r, xl=xl, yl=yl), 'fetch', [ae.shape] * 4 + [...  1.43 us
    pallas_call x1, Pallas kernels, per_device(): call(lambda *r: send_body(*r, xl=xl, yl=yl, nw=nw, owned=owned), 'send',...  1.34 us
    ppermute x6, waiting for transfers between devices, over_wl(): lax.ppermute(v, 'wl', [(i, i ^ k) for i in range(nw)])  1.11 us
  transfers between devices with their start and end apart: 13, of which 6 were waited for; matrix products, arithmetic and copies ran while one was open for 0% of the time, Pallas kernels for 14%

profile of v4, /device:TPU:9, one launch (start us, length us, event | category | flops | bytes accessed | tf_op | source)
XLA Modules:
  0.0 34.9 jit_solution(14637518955336704679)
XLA Ops:
  0.6 1.8 %collective-permute-start.2 = (f32[2,8,32]{2,1,0:T(8,128)}, f32[2,8,32]{2,1,0:T(8,128)S(1)}, u32[]{:S(2)}, u32[]{:S(2)}) collective-permute-start(f32[2,8,32]{2,1,0:T(8,128)} %bitcast.12), channel_id=1, source_target_pairs={{0,24},{8,16},{16,8},{24,0},{1,25},{9,17},{17,9},{25,1},{2,26},{10... | collective-permute-start | bytes 6152 | tf_op jit(solution)/shard_map/ppermute | solution.py:452
  2.5 0.3 collective-permute-start.1
  2.7 0.2 collective-permute-start
  3.6 1.4 %fetch.1 = (f32[768,128]{1,0:T(8,128)S(1)}, f32[768,128]{1,0:T(8,128)S(1)}, f32[768,128]{1,0:T(8,128)S(1)}, f32[768,128]{1,0:T(8,128)S(1)}, f32[256,128]{1,0:T(8...) custom-call(f32[768,128]{1,0:T(8,128)} %bitcast.17, ...), custom_call_target="tpu_custom_call" | custom-call | tf_op jit(solution)/shard_map/fetch/pallas_call | solution.py:463
  5.1 0.1 first.1.r_6_
  5.2 0.0 collective-permute-done.2.r_12_
  5.2 0.0 collective-permute-done.1.r_11_
  5.2 0.0 collective-permute-done.r_10_
  5.3 1.3 %send.1 = (f32[8,32,128]{2,1,0:T(8,128)S(1)}, f32[32,128]{1,0:T(8,128)S(1)}, f32[19,32,128]{2,1,0:T(8,128)S(1)}, f32[19,32,128]{2,1,0:T(8,128)S(1)}, f32[60,8,12...) custom-call(s32[1]{0:T(128)S(6)} %copy.13.r_0_.r_1_, ...), custom_call_target="tpu_custom_call" | custom-call | tf_op jit(solution)/shard_map/send/pallas_call | solution.py:469
  6.6 1.2 %collective-permute-start.6 = (f32[21,8,128]{2,1,0:T(8,128)S(1)}, f32[21,8,128]{2,1,0:T(8,128)S(1)}, u32[]{:S(2)}, u32[]{:S(2)}) collective-permute-start(f32[21,8,128]{2,1,0:T(8,128)S(1)} %get-tuple-element.37), channel_id=1, source_target_pairs={{0,5},{1,4},{2,7},{3,6},{4,1},{5,0},{6,3},{7,2},{8,13},{9,12},{10,... | collective-permute-start | bytes 258056 | tf_op jit(solution)/shard_map/ppermute | solution.py:32
  7.8 4.3 %collective-permute-start.7 = (f32[21,8,128]{2,1,0:T(8,128)S(1)}, f32[21,8,128]{2,1,0:T(8,128)S(1)}, u32[]{:S(2)}, u32[]{:S(2)}) collective-permute-start(f32[21,8,128]{2,1,0:T(8,128)S(1)} %get-tuple-element.38), channel_id=1, source_target_pairs={{1,6},{2,5},{5,2},{6,1},{9,14},{10,13},{13,10},{14,9},{17,22},{18,... | collective-permute-start | bytes 258056 | tf_op jit(solution)/shard_map/ppermute | solution.py:32
  12.1 0.1 collective-permute-start.3
  12.1 2.0 %collective-permute-start.4 = (f32[19,32,128]{2,1,0:T(8,128)S(1)}, f32[19,32,128]{2,1,0:T(8,128)S(1)}, u32[]{:S(2)}, u32[]{:S(2)}) collective-permute-start(f32[19,32,128]{2,1,0:T(8,128)S(1)} %get-tuple-element.35), channel_id=1, source_target_pairs={{1,2},{2,1},{5,6},{6,5},{9,10},{10,9},{13,14},{14,13},{17,18},{18,... | collective-permute-start | bytes 933896 | tf_op jit(solution)/shard_map/ppermute | solution.py:32
  14.1 1.2 %collective-permute-start.5 = (f32[60,8,128]{2,1,0:T(8,128)S(1)}, f32[60,8,128]{2,1,0:T(8,128)S(1)}, u32[]{:S(2)}, u32[]{:S(2)}) collective-permute-start(f32[60,8,128]{2,1,0:T(8,128)S(1)} %get-tuple-element.36), channel_id=1, source_target_pairs={{0,4},{1,5},{2,6},{3,7},{4,0},{5,1},{6,2},{7,3},{8,12},{9,13},{10,... | collective-permute-start | bytes 737288 | tf_op jit(solution)/shard_map/ppermute | solution.py:32
  15.4 0.0 collective-permute-done.6.r_9_.r_10_
  15.4 0.2 collective-permute-start.8
  15.6 0.0 collective-permute-done.7.r_10_.r_11_
  15.6 3.2 %collective-permute-start.9 = (f32[14,32,128]{2,1,0:T(8,128)S(1)}, f32[14,32,128]{2,1,0:T(8,128)S(1)}, u32[]{:S(2)}, u32[]{:S(2)}) collective-permute-start(f32[14,32,128]{2,1,0:T(8,128)S(1)} %get-tuple-element.44), channel_id=1, source_target_pairs={{1,2},{2,1},{5,6},{6,5},{9,10},{10,9},{13,14},{14,13},{17,18},{18,... | collective-permute-start | bytes 688136 | tf_op jit(solution)/shard_map/ppermute | solution.py:32
  19.4 0.8 %collective-permute-done.5.r_8_.r_9_ = f32[60,8,128]{2,1,0:T(8,128)S(1)} collective-permute-done((f32[60,8,128]{2,1,0:T(8,128)S(1)}, f32[60,8,128]{2,1,0:T(8,128)S(1)}, u32[]{:S(2)}, u32[]{:S(2)}) %collective-permute-start.5) | collective-permute-done | bytes 245792 | tf_op jit(solution)/shard_map/ppermute | solution.py:32
  20.2 0.0 collective-permute-done.3.r_6_
  20.2 1.2 %collective-permute-done.4.r_7_ = f32[19,32,128]{2,1,0:T(8,128)S(1)} collective-permute-done((f32[19,32,128]{2,1,0:T(8,128)S(1)}, f32[19,32,128]{2,1,0:T(8,128)S(1)}, u32[]{:S(2)}, u32[]{:S(2)}) %collective-permute-start.4) | collective-permute-done | bytes 311328 | tf_op jit(solution)/shard_map/ppermute | solution.py:32
  21.4 2.5 %forward.1 = (f32[18,40,128]{2,1,0:T(8,128)S(1)}, f32[3,18,40,128]{3,2,1,0:T(8,128)S(1)}, f32[3,18,40,128]{3,2,1,0:T(8,128)S(1)}, f32[3,18,40,128]{3,2,1,0:T(8,128)S(1)}) custom-call(s32[1]{0:T(128)S(6)} %copy.12.r_0_, s32[1]{0:T(128)S(6)} %copy.13.r_0_.r_1_, f32[768,128]{1,0:T(8,128)S(1)} %get-tuple-element.26.r_0_.r_1_.r_2_, ...), custom_call_target="tpu_custom_call" | custom-call | tf_op jit(solution)/shard_map/forward/pallas_call | solution.py:480
  23.9 0.5 %collective-permute-done.8.r_7_ = f32[14,32,128]{2,1,0:T(8,128)S(1)} collective-permute-done((f32[14,32,128]{2,1,0:T(8,128)S(1)}, f32[14,32,128]{2,1,0:T(8,128)S(1)}, u32[]{:S(2)}, u32[]{:S(2)}) %collective-permute-start.8) | collective-permute-done | bytes 229408 | tf_op jit(solution)/shard_map/ppermute | solution.py:32
  24.4 1.9 %collective-permute-done.9.r_8_ = f32[14,32,128]{2,1,0:T(8,128)S(1)} collective-permute-done((f32[14,32,128]{2,1,0:T(8,128)S(1)}, f32[14,32,128]{2,1,0:T(8,128)S(1)}, u32[]{:S(2)}, u32[]{:S(2)}) %collective-permute-start.9) | collective-permute-done | bytes 229408 | tf_op jit(solution)/shard_map/ppermute | solution.py:32
  26.3 1.8 %adjoint.1 = (f32[3,18,40,128]{3,2,1,0:T(8,128)S(1)}, f32[32,128]{1,0:T(8,128)S(1)}) custom-call(s32[1]{0:T(128)S(6)} %copy.13.r_0_.r_1_, f32[768,128]{1,0:T(8,128)S(1)} %get-tuple-element.28.r_3_.r_1_, f32[768,128]{1,0:T(8,128)S(1)} %get-tuple-element.29.r_4_.r_2_, f32[18,40,128]{2,1,0:T(8,128)S(1)} %get-tuple-element.40.r_3_, ...), custom_call_target="tpu_custom_call" | custom-call | tf_op jit(solution)/shard_map/adjoint/pallas_call | solution.py:485
  28.1 3.4 %collective-permute-start.12 = (f32[32,128]{1,0:T(8,128)S(1)}, f32[32,128]{1,0:T(8,128)S(1)}, u32[]{:S(2)}, u32[]{:S(2)}) collective-permute-start(f32[32,128]{1,0:T(8,128)S(1)} %get-tuple-element.48.r_0_), channel_id=1, source_target_pairs={{0,24},{8,16},{16,8},{24,0},{1,25},{9,17},{17,9},{25,1},{2,26},{10... | collective-permute-start | bytes 49160 | tf_op jit(solution)/shard_map/ppermute | solution.py:452
  31.6 0.4 %collective-permute-start.11 = (f32[32,128]{1,0:T(8,128)S(1)}, f32[32,128]{1,0:T(8,128)S(1)}, u32[]{:S(2)}, u32[]{:S(2)}) collective-permute-start(f32[32,128]{1,0:T(8,128)S(1)} %get-tuple-element.48.r_0_), channel_id=1, source_target_pairs={{0,16},{8,24},{16,0},{24,8},{1,17},{9,25},{17,1},{25,9},{2,18},{10... | collective-permute-start | bytes 49160 | tf_op jit(solution)/shard_map/ppermute | solution.py:452
  31.9 0.1 collective-permute-start.10
  32.0 1.0 %store.1 = (f32[768,128]{1,0:T(8,128)}, f32[768,128]{1,0:T(8,128)}) custom-call(f32[3,18,40,128]{3,2,1,0:T(8,128)S(1)} %get-tuple-element.39.r_6_.r_0_, f32[3,18,40,128]{3,2,1,0:T(8,128)S(1)} %get-tuple-element.45.r_1_), custom_call_target="tpu_custom_call" | custom-call | tf_op jit(solution)/shard_map/store/pallas_call | solution.py:490
  33.0 0.3 collective-permute-done.12.r_3_
  33.4 0.8 %collective-permute-done.11.r_2_ = f32[32,128]{1,0:T(8,128)S(1)} collective-permute-done((f32[32,128]{1,0:T(8,128)S(1)}, f32[32,128]{1,0:T(8,128)S(1)}, u32[]{:S(2)}, u32[]{:S(2)}) %collective-permute-start.11) | collective-permute-done | bytes 16416 | tf_op jit(solution)/shard_map/ppermute | solution.py:452
  34.1 0.7 %gather_sum.1 = f32[2,8,32]{2,1,0:T(8,128)} custom-call(f32[32,128]{1,0:T(8,128)S(1)} %get-tuple-element.48.r_0_, f32[32,128]{1,0:T(8,128)S(1)} %collective-permute-done.10.r_1_, f32[32,128]{1,0:T(8,128)S(1)} %collective-permute-done.11.r_2_, f32[32,128]{1,0:T(8,128)S(1)} %collective-permute-done.12.r_3_), custom_call_target="tpu_custom_call" | custom-call | tf_op jit(solution)/shard_map/gather_sum/pallas_call | solution.py:492
  (5 shorter events, 0.0 us)
Async XLA Ops:
  0.6 4.6 %collective-permute-start.2 = (f32[2,8,32]{2,1,0:T(8,128)}, f32[2,8,32]{2,1,0:T(8,128)S(1)}, u32[]{:S(2)}, u32[]{:S(2)}) collective-permute-start(f32[2,8,32]{2,1,0:T(8,128)} %bitcast.12), channel_id=1, source_target_pairs={{0,24},{8,16},{16,8},{24,0},{1,25},{9,17},{17,9},{25,1},{2,26},{10... | collective-permute-start | bytes 6152 | tf_op jit(solution)/shard_map/ppermute | solution.py:452
  2.5 2.8 %collective-permute-start.1 = (f32[2,8,32]{2,1,0:T(8,128)}, f32[2,8,32]{2,1,0:T(8,128)S(1)}, u32[]{:S(2)}, u32[]{:S(2)}) collective-permute-start(f32[2,8,32]{2,1,0:T(8,128)} %bitcast.13), channel_id=1, source_target_pairs={{0,16},{8,24},{16,0},{24,8},{1,17},{9,25},{17,1},{25,9},{2,18},{10... | collective-permute-start | bytes 6152 | tf_op jit(solution)/shard_map/ppermute | solution.py:452
  2.7 2.5 %collective-permute-start = (f32[2,8,32]{2,1,0:T(8,128)}, f32[2,8,32]{2,1,0:T(8,128)S(1)}, u32[]{:S(2)}, u32[]{:S(2)}) collective-permute-start(f32[2,8,32]{2,1,0:T(8,128)} %bitcast.14), channel_id=1, source_target_pairs={{0,8},{8,0},{16,24},{24,16},{1,9},{9,1},{17,25},{25,17},{2,10},{10... | collective-permute-start | bytes 6152 | tf_op jit(solution)/shard_map/ppermute | solution.py:452
  3.6 1.6 %copy-start = (f32[2,32,8]{1,2,0:T(8,128)S(1)}, f32[2,32,8]{1,2,0:T(8,128)}, u32[]{:S(2)}) copy-start(f32[2,32,8]{1,2,0:T(8,128)} %param.14) | copy-start | bytes 6148
  3.6 1.6 %copy-start.1 = (f32[1,32,8]{1,2,0:T(8,128)S(1)}, f32[1,32,8]{1,2,0:T(8,128)}, u32[]{:S(2)}) copy-start(f32[1,32,8]{1,2,0:T(8,128)} %param.15) | copy-start | bytes 3076
  6.6 8.8 %collective-permute-start.6 = (f32[21,8,128]{2,1,0:T(8,128)S(1)}, f32[21,8,128]{2,1,0:T(8,128)S(1)}, u32[]{:S(2)}, u32[]{:S(2)}) collective-permute-start(f32[21,8,128]{2,1,0:T(8,128)S(1)} %get-tuple-element.37), channel_id=1, source_target_pairs={{0,5},{1,4},{2,7},{3,6},{4,1},{5,0},{6,3},{7,2},{8,13},{9,12},{10,... | collective-permute-start | bytes 258056 | tf_op jit(solution)/shard_map/ppermute | solution.py:32
  7.8 7.8 %collective-permute-start.7 = (f32[21,8,128]{2,1,0:T(8,128)S(1)}, f32[21,8,128]{2,1,0:T(8,128)S(1)}, u32[]{:S(2)}, u32[]{:S(2)}) collective-permute-start(f32[21,8,128]{2,1,0:T(8,128)S(1)} %get-tuple-element.38), channel_id=1, source_target_pairs={{1,6},{2,5},{5,2},{6,1},{9,14},{10,13},{13,10},{14,9},{17,22},{18,... | collective-permute-start | bytes 258056 | tf_op jit(solution)/shard_map/ppermute | solution.py:32
  12.1 8.1 %collective-permute-start.3 = (f32[19,32,128]{2,1,0:T(8,128)S(1)}, f32[19,32,128]{2,1,0:T(8,128)S(1)}, u32[]{:S(2)}, u32[]{:S(2)}) collective-permute-start(f32[19,32,128]{2,1,0:T(8,128)S(1)} %get-tuple-element.34), channel_id=1, source_target_pairs={{0,1},{1,0},{2,3},{3,2},{4,5},{5,4},{6,7},{7,6},{8,9},{9,8},{10,11... | collective-permute-start | bytes 933896 | tf_op jit(solution)/shard_map/ppermute | solution.py:32
  12.1 9.3 %collective-permute-start.4 = (f32[19,32,128]{2,1,0:T(8,128)S(1)}, f32[19,32,128]{2,1,0:T(8,128)S(1)}, u32[]{:S(2)}, u32[]{:S(2)}) collective-permute-start(f32[19,32,128]{2,1,0:T(8,128)S(1)} %get-tuple-element.35), channel_id=1, source_target_pairs={{1,2},{2,1},{5,6},{6,5},{9,10},{10,9},{13,14},{14,13},{17,18},{18,... | collective-permute-start | bytes 933896 | tf_op jit(solution)/shard_map/ppermute | solution.py:32
  14.1 6.0 %collective-permute-start.5 = (f32[60,8,128]{2,1,0:T(8,128)S(1)}, f32[60,8,128]{2,1,0:T(8,128)S(1)}, u32[]{:S(2)}, u32[]{:S(2)}) collective-permute-start(f32[60,8,128]{2,1,0:T(8,128)S(1)} %get-tuple-element.36), channel_id=1, source_target_pairs={{0,4},{1,5},{2,6},{3,7},{4,0},{5,1},{6,2},{7,3},{8,12},{9,13},{10,... | collective-permute-start | bytes 737288 | tf_op jit(solution)/shard_map/ppermute | solution.py:32
  15.4 9.0 %collective-permute-start.8 = (f32[14,32,128]{2,1,0:T(8,128)S(1)}, f32[14,32,128]{2,1,0:T(8,128)S(1)}, u32[]{:S(2)}, u32[]{:S(2)}) collective-permute-start(f32[14,32,128]{2,1,0:T(8,128)S(1)} %get-tuple-element.43), channel_id=1, source_target_pairs={{0,1},{1,0},{2,3},{3,2},{4,5},{5,4},{6,7},{7,6},{8,9},{9,8},{10,11... | collective-permute-start | bytes 688136 | tf_op jit(solution)/shard_map/ppermute | solution.py:32
  15.6 10.7 %collective-permute-start.9 = (f32[14,32,128]{2,1,0:T(8,128)S(1)}, f32[14,32,128]{2,1,0:T(8,128)S(1)}, u32[]{:S(2)}, u32[]{:S(2)}) collective-permute-start(f32[14,32,128]{2,1,0:T(8,128)S(1)} %get-tuple-element.44), channel_id=1, source_target_pairs={{1,2},{2,1},{5,6},{6,5},{9,10},{10,9},{13,14},{14,13},{17,18},{18,... | collective-permute-start | bytes 688136 | tf_op jit(solution)/shard_map/ppermute | solution.py:32
  28.1 5.2 %collective-permute-start.12 = (f32[32,128]{1,0:T(8,128)S(1)}, f32[32,128]{1,0:T(8,128)S(1)}, u32[]{:S(2)}, u32[]{:S(2)}) collective-permute-start(f32[32,128]{1,0:T(8,128)S(1)} %get-tuple-element.48.r_0_), channel_id=1, source_target_pairs={{0,24},{8,16},{16,8},{24,0},{1,25},{9,17},{17,9},{25,1},{2,26},{10... | collective-permute-start | bytes 49160 | tf_op jit(solution)/shard_map/ppermute | solution.py:452
  31.6 2.6 %collective-permute-start.11 = (f32[32,128]{1,0:T(8,128)S(1)}, f32[32,128]{1,0:T(8,128)S(1)}, u32[]{:S(2)}, u32[]{:S(2)}) collective-permute-start(f32[32,128]{1,0:T(8,128)S(1)} %get-tuple-element.48.r_0_), channel_id=1, source_target_pairs={{0,16},{8,24},{16,0},{24,8},{1,17},{9,25},{17,1},{25,9},{2,18},{10... | collective-permute-start | bytes 49160 | tf_op jit(solution)/shard_map/ppermute | solution.py:452
  31.9 2.2 %collective-permute-start.10 = (f32[32,128]{1,0:T(8,128)S(1)}, f32[32,128]{1,0:T(8,128)S(1)}, u32[]{:S(2)}, u32[]{:S(2)}) collective-permute-start(f32[32,128]{1,0:T(8,128)S(1)} %get-tuple-element.48.r_0_), channel_id=1, source_target_pairs={{0,8},{8,0},{16,24},{24,16},{1,9},{9,1},{17,25},{25,17},{2,10},{10... | collective-permute-start | bytes 49160 | tf_op jit(solution)/shard_map/ppermute | solution.py:452

commit v5 on v4

--- a/solution.py
+++ b/solution.py
@@ -15,7 +15,7 @@
 BF16 = jnp.bfloat16
 FH = 5
 AH = 3
-WIN = 16
+WIN = 8
 PER = 128 // WIN
 PROF = 112
 

time: 35.1 us -> 34.7 us (0.989)
  waiting for transfers between devices: 5.57 us -> 5.17 us
    ppermute x7, waiting for transfers between devices: 4.45 us -> 4.06 us  [swap(): return lax.ppermute(block, ('gx', 'gy'), route)]
  transfers between devices with their start and end apart: 13 -> 13, of which waited for: 6 -> 6; matrix products, arithmetic and copies ran while one was open for 0% -> 0% of each run, Pallas kernels for 14% -> 15%
where the time goes in v5:
time: 34.7 us; the launch traced here: 34.5 us
  starting transfers between devices  18.3 us (53%)
  Pallas kernels  9 us (26%)
  waiting for transfers between devices  5.17 us (15%)
  between operations  2.06 us (6%)
    ppermute x7, starting transfers between devices, swap(): return lax.ppermute(block, ('gx', 'gy'), route)  12.1 us
    ppermute x6, starting transfers between devices, over_wl(): lax.ppermute(v, 'wl', [(i, i ^ k) for i in range(nw)])  6.2 us
    ppermute x7, waiting for transfers between devices, swap(): return lax.ppermute(block, ('gx', 'gy'), route)  4.06 us
    pallas_call x1, Pallas kernels, per_device(): call(lambda *r: forward_body(*r, xl=xl, yl=yl, signals=signals), 'forward...  2.52 us
    pallas_call x1, Pallas kernels, per_device(): call(lambda *r: adjoint_body(*r, xl=xl, yl=yl, omegas=omegas), 'adjoint',...  1.85 us
    pallas_call x1, Pallas kernels, per_device(): call(lambda *r: fetch_body(*r, xl=xl, yl=yl), 'fetch', [ae.shape] * 4 + [...  1.43 us
    pallas_call x1, Pallas kernels, per_device(): call(lambda *r: send_body(*r, xl=xl, yl=yl, nw=nw, owned=owned), 'send',...  1.34 us
    ppermute x6, waiting for transfers between devices, over_wl(): lax.ppermute(v, 'wl', [(i, i ^ k) for i in range(nw)])  1.11 us
  transfers between devices with their start and end apart: 13, of which 6 were waited for; matrix products, arithmetic and copies ran while one was open for 0% of the time, Pallas kernels for 15%

profile of v5, /device:TPU:9, one launch (start us, length us, event | category | flops | bytes accessed | tf_op | source)
XLA Modules:
  0.0 34.5 jit_solution(14406088607180760077)
XLA Ops:
  0.6 1.8 %collective-permute-start.2 = (f32[2,8,32]{2,1,0:T(8,128)}, f32[2,8,32]{2,1,0:T(8,128)S(1)}, u32[]{:S(2)}, u32[]{:S(2)}) collective-permute-start(f32[2,8,32]{2,1,0:T(8,128)} %bitcast.12), channel_id=1, source_target_pairs={{0,24},{8,16},{16,8},{24,0},{1,25},{9,17},{17,9},{25,1},{2,26},{10... | collective-permute-start | bytes 6152 | tf_op jit(solution)/shard_map/ppermute | solution.py:452
  2.5 0.3 collective-permute-start.1
  2.7 0.2 collective-permute-start
  3.6 1.4 %fetch.1 = (f32[768,128]{1,0:T(8,128)S(1)}, f32[768,128]{1,0:T(8,128)S(1)}, f32[768,128]{1,0:T(8,128)S(1)}, f32[768,128]{1,0:T(8,128)S(1)}, f32[256,128]{1,0:T(8...) custom-call(f32[768,128]{1,0:T(8,128)} %bitcast.17, ...), custom_call_target="tpu_custom_call" | custom-call | tf_op jit(solution)/shard_map/fetch/pallas_call | solution.py:463
  5.1 0.1 first.1.r_6_
  5.2 0.0 collective-permute-done.2.r_12_
  5.2 0.0 collective-permute-done.1.r_11_
  5.2 0.0 collective-permute-done.r_10_
  5.3 1.3 %send.1 = (f32[8,32,128]{2,1,0:T(8,128)S(1)}, f32[32,128]{1,0:T(8,128)S(1)}, f32[18,32,128]{2,1,0:T(8,128)S(1)}, f32[18,32,128]{2,1,0:T(8,128)S(1)}, f32[57,8,12...) custom-call(s32[1]{0:T(128)S(6)} %copy.13.r_0_.r_1_, ...), custom_call_target="tpu_custom_call" | custom-call | tf_op jit(solution)/shard_map/send/pallas_call | solution.py:469
  6.6 1.2 %collective-permute-start.6 = (f32[19,8,128]{2,1,0:T(8,128)S(1)}, f32[19,8,128]{2,1,0:T(8,128)S(1)}, u32[]{:S(2)}, u32[]{:S(2)}) collective-permute-start(f32[19,8,128]{2,1,0:T(8,128)S(1)} %get-tuple-element.37), channel_id=1, source_target_pairs={{0,5},{1,4},{2,7},{3,6},{4,1},{5,0},{6,3},{7,2},{8,13},{9,12},{10,... | collective-permute-start | bytes 233480 | tf_op jit(solution)/shard_map/ppermute | solution.py:32
  7.8 4.3 %collective-permute-start.7 = (f32[19,8,128]{2,1,0:T(8,128)S(1)}, f32[19,8,128]{2,1,0:T(8,128)S(1)}, u32[]{:S(2)}, u32[]{:S(2)}) collective-permute-start(f32[19,8,128]{2,1,0:T(8,128)S(1)} %get-tuple-element.38), channel_id=1, source_target_pairs={{1,6},{2,5},{5,2},{6,1},{9,14},{10,13},{13,10},{14,9},{17,22},{18,... | collective-permute-start | bytes 233480 | tf_op jit(solution)/shard_map/ppermute | solution.py:32
  12.1 0.1 collective-permute-start.3
  12.1 2.0 %collective-permute-start.4 = (f32[18,32,128]{2,1,0:T(8,128)S(1)}, f32[18,32,128]{2,1,0:T(8,128)S(1)}, u32[]{:S(2)}, u32[]{:S(2)}) collective-permute-start(f32[18,32,128]{2,1,0:T(8,128)S(1)} %get-tuple-element.35), channel_id=1, source_target_pairs={{1,2},{2,1},{5,6},{6,5},{9,10},{10,9},{13,14},{14,13},{17,18},{18,... | collective-permute-start | bytes 884744 | tf_op jit(solution)/shard_map/ppermute | solution.py:32
  14.1 1.2 %collective-permute-start.5 = (f32[57,8,128]{2,1,0:T(8,128)S(1)}, f32[57,8,128]{2,1,0:T(8,128)S(1)}, u32[]{:S(2)}, u32[]{:S(2)}) collective-permute-start(f32[57,8,128]{2,1,0:T(8,128)S(1)} %get-tuple-element.36), channel_id=1, source_target_pairs={{0,4},{1,5},{2,6},{3,7},{4,0},{5,1},{6,2},{7,3},{8,12},{9,13},{10,... | collective-permute-start | bytes 700424 | tf_op jit(solution)/shard_map/ppermute | solution.py:32
  15.4 0.0 collective-permute-done.6.r_9_.r_10_
  15.4 0.2 collective-permute-start.8
  15.6 0.0 collective-permute-done.7.r_10_.r_11_
  15.6 3.2 %collective-permute-start.9 = (f32[14,32,128]{2,1,0:T(8,128)S(1)}, f32[14,32,128]{2,1,0:T(8,128)S(1)}, u32[]{:S(2)}, u32[]{:S(2)}) collective-permute-start(f32[14,32,128]{2,1,0:T(8,128)S(1)} %get-tuple-element.44), channel_id=1, source_target_pairs={{1,2},{2,1},{5,6},{6,5},{9,10},{10,9},{13,14},{14,13},{17,18},{18,... | collective-permute-start | bytes 688136 | tf_op jit(solution)/shard_map/ppermute | solution.py:32
  19.4 0.5 %collective-permute-done.5.r_8_.r_9_ = f32[57,8,128]{2,1,0:T(8,128)S(1)} collective-permute-done((f32[57,8,128]{2,1,0:T(8,128)S(1)}, f32[57,8,128]{2,1,0:T(8,128)S(1)}, u32[]{:S(2)}, u32[]{:S(2)}) %collective-permute-start.5) | collective-permute-done | bytes 233504 | tf_op jit(solution)/shard_map/ppermute | solution.py:32
  19.9 0.0 collective-permute-done.3.r_6_
  19.9 1.2 %collective-permute-done.4.r_7_ = f32[18,32,128]{2,1,0:T(8,128)S(1)} collective-permute-done((f32[18,32,128]{2,1,0:T(8,128)S(1)}, f32[18,32,128]{2,1,0:T(8,128)S(1)}, u32[]{:S(2)}, u32[]{:S(2)}) %collective-permute-start.4) | collective-permute-done | bytes 294944 | tf_op jit(solution)/shard_map/ppermute | solution.py:32
  21.1 2.5 %forward.1 = (f32[18,40,128]{2,1,0:T(8,128)S(1)}, f32[3,18,40,128]{3,2,1,0:T(8,128)S(1)}, f32[3,18,40,128]{3,2,1,0:T(8,128)S(1)}, f32[3,18,40,128]{3,2,1,0:T(8,128)S(1)}) custom-call(s32[1]{0:T(128)S(6)} %copy.12.r_0_, s32[1]{0:T(128)S(6)} %copy.13.r_0_.r_1_, f32[768,128]{1,0:T(8,128)S(1)} %get-tuple-element.26.r_0_.r_1_.r_2_, ...), custom_call_target="tpu_custom_call" | custom-call | tf_op jit(solution)/shard_map/forward/pallas_call | solution.py:480
  23.6 0.5 %collective-permute-done.8.r_7_ = f32[14,32,128]{2,1,0:T(8,128)S(1)} collective-permute-done((f32[14,32,128]{2,1,0:T(8,128)S(1)}, f32[14,32,128]{2,1,0:T(8,128)S(1)}, u32[]{:S(2)}, u32[]{:S(2)}) %collective-permute-start.8) | collective-permute-done | bytes 229408 | tf_op jit(solution)/shard_map/ppermute | solution.py:32
  24.1 1.9 %collective-permute-done.9.r_8_ = f32[14,32,128]{2,1,0:T(8,128)S(1)} collective-permute-done((f32[14,32,128]{2,1,0:T(8,128)S(1)}, f32[14,32,128]{2,1,0:T(8,128)S(1)}, u32[]{:S(2)}, u32[]{:S(2)}) %collective-permute-start.9) | collective-permute-done | bytes 229408 | tf_op jit(solution)/shard_map/ppermute | solution.py:32
  26.0 1.8 %adjoint.1 = (f32[3,18,40,128]{3,2,1,0:T(8,128)S(1)}, f32[32,128]{1,0:T(8,128)S(1)}) custom-call(s32[1]{0:T(128)S(6)} %copy.13.r_0_.r_1_, f32[768,128]{1,0:T(8,128)S(1)} %get-tuple-element.28.r_3_.r_1_, f32[768,128]{1,0:T(8,128)S(1)} %get-tuple-element.29.r_4_.r_2_, f32[18,40,128]{2,1,0:T(8,128)S(1)} %get-tuple-element.40.r_3_, ...), custom_call_target="tpu_custom_call" | custom-call | tf_op jit(solution)/shard_map/adjoint/pallas_call | solution.py:485
  27.8 3.4 %collective-permute-start.12 = (f32[32,128]{1,0:T(8,128)S(1)}, f32[32,128]{1,0:T(8,128)S(1)}, u32[]{:S(2)}, u32[]{:S(2)}) collective-permute-start(f32[32,128]{1,0:T(8,128)S(1)} %get-tuple-element.48.r_0_), channel_id=1, source_target_pairs={{0,24},{8,16},{16,8},{24,0},{1,25},{9,17},{17,9},{25,1},{2,26},{10... | collective-permute-start | bytes 49160 | tf_op jit(solution)/shard_map/ppermute | solution.py:452
  31.2 0.4 %collective-permute-start.11 = (f32[32,128]{1,0:T(8,128)S(1)}, f32[32,128]{1,0:T(8,128)S(1)}, u32[]{:S(2)}, u32[]{:S(2)}) collective-permute-start(f32[32,128]{1,0:T(8,128)S(1)} %get-tuple-element.48.r_0_), channel_id=1, source_target_pairs={{0,16},{8,24},{16,0},{24,8},{1,17},{9,25},{17,1},{25,9},{2,18},{10... | collective-permute-start | bytes 49160 | tf_op jit(solution)/shard_map/ppermute | solution.py:452
  31.6 0.1 collective-permute-start.10
  31.7 1.0 %store.1 = (f32[768,128]{1,0:T(8,128)}, f32[768,128]{1,0:T(8,128)}) custom-call(f32[3,18,40,128]{3,2,1,0:T(8,128)S(1)} %get-tuple-element.39.r_6_.r_0_, f32[3,18,40,128]{3,2,1,0:T(8,128)S(1)} %get-tuple-element.45.r_1_), custom_call_target="tpu_custom_call" | custom-call | tf_op jit(solution)/shard_map/store/pallas_call | solution.py:490
  32.7 0.3 %collective-permute-done.12.r_3_ = f32[32,128]{1,0:T(8,128)S(1)} collective-permute-done((f32[32,128]{1,0:T(8,128)S(1)}, f32[32,128]{1,0:T(8,128)S(1)}, u32[]{:S(2)}, u32[]{:S(2)}) %collective-permute-start.12) | collective-permute-done | bytes 16416 | tf_op jit(solution)/shard_map/ppermute | solution.py:452
  33.1 0.8 %collective-permute-done.11.r_2_ = f32[32,128]{1,0:T(8,128)S(1)} collective-permute-done((f32[32,128]{1,0:T(8,128)S(1)}, f32[32,128]{1,0:T(8,128)S(1)}, u32[]{:S(2)}, u32[]{:S(2)}) %collective-permute-start.11) | collective-permute-done | bytes 16416 | tf_op jit(solution)/shard_map/ppermute | solution.py:452
  33.8 0.7 %gather_sum.1 = f32[2,8,32]{2,1,0:T(8,128)} custom-call(f32[32,128]{1,0:T(8,128)S(1)} %get-tuple-element.48.r_0_, f32[32,128]{1,0:T(8,128)S(1)} %collective-permute-done.10.r_1_, f32[32,128]{1,0:T(8,128)S(1)} %collective-permute-done.11.r_2_, f32[32,128]{1,0:T(8,128)S(1)} %collective-permute-done.12.r_3_), custom_call_target="tpu_custom_call" | custom-call | tf_op jit(solution)/shard_map/gather_sum/pallas_call | solution.py:492
  (5 shorter events, 0.0 us)
Async XLA Ops:
  0.6 4.6 %collective-permute-start.2 = (f32[2,8,32]{2,1,0:T(8,128)}, f32[2,8,32]{2,1,0:T(8,128)S(1)}, u32[]{:S(2)}, u32[]{:S(2)}) collective-permute-start(f32[2,8,32]{2,1,0:T(8,128)} %bitcast.12), channel_id=1, source_target_pairs={{0,24},{8,16},{16,8},{24,0},{1,25},{9,17},{17,9},{25,1},{2,26},{10... | collective-permute-start | bytes 6152 | tf_op jit(solution)/shard_map/ppermute | solution.py:452
  2.5 2.8 %collective-permute-start.1 = (f32[2,8,32]{2,1,0:T(8,128)}, f32[2,8,32]{2,1,0:T(8,128)S(1)}, u32[]{:S(2)}, u32[]{:S(2)}) collective-permute-start(f32[2,8,32]{2,1,0:T(8,128)} %bitcast.13), channel_id=1, source_target_pairs={{0,16},{8,24},{16,0},{24,8},{1,17},{9,25},{17,1},{25,9},{2,18},{10... | collective-permute-start | bytes 6152 | tf_op jit(solution)/shard_map/ppermute | solution.py:452
  2.7 2.5 %collective-permute-start = (f32[2,8,32]{2,1,0:T(8,128)}, f32[2,8,32]{2,1,0:T(8,128)S(1)}, u32[]{:S(2)}, u32[]{:S(2)}) collective-permute-start(f32[2,8,32]{2,1,0:T(8,128)} %bitcast.14), channel_id=1, source_target_pairs={{0,8},{8,0},{16,24},{24,16},{1,9},{9,1},{17,25},{25,17},{2,10},{10... | collective-permute-start | bytes 6152 | tf_op jit(solution)/shard_map/ppermute | solution.py:452
  3.6 1.6 %copy-start = (f32[2,32,8]{1,2,0:T(8,128)S(1)}, f32[2,32,8]{1,2,0:T(8,128)}, u32[]{:S(2)}) copy-start(f32[2,32,8]{1,2,0:T(8,128)} %param.14) | copy-start | bytes 6148
  3.6 1.6 %copy-start.1 = (f32[1,32,8]{1,2,0:T(8,128)S(1)}, f32[1,32,8]{1,2,0:T(8,128)}, u32[]{:S(2)}) copy-start(f32[1,32,8]{1,2,0:T(8,128)} %param.15) | copy-start | bytes 3076
  6.6 8.8 %collective-permute-start.6 = (f32[19,8,128]{2,1,0:T(8,128)S(1)}, f32[19,8,128]{2,1,0:T(8,128)S(1)}, u32[]{:S(2)}, u32[]{:S(2)}) collective-permute-start(f32[19,8,128]{2,1,0:T(8,128)S(1)} %get-tuple-element.37), channel_id=1, source_target_pairs={{0,5},{1,4},{2,7},{3,6},{4,1},{5,0},{6,3},{7,2},{8,13},{9,12},{10,... | collective-permute-start | bytes 233480 | tf_op jit(solution)/shard_map/ppermute | solution.py:32
  7.8 7.8 %collective-permute-start.7 = (f32[19,8,128]{2,1,0:T(8,128)S(1)}, f32[19,8,128]{2,1,0:T(8,128)S(1)}, u32[]{:S(2)}, u32[]{:S(2)}) collective-permute-start(f32[19,8,128]{2,1,0:T(8,128)S(1)} %get-tuple-element.38), channel_id=1, source_target_pairs={{1,6},{2,5},{5,2},{6,1},{9,14},{10,13},{13,10},{14,9},{17,22},{18,... | collective-permute-start | bytes 233480 | tf_op jit(solution)/shard_map/ppermute | solution.py:32
  12.1 7.8 %collective-permute-start.3 = (f32[18,32,128]{2,1,0:T(8,128)S(1)}, f32[18,32,128]{2,1,0:T(8,128)S(1)}, u32[]{:S(2)}, u32[]{:S(2)}) collective-permute-start(f32[18,32,128]{2,1,0:T(8,128)S(1)} %get-tuple-element.34), channel_id=1, source_target_pairs={{0,1},{1,0},{2,3},{3,2},{4,5},{5,4},{6,7},{7,6},{8,9},{9,8},{10,11... | collective-permute-start | bytes 884744 | tf_op jit(solution)/shard_map/ppermute | solution.py:32
  12.1 8.9 %collective-permute-start.4 = (f32[18,32,128]{2,1,0:T(8,128)S(1)}, f32[18,32,128]{2,1,0:T(8,128)S(1)}, u32[]{:S(2)}, u32[]{:S(2)}) collective-permute-start(f32[18,32,128]{2,1,0:T(8,128)S(1)} %get-tuple-element.35), channel_id=1, source_target_pairs={{1,2},{2,1},{5,6},{6,5},{9,10},{10,9},{13,14},{14,13},{17,18},{18,... | collective-permute-start | bytes 884744 | tf_op jit(solution)/shard_map/ppermute | solution.py:32
  14.1 5.8 %collective-permute-start.5 = (f32[57,8,128]{2,1,0:T(8,128)S(1)}, f32[57,8,128]{2,1,0:T(8,128)S(1)}, u32[]{:S(2)}, u32[]{:S(2)}) collective-permute-start(f32[57,8,128]{2,1,0:T(8,128)S(1)} %get-tuple-element.36), channel_id=1, source_target_pairs={{0,4},{1,5},{2,6},{3,7},{4,0},{5,1},{6,2},{7,3},{8,12},{9,13},{10,... | collective-permute-start | bytes 700424 | tf_op jit(solution)/shard_map/ppermute | solution.py:32
  15.4 8.7 %collective-permute-start.8 = (f32[14,32,128]{2,1,0:T(8,128)S(1)}, f32[14,32,128]{2,1,0:T(8,128)S(1)}, u32[]{:S(2)}, u32[]{:S(2)}) collective-permute-start(f32[14,32,128]{2,1,0:T(8,128)S(1)} %get-tuple-element.43), channel_id=1, source_target_pairs={{0,1},{1,0},{2,3},{3,2},{4,5},{5,4},{6,7},{7,6},{8,9},{9,8},{10,11... | collective-permute-start | bytes 688136 | tf_op jit(solution)/shard_map/ppermute | solution.py:32
  15.6 10.4 %collective-permute-start.9 = (f32[14,32,128]{2,1,0:T(8,128)S(1)}, f32[14,32,128]{2,1,0:T(8,128)S(1)}, u32[]{:S(2)}, u32[]{:S(2)}) collective-permute-start(f32[14,32,128]{2,1,0:T(8,128)S(1)} %get-tuple-element.44), channel_id=1, source_target_pairs={{1,2},{2,1},{5,6},{6,5},{9,10},{10,9},{13,14},{14,13},{17,18},{18,... | collective-permute-start | bytes 688136 | tf_op jit(solution)/shard_map/ppermute | solution.py:32
  27.8 5.2 %collective-permute-start.12 = (f32[32,128]{1,0:T(8,128)S(1)}, f32[32,128]{1,0:T(8,128)S(1)}, u32[]{:S(2)}, u32[]{:S(2)}) collective-permute-start(f32[32,128]{1,0:T(8,128)S(1)} %get-tuple-element.48.r_0_), channel_id=1, source_target_pairs={{0,24},{8,16},{16,8},{24,0},{1,25},{9,17},{17,9},{25,1},{2,26},{10... | collective-permute-start | bytes 49160 | tf_op jit(solution)/shard_map/ppermute | solution.py:452
  31.2 2.6 %collective-permute-start.11 = (f32[32,128]{1,0:T(8,128)S(1)}, f32[32,128]{1,0:T(8,128)S(1)}, u32[]{:S(2)}, u32[]{:S(2)}) collective-permute-start(f32[32,128]{1,0:T(8,128)S(1)} %get-tuple-element.48.r_0_), channel_id=1, source_target_pairs={{0,16},{8,24},{16,0},{24,8},{1,17},{9,25},{17,1},{25,9},{2,18},{10... | collective-permute-start | bytes 49160 | tf_op jit(solution)/shard_map/ppermute | solution.py:452
  31.6 2.2 %collective-permute-start.10 = (f32[32,128]{1,0:T(8,128)S(1)}, f32[32,128]{1,0:T(8,128)S(1)}, u32[]{:S(2)}, u32[]{:S(2)}) collective-permute-start(f32[32,128]{1,0:T(8,128)S(1)} %get-tuple-element.48.r_0_), channel_id=1, source_target_pairs={{0,8},{8,0},{16,24},{24,16},{1,9},{9,1},{17,25},{25,17},{2,10},{10... | collective-permute-start | bytes 49160 | tf_op jit(solution)/shard_map/ppermute | solution.py:452

commit v6 on v5

--- a/solution.py
+++ b/solution.py
@@ -15,9 +15,9 @@
 BF16 = jnp.bfloat16
 FH = 5
 AH = 3
-WIN = 8
+WIN = 7
 PER = 128 // WIN
-PROF = 112
+PROF = 120
 
 
 def swap(block, flip_x, parity):
@@ -41,7 +41,7 @@
 F_RAW = side_parts(*FWD) + CO_RAW
 A_RAW = side_parts(*ADJ)
 F_WIN = [("fe", c, i) for c in range(3) for i in (2, 3, 4)] + [("fh", 1, 2)]
-F_WIN += [("fh", c, i) for c in range(3) for i in (3, 4)] + CO_WIN
+F_WIN += [("fh", c, 3) for c in range(3)] + [("fh", 0, 4), ("fh", 2, 4)] + CO_WIN
 C_RAW = side_parts(*FWD) + [("fe", 1, 2)] + A_RAW + [("ae", 1, 2)] + CO_RAW
 C_WIN = [(n, c, i) for n in FWD for c in range(3) for i in range(FH)] + CO_RAW + CO_WIN
 

time: 34.7 us -> 34.4 us (level)
  waiting for transfers between devices: 5.17 us -> 4.82 us
    ppermute x7, waiting for transfers between devices: 4.06 us -> 3.7 us  [swap(): return lax.ppermute(block, ('gx', 'gy'), route)]
where the time goes in v6:
time: 34.4 us; the launch traced here: 34.2 us
  starting transfers between devices  18.3 us (53%)
  Pallas kernels  9 us (26%)
  waiting for transfers between devices  4.82 us (14%)
  between operations  2.06 us (6%)
    ppermute x7, starting transfers between devices, swap(): return lax.ppermute(block, ('gx', 'gy'), route)  12.1 us
    ppermute x6, starting transfers between devices, over_wl(): lax.ppermute(v, 'wl', [(i, i ^ k) for i in range(nw)])  6.2 us
    ppermute x7, waiting for transfers between devices, swap(): return lax.ppermute(block, ('gx', 'gy'), route)  3.7 us
    pallas_call x1, Pallas kernels, per_device(): call(lambda *r: forward_body(*r, xl=xl, yl=yl, signals=signals), 'forward...  2.52 us
    pallas_call x1, Pallas kernels, per_device(): call(lambda *r: adjoint_body(*r, xl=xl, yl=yl, omegas=omegas), 'adjoint',...  1.86 us
    pallas_call x1, Pallas kernels, per_device(): call(lambda *r: fetch_body(*r, xl=xl, yl=yl), 'fetch', [ae.shape] * 4 + [...  1.43 us
    pallas_call x1, Pallas kernels, per_device(): call(lambda *r: send_body(*r, xl=xl, yl=yl, nw=nw, owned=owned), 'send',...  1.32 us
    ppermute x6, waiting for transfers between devices, over_wl(): lax.ppermute(v, 'wl', [(i, i ^ k) for i in range(nw)])  1.11 us
  transfers between devices with their start and end apart: 13, of which 6 were waited for; matrix products, arithmetic and copies ran while one was open for 0% of the time, Pallas kernels for 15%

profile of v6, /device:TPU:9, one launch (start us, length us, event | category | flops | bytes accessed | tf_op | source)
XLA Modules:
  0.0 34.2 jit_solution(16257816710113794049)
XLA Ops:
  0.6 1.8 %collective-permute-start.2 = (f32[2,8,32]{2,1,0:T(8,128)}, f32[2,8,32]{2,1,0:T(8,128)S(1)}, u32[]{:S(2)}, u32[]{:S(2)}) collective-permute-start(f32[2,8,32]{2,1,0:T(8,128)} %bitcast.12), channel_id=1, source_target_pairs={{0,24},{8,16},{16,8},{24,0},{1,25},{9,17},{17,9},{25,1},{2,26},{10... | collective-permute-start | bytes 6152 | tf_op jit(solution)/shard_map/ppermute | solution.py:452
  2.5 0.3 collective-permute-start.1
  2.7 0.2 collective-permute-start
  3.6 1.4 %fetch.1 = (f32[768,128]{1,0:T(8,128)S(1)}, f32[768,128]{1,0:T(8,128)S(1)}, f32[768,128]{1,0:T(8,128)S(1)}, f32[768,128]{1,0:T(8,128)S(1)}, f32[256,128]{1,0:T(8...) custom-call(f32[768,128]{1,0:T(8,128)} %bitcast.17, ...), custom_call_target="tpu_custom_call" | custom-call | tf_op jit(solution)/shard_map/fetch/pallas_call | solution.py:463
  5.1 0.1 first.1.r_6_
  5.2 0.0 collective-permute-done.2.r_12_
  5.2 0.0 collective-permute-done.1.r_11_
  5.2 0.0 collective-permute-done.r_10_
  5.3 1.3 %send.1 = (f32[8,32,128]{2,1,0:T(8,128)S(1)}, f32[32,128]{1,0:T(8,128)S(1)}, f32[17,32,128]{2,1,0:T(8,128)S(1)}, f32[17,32,128]{2,1,0:T(8,128)S(1)}, f32[57,8,12...) custom-call(s32[1]{0:T(128)S(6)} %copy.13.r_0_.r_1_, ...), custom_call_target="tpu_custom_call" | custom-call | tf_op jit(solution)/shard_map/send/pallas_call | solution.py:469
  6.6 1.2 %collective-permute-start.6 = (f32[18,8,128]{2,1,0:T(8,128)S(1)}, f32[18,8,128]{2,1,0:T(8,128)S(1)}, u32[]{:S(2)}, u32[]{:S(2)}) collective-permute-start(f32[18,8,128]{2,1,0:T(8,128)S(1)} %get-tuple-element.37), channel_id=1, source_target_pairs={{0,5},{1,4},{2,7},{3,6},{4,1},{5,0},{6,3},{7,2},{8,13},{9,12},{10,... | collective-permute-start | bytes 221192 | tf_op jit(solution)/shard_map/ppermute | solution.py:32
  7.8 4.3 %collective-permute-start.7 = (f32[18,8,128]{2,1,0:T(8,128)S(1)}, f32[18,8,128]{2,1,0:T(8,128)S(1)}, u32[]{:S(2)}, u32[]{:S(2)}) collective-permute-start(f32[18,8,128]{2,1,0:T(8,128)S(1)} %get-tuple-element.38), channel_id=1, source_target_pairs={{1,6},{2,5},{5,2},{6,1},{9,14},{10,13},{13,10},{14,9},{17,22},{18,... | collective-permute-start | bytes 221192 | tf_op jit(solution)/shard_map/ppermute | solution.py:32
  12.1 0.1 collective-permute-start.3
  12.1 2.0 %collective-permute-start.4 = (f32[17,32,128]{2,1,0:T(8,128)S(1)}, f32[17,32,128]{2,1,0:T(8,128)S(1)}, u32[]{:S(2)}, u32[]{:S(2)}) collective-permute-start(f32[17,32,128]{2,1,0:T(8,128)S(1)} %get-tuple-element.35), channel_id=1, source_target_pairs={{1,2},{2,1},{5,6},{6,5},{9,10},{10,9},{13,14},{14,13},{17,18},{18,... | collective-permute-start | bytes 835592 | tf_op jit(solution)/shard_map/ppermute | solution.py:32
  14.1 1.2 %collective-permute-start.5 = (f32[57,8,128]{2,1,0:T(8,128)S(1)}, f32[57,8,128]{2,1,0:T(8,128)S(1)}, u32[]{:S(2)}, u32[]{:S(2)}) collective-permute-start(f32[57,8,128]{2,1,0:T(8,128)S(1)} %get-tuple-element.36), channel_id=1, source_target_pairs={{0,4},{1,5},{2,6},{3,7},{4,0},{5,1},{6,2},{7,3},{8,12},{9,13},{10,... | collective-permute-start | bytes 700424 | tf_op jit(solution)/shard_map/ppermute | solution.py:32
  15.4 0.0 collective-permute-done.6.r_9_.r_10_
  15.4 0.2 collective-permute-start.8
  15.6 0.0 collective-permute-done.7.r_10_.r_11_
  15.6 3.2 %collective-permute-start.9 = (f32[14,32,128]{2,1,0:T(8,128)S(1)}, f32[14,32,128]{2,1,0:T(8,128)S(1)}, u32[]{:S(2)}, u32[]{:S(2)}) collective-permute-start(f32[14,32,128]{2,1,0:T(8,128)S(1)} %get-tuple-element.44), channel_id=1, source_target_pairs={{1,2},{2,1},{5,6},{6,5},{9,10},{10,9},{13,14},{14,13},{17,18},{18,... | collective-permute-start | bytes 688136 | tf_op jit(solution)/shard_map/ppermute | solution.py:32
  19.4 0.5 %collective-permute-done.5.r_8_.r_9_ = f32[57,8,128]{2,1,0:T(8,128)S(1)} collective-permute-done((f32[57,8,128]{2,1,0:T(8,128)S(1)}, f32[57,8,128]{2,1,0:T(8,128)S(1)}, u32[]{:S(2)}, u32[]{:S(2)}) %collective-permute-start.5) | collective-permute-done | bytes 233504 | tf_op jit(solution)/shard_map/ppermute | solution.py:32
  19.9 0.0 collective-permute-done.3.r_6_
  19.9 0.8 %collective-permute-done.4.r_7_ = f32[17,32,128]{2,1,0:T(8,128)S(1)} collective-permute-done((f32[17,32,128]{2,1,0:T(8,128)S(1)}, f32[17,32,128]{2,1,0:T(8,128)S(1)}, u32[]{:S(2)}, u32[]{:S(2)}) %collective-permute-start.4) | collective-permute-done | bytes 278560 | tf_op jit(solution)/shard_map/ppermute | solution.py:32
  20.7 2.5 %forward.1 = (f32[18,40,128]{2,1,0:T(8,128)S(1)}, f32[3,18,40,128]{3,2,1,0:T(8,128)S(1)}, f32[3,18,40,128]{3,2,1,0:T(8,128)S(1)}, f32[3,18,40,128]{3,2,1,0:T(8,128)S(1)}) custom-call(s32[1]{0:T(128)S(6)} %copy.12.r_0_, s32[1]{0:T(128)S(6)} %copy.13.r_0_.r_1_, f32[768,128]{1,0:T(8,128)S(1)} %get-tuple-element.26.r_0_.r_1_.r_2_, ...), custom_call_target="tpu_custom_call" | custom-call | tf_op jit(solution)/shard_map/forward/pallas_call | solution.py:480
  23.2 0.5 %collective-permute-done.8.r_7_ = f32[14,32,128]{2,1,0:T(8,128)S(1)} collective-permute-done((f32[14,32,128]{2,1,0:T(8,128)S(1)}, f32[14,32,128]{2,1,0:T(8,128)S(1)}, u32[]{:S(2)}, u32[]{:S(2)}) %collective-permute-start.8) | collective-permute-done | bytes 229408 | tf_op jit(solution)/shard_map/ppermute | solution.py:32
  23.7 1.9 %collective-permute-done.9.r_8_ = f32[14,32,128]{2,1,0:T(8,128)S(1)} collective-permute-done((f32[14,32,128]{2,1,0:T(8,128)S(1)}, f32[14,32,128]{2,1,0:T(8,128)S(1)}, u32[]{:S(2)}, u32[]{:S(2)}) %collective-permute-start.9) | collective-permute-done | bytes 229408 | tf_op jit(solution)/shard_map/ppermute | solution.py:32
  25.6 1.9 %adjoint.1 = (f32[3,18,40,128]{3,2,1,0:T(8,128)S(1)}, f32[32,128]{1,0:T(8,128)S(1)}) custom-call(s32[1]{0:T(128)S(6)} %copy.13.r_0_.r_1_, f32[768,128]{1,0:T(8,128)S(1)} %get-tuple-element.28.r_3_.r_1_, f32[768,128]{1,0:T(8,128)S(1)} %get-tuple-element.29.r_4_.r_2_, f32[18,40,128]{2,1,0:T(8,128)S(1)} %get-tuple-element.40.r_3_, ...), custom_call_target="tpu_custom_call" | custom-call | tf_op jit(solution)/shard_map/adjoint/pallas_call | solution.py:485
  27.5 3.4 %collective-permute-start.12 = (f32[32,128]{1,0:T(8,128)S(1)}, f32[32,128]{1,0:T(8,128)S(1)}, u32[]{:S(2)}, u32[]{:S(2)}) collective-permute-start(f32[32,128]{1,0:T(8,128)S(1)} %get-tuple-element.48.r_0_), channel_id=1, source_target_pairs={{0,24},{8,16},{16,8},{24,0},{1,25},{9,17},{17,9},{25,1},{2,26},{10... | collective-permute-start | bytes 49160 | tf_op jit(solution)/shard_map/ppermute | solution.py:452
  30.9 0.4 %collective-permute-start.11 = (f32[32,128]{1,0:T(8,128)S(1)}, f32[32,128]{1,0:T(8,128)S(1)}, u32[]{:S(2)}, u32[]{:S(2)}) collective-permute-start(f32[32,128]{1,0:T(8,128)S(1)} %get-tuple-element.48.r_0_), channel_id=1, source_target_pairs={{0,16},{8,24},{16,0},{24,8},{1,17},{9,25},{17,1},{25,9},{2,18},{10... | collective-permute-start | bytes 49160 | tf_op jit(solution)/shard_map/ppermute | solution.py:452
  31.3 0.1 collective-permute-start.10
  31.4 1.0 %store.1 = (f32[768,128]{1,0:T(8,128)}, f32[768,128]{1,0:T(8,128)}) custom-call(f32[3,18,40,128]{3,2,1,0:T(8,128)S(1)} %get-tuple-element.39.r_6_.r_0_, f32[3,18,40,128]{3,2,1,0:T(8,128)S(1)} %get-tuple-element.45.r_1_), custom_call_target="tpu_custom_call" | custom-call | tf_op jit(solution)/shard_map/store/pallas_call | solution.py:490
  32.4 0.3 %collective-permute-done.12.r_3_ = f32[32,128]{1,0:T(8,128)S(1)} collective-permute-done((f32[32,128]{1,0:T(8,128)S(1)}, f32[32,128]{1,0:T(8,128)S(1)}, u32[]{:S(2)}, u32[]{:S(2)}) %collective-permute-start.12) | collective-permute-done | bytes 16416 | tf_op jit(solution)/shard_map/ppermute | solution.py:452
  32.7 0.8 %collective-permute-done.11.r_2_ = f32[32,128]{1,0:T(8,128)S(1)} collective-permute-done((f32[32,128]{1,0:T(8,128)S(1)}, f32[32,128]{1,0:T(8,128)S(1)}, u32[]{:S(2)}, u32[]{:S(2)}) %collective-permute-start.11) | collective-permute-done | bytes 16416 | tf_op jit(solution)/shard_map/ppermute | solution.py:452
  33.5 0.7 %gather_sum.1 = f32[2,8,32]{2,1,0:T(8,128)} custom-call(f32[32,128]{1,0:T(8,128)S(1)} %get-tuple-element.48.r_0_, f32[32,128]{1,0:T(8,128)S(1)} %collective-permute-done.10.r_1_, f32[32,128]{1,0:T(8,128)S(1)} %collective-permute-done.11.r_2_, f32[32,128]{1,0:T(8,128)S(1)} %collective-permute-done.12.r_3_), custom_call_target="tpu_custom_call" | custom-call | tf_op jit(solution)/shard_map/gather_sum/pallas_call | solution.py:492
  (5 shorter events, 0.0 us)
Async XLA Ops:
  0.6 4.6 %collective-permute-start.2 = (f32[2,8,32]{2,1,0:T(8,128)}, f32[2,8,32]{2,1,0:T(8,128)S(1)}, u32[]{:S(2)}, u32[]{:S(2)}) collective-permute-start(f32[2,8,32]{2,1,0:T(8,128)} %bitcast.12), channel_id=1, source_target_pairs={{0,24},{8,16},{16,8},{24,0},{1,25},{9,17},{17,9},{25,1},{2,26},{10... | collective-permute-start | bytes 6152 | tf_op jit(solution)/shard_map/ppermute | solution.py:452
  2.5 2.8 %collective-permute-start.1 = (f32[2,8,32]{2,1,0:T(8,128)}, f32[2,8,32]{2,1,0:T(8,128)S(1)}, u32[]{:S(2)}, u32[]{:S(2)}) collective-permute-start(f32[2,8,32]{2,1,0:T(8,128)} %bitcast.13), channel_id=1, source_target_pairs={{0,16},{8,24},{16,0},{24,8},{1,17},{9,25},{17,1},{25,9},{2,18},{10... | collective-permute-start | bytes 6152 | tf_op jit(solution)/shard_map/ppermute | solution.py:452
  2.7 2.5 %collective-permute-start = (f32[2,8,32]{2,1,0:T(8,128)}, f32[2,8,32]{2,1,0:T(8,128)S(1)}, u32[]{:S(2)}, u32[]{:S(2)}) collective-permute-start(f32[2,8,32]{2,1,0:T(8,128)} %bitcast.14), channel_id=1, source_target_pairs={{0,8},{8,0},{16,24},{24,16},{1,9},{9,1},{17,25},{25,17},{2,10},{10... | collective-permute-start | bytes 6152 | tf_op jit(solution)/shard_map/ppermute | solution.py:452
  3.6 1.6 %copy-start = (f32[2,32,8]{1,2,0:T(8,128)S(1)}, f32[2,32,8]{1,2,0:T(8,128)}, u32[]{:S(2)}) copy-start(f32[2,32,8]{1,2,0:T(8,128)} %param.14) | copy-start | bytes 6148
  3.6 1.6 %copy-start.1 = (f32[1,32,8]{1,2,0:T(8,128)S(1)}, f32[1,32,8]{1,2,0:T(8,128)}, u32[]{:S(2)}) copy-start(f32[1,32,8]{1,2,0:T(8,128)} %param.15) | copy-start | bytes 3076
  6.6 8.8 %collective-permute-start.6 = (f32[18,8,128]{2,1,0:T(8,128)S(1)}, f32[18,8,128]{2,1,0:T(8,128)S(1)}, u32[]{:S(2)}, u32[]{:S(2)}) collective-permute-start(f32[18,8,128]{2,1,0:T(8,128)S(1)} %get-tuple-element.37), channel_id=1, source_target_pairs={{0,5},{1,4},{2,7},{3,6},{4,1},{5,0},{6,3},{7,2},{8,13},{9,12},{10,... | collective-permute-start | bytes 221192 | tf_op jit(solution)/shard_map/ppermute | solution.py:32
  7.8 7.8 %collective-permute-start.7 = (f32[18,8,128]{2,1,0:T(8,128)S(1)}, f32[18,8,128]{2,1,0:T(8,128)S(1)}, u32[]{:S(2)}, u32[]{:S(2)}) collective-permute-start(f32[18,8,128]{2,1,0:T(8,128)S(1)} %get-tuple-element.38), channel_id=1, source_target_pairs={{1,6},{2,5},{5,2},{6,1},{9,14},{10,13},{13,10},{14,9},{17,22},{18,... | collective-permute-start | bytes 221192 | tf_op jit(solution)/shard_map/ppermute | solution.py:32
  12.1 7.8 %collective-permute-start.3 = (f32[17,32,128]{2,1,0:T(8,128)S(1)}, f32[17,32,128]{2,1,0:T(8,128)S(1)}, u32[]{:S(2)}, u32[]{:S(2)}) collective-permute-start(f32[17,32,128]{2,1,0:T(8,128)S(1)} %get-tuple-element.34), channel_id=1, source_target_pairs={{0,1},{1,0},{2,3},{3,2},{4,5},{5,4},{6,7},{7,6},{8,9},{9,8},{10,11... | collective-permute-start | bytes 835592 | tf_op jit(solution)/shard_map/ppermute | solution.py:32
  12.1 8.6 %collective-permute-start.4 = (f32[17,32,128]{2,1,0:T(8,128)S(1)}, f32[17,32,128]{2,1,0:T(8,128)S(1)}, u32[]{:S(2)}, u32[]{:S(2)}) collective-permute-start(f32[17,32,128]{2,1,0:T(8,128)S(1)} %get-tuple-element.35), channel_id=1, source_target_pairs={{1,2},{2,1},{5,6},{6,5},{9,10},{10,9},{13,14},{14,13},{17,18},{18,... | collective-permute-start | bytes 835592 | tf_op jit(solution)/shard_map/ppermute | solution.py:32
  14.1 5.8 %collective-permute-start.5 = (f32[57,8,128]{2,1,0:T(8,128)S(1)}, f32[57,8,128]{2,1,0:T(8,128)S(1)}, u32[]{:S(2)}, u32[]{:S(2)}) collective-permute-start(f32[57,8,128]{2,1,0:T(8,128)S(1)} %get-tuple-element.36), channel_id=1, source_target_pairs={{0,4},{1,5},{2,6},{3,7},{4,0},{5,1},{6,2},{7,3},{8,12},{9,13},{10,... | collective-permute-start | bytes 700424 | tf_op jit(solution)/shard_map/ppermute | solution.py:32
  15.4 8.3 %collective-permute-start.8 = (f32[14,32,128]{2,1,0:T(8,128)S(1)}, f32[14,32,128]{2,1,0:T(8,128)S(1)}, u32[]{:S(2)}, u32[]{:S(2)}) collective-permute-start(f32[14,32,128]{2,1,0:T(8,128)S(1)} %get-tuple-element.43), channel_id=1, source_target_pairs={{0,1},{1,0},{2,3},{3,2},{4,5},{5,4},{6,7},{7,6},{8,9},{9,8},{10,11... | collective-permute-start | bytes 688136 | tf_op jit(solution)/shard_map/ppermute | solution.py:32
  15.6 10.1 %collective-permute-start.9 = (f32[14,32,128]{2,1,0:T(8,128)S(1)}, f32[14,32,128]{2,1,0:T(8,128)S(1)}, u32[]{:S(2)}, u32[]{:S(2)}) collective-permute-start(f32[14,32,128]{2,1,0:T(8,128)S(1)} %get-tuple-element.44), channel_id=1, source_target_pairs={{1,2},{2,1},{5,6},{6,5},{9,10},{10,9},{13,14},{14,13},{17,18},{18,... | collective-permute-start | bytes 688136 | tf_op jit(solution)/shard_map/ppermute | solution.py:32
  27.5 5.2 %collective-permute-start.12 = (f32[32,128]{1,0:T(8,128)S(1)}, f32[32,128]{1,0:T(8,128)S(1)}, u32[]{:S(2)}, u32[]{:S(2)}) collective-permute-start(f32[32,128]{1,0:T(8,128)S(1)} %get-tuple-element.48.r_0_), channel_id=1, source_target_pairs={{0,24},{8,16},{16,8},{24,0},{1,25},{9,17},{17,9},{25,1},{2,26},{10... | collective-permute-start | bytes 49160 | tf_op jit(solution)/shard_map/ppermute | solution.py:452
  30.9 2.6 %collective-permute-start.11 = (f32[32,128]{1,0:T(8,128)S(1)}, f32[32,128]{1,0:T(8,128)S(1)}, u32[]{:S(2)}, u32[]{:S(2)}) collective-permute-start(f32[32,128]{1,0:T(8,128)S(1)} %get-tuple-element.48.r_0_), channel_id=1, source_target_pairs={{0,16},{8,24},{16,0},{24,8},{1,17},{9,25},{17,1},{25,9},{2,18},{10... | collective-permute-start | bytes 49160 | tf_op jit(solution)/shard_map/ppermute | solution.py:452
  31.3 2.2 %collective-permute-start.10 = (f32[32,128]{1,0:T(8,128)S(1)}, f32[32,128]{1,0:T(8,128)S(1)}, u32[]{:S(2)}, u32[]{:S(2)}) collective-permute-start(f32[32,128]{1,0:T(8,128)S(1)} %get-tuple-element.48.r_0_), channel_id=1, source_target_pairs={{0,8},{8,0},{16,24},{24,16},{1,9},{9,1},{17,25},{25,17},{2,10},{10... | collective-permute-start | bytes 49160 | tf_op jit(solution)/shard_map/ppermute | solution.py:452

commit v7 on v6

--- a/solution.py
+++ b/solution.py
@@ -85,7 +85,7 @@
 
 
 def fetch_body(ae, ah, fe, fh, bg, *rest, xl, yl):
-    outs, (h1, aa, ab, sems) = rest[:5], rest[5:]
+    outs, (h1, fh1, aa, ab, sems) = rest[:5], rest[5:]
     copies = [pltpu.make_async_copy(s, d, sems.at[i]) for i, (s, d) in enumerate(zip((ae, ah, fe, fh, bg), outs))]
     for c in copies:
         c.start()
@@ -97,12 +97,10 @@
     for u, (name, c, i) in enumerate(A_RAW):
         for dst, up in ((aa, gy % 2 == 0), (ab, gy % 2 == 1)):
             dst[u] = edge_row(e, h, h1, name == "ah", c, i, up, 0, xl, xl, yl)
-    for c in copies[2:]:
-        c.wait()
-
-
-def first_body(fe, fh, h1, *, xl, yl):
-    stepped(fe, fh, h1, xl, yl)
+    copies[2].wait()
+    copies[3].wait()
+    stepped(outs[2], outs[3], fh1, xl, yl)
+    copies[4].wait()
 
 
 def send_body(mon, fe, fh, ae, ah, bg, fh1, ah1, sp, *rest, xl, yl, nw, owned):
@@ -460,12 +458,11 @@
     layers = over_wl(jnp.transpose(design, (0, 2, 1)))
     fe, fh, ae, ah, bg = flat
     h1 = (3, yl, xl, nz)
-    ae, ah, fe, fh, bg, ah1, aa, ab = call(
+    ae, ah, fe, fh, bg, ah1, fh1, aa, ab = call(
         lambda *r: fetch_body(*r, xl=xl, yl=yl), "fetch",
-        [ae.shape] * 4 + [bg.shape, h1, a_side, a_side], [hbm] * 5, [pltpu.SemaphoreType.DMA((5,))],
+        [ae.shape] * 4 + [bg.shape, h1, h1, a_side, a_side], [hbm] * 5, [pltpu.SemaphoreType.DMA((5,))],
     )(*[pltpu.with_memory_space_constraint(v, pltpu.HBM) for v in (ae, ah, fe, fh, bg)])
     raa, rab = swap(aa, False, 0), swap(ab, False, 1)
-    (fh1,) = call(lambda *r: first_body(*r, xl=xl, yl=yl), "first", [h1], [vmem] * 2)(fe, fh)
     co, prof_t, fa, fb, px, da, db = call(
         lambda *r: send_body(*r, xl=xl, yl=yl, nw=nw, owned=owned), "send",
         [(yl, xl, nz), (xl, nz), f_side, f_side, beside, corner, corner],

time: 34.4 us -> 34.3 us (level)
  no operation moved by 1% of the time
where the time goes in v7:
time: 34.3 us; the launch traced here: 34.1 us
  starting transfers between devices  18.4 us (54%)
  Pallas kernels  8.96 us (26%)
  waiting for transfers between devices  4.77 us (14%)
  between operations  2.03 us (6%)
    ppermute x7, starting transfers between devices, swap(): return lax.ppermute(block, ('gx', 'gy'), route)  12.1 us
    ppermute x6, starting transfers between devices, over_wl(): lax.ppermute(v, 'wl', [(i, i ^ k) for i in range(nw)])  6.26 us
    ppermute x7, waiting for transfers between devices, swap(): return lax.ppermute(block, ('gx', 'gy'), route)  3.64 us
    pallas_call x1, Pallas kernels, per_device(): call(lambda *r: forward_body(*r, xl=xl, yl=yl, signals=signals), 'forward...  2.52 us
    pallas_call x1, Pallas kernels, per_device(): call(lambda *r: adjoint_body(*r, xl=xl, yl=yl, omegas=omegas), 'adjoint',...  1.86 us
    pallas_call x1, Pallas kernels, per_device(): call(lambda *r: fetch_body(*r, xl=xl, yl=yl), 'fetch', [ae.shape] * 4 + [...  1.54 us
    pallas_call x1, Pallas kernels, per_device(): call(lambda *r: send_body(*r, xl=xl, yl=yl, nw=nw, owned=owned), 'send',...  1.32 us
    ppermute x6, waiting for transfers between devices, over_wl(): lax.ppermute(v, 'wl', [(i, i ^ k) for i in range(nw)])  1.14 us
  transfers between devices with their start and end apart: 13, of which 6 were waited for; matrix products, arithmetic and copies ran while one was open for 0% of the time, Pallas kernels for 15%

profile of v7, /device:TPU:9, one launch (start us, length us, event | category | flops | bytes accessed | tf_op | source)
XLA Modules:
  0.0 34.1 jit_solution(7442356060150614789)
XLA Ops:
  0.7 1.8 %collective-permute-start.2 = (f32[2,8,32]{2,1,0:T(8,128)}, f32[2,8,32]{2,1,0:T(8,128)S(1)}, u32[]{:S(2)}, u32[]{:S(2)}) collective-permute-start(f32[2,8,32]{2,1,0:T(8,128)} %bitcast.12), channel_id=1, source_target_pairs={{0,24},{8,16},{16,8},{24,0},{1,25},{9,17},{17,9},{25,1},{2,26},{10... | collective-permute-start | bytes 6152 | tf_op jit(solution)/shard_map/ppermute | solution.py:450
  2.5 0.3 collective-permute-start.1
  2.7 0.2 collective-permute-start
  3.6 1.5 %fetch.1 = (f32[768,128]{1,0:T(8,128)S(1)}, f32[768,128]{1,0:T(8,128)S(1)}, f32[768,128]{1,0:T(8,128)S(1)}, f32[768,128]{1,0:T(8,128)S(1)}, f32[256,128]{1,0:T(8...) custom-call(f32[768,128]{1,0:T(8,128)} %bitcast.17, ...), custom_call_target="tpu_custom_call" | custom-call | tf_op jit(solution)/shard_map/fetch/pallas_call | solution.py:461
  5.2 0.0 collective-permute-done.2.r_12_
  5.2 0.0 collective-permute-done.1.r_11_
  5.2 0.0 collective-permute-done.r_10_
  5.2 1.3 %send.1 = (f32[8,32,128]{2,1,0:T(8,128)S(1)}, f32[32,128]{1,0:T(8,128)S(1)}, f32[17,32,128]{2,1,0:T(8,128)S(1)}, f32[17,32,128]{2,1,0:T(8,128)S(1)}, f32[57,8,12...) custom-call(s32[1]{0:T(128)S(6)} %copy.13.r_0_.r_1_, ...), custom_call_target="tpu_custom_call" | custom-call | tf_op jit(solution)/shard_map/send/pallas_call | solution.py:466
  6.5 1.2 %collective-permute-start.6 = (f32[18,8,128]{2,1,0:T(8,128)S(1)}, f32[18,8,128]{2,1,0:T(8,128)S(1)}, u32[]{:S(2)}, u32[]{:S(2)}) collective-permute-start(f32[18,8,128]{2,1,0:T(8,128)S(1)} %get-tuple-element.39), channel_id=1, source_target_pairs={{0,5},{1,4},{2,7},{3,6},{4,1},{5,0},{6,3},{7,2},{8,13},{9,12},{10,... | collective-permute-start | bytes 221192 | tf_op jit(solution)/shard_map/ppermute | solution.py:32
  7.7 4.3 %collective-permute-start.7 = (f32[18,8,128]{2,1,0:T(8,128)S(1)}, f32[18,8,128]{2,1,0:T(8,128)S(1)}, u32[]{:S(2)}, u32[]{:S(2)}) collective-permute-start(f32[18,8,128]{2,1,0:T(8,128)S(1)} %get-tuple-element.40), channel_id=1, source_target_pairs={{1,6},{2,5},{5,2},{6,1},{9,14},{10,13},{13,10},{14,9},{17,22},{18,... | collective-permute-start | bytes 221192 | tf_op jit(solution)/shard_map/ppermute | solution.py:32
  12.0 0.1 collective-permute-start.3
  12.1 2.0 %collective-permute-start.4 = (f32[17,32,128]{2,1,0:T(8,128)S(1)}, f32[17,32,128]{2,1,0:T(8,128)S(1)}, u32[]{:S(2)}, u32[]{:S(2)}) collective-permute-start(f32[17,32,128]{2,1,0:T(8,128)S(1)} %get-tuple-element.37), channel_id=1, source_target_pairs={{1,2},{2,1},{5,6},{6,5},{9,10},{10,9},{13,14},{14,13},{17,18},{18,... | collective-permute-start | bytes 835592 | tf_op jit(solution)/shard_map/ppermute | solution.py:32
  14.1 1.2 %collective-permute-start.5 = (f32[57,8,128]{2,1,0:T(8,128)S(1)}, f32[57,8,128]{2,1,0:T(8,128)S(1)}, u32[]{:S(2)}, u32[]{:S(2)}) collective-permute-start(f32[57,8,128]{2,1,0:T(8,128)S(1)} %get-tuple-element.38), channel_id=1, source_target_pairs={{0,4},{1,5},{2,6},{3,7},{4,0},{5,1},{6,2},{7,3},{8,12},{9,13},{10,... | collective-permute-start | bytes 700424 | tf_op jit(solution)/shard_map/ppermute | solution.py:32
  15.3 0.0 collective-permute-done.6.r_9_.r_10_
  15.3 0.2 collective-permute-start.8
  15.5 0.0 collective-permute-done.7.r_10_.r_11_
  15.5 3.2 %collective-permute-start.9 = (f32[14,32,128]{2,1,0:T(8,128)S(1)}, f32[14,32,128]{2,1,0:T(8,128)S(1)}, u32[]{:S(2)}, u32[]{:S(2)}) collective-permute-start(f32[14,32,128]{2,1,0:T(8,128)S(1)} %get-tuple-element.46), channel_id=1, source_target_pairs={{1,2},{2,1},{5,6},{6,5},{9,10},{10,9},{13,14},{14,13},{17,18},{18,... | collective-permute-start | bytes 688136 | tf_op jit(solution)/shard_map/ppermute | solution.py:32
  19.3 0.4 %collective-permute-done.5.r_8_.r_9_ = f32[57,8,128]{2,1,0:T(8,128)S(1)} collective-permute-done((f32[57,8,128]{2,1,0:T(8,128)S(1)}, f32[57,8,128]{2,1,0:T(8,128)S(1)}, u32[]{:S(2)}, u32[]{:S(2)}) %collective-permute-start.5) | collective-permute-done | bytes 233504 | tf_op jit(solution)/shard_map/ppermute | solution.py:32
  19.8 0.0 collective-permute-done.3.r_6_
  19.8 0.8 %collective-permute-done.4.r_7_ = f32[17,32,128]{2,1,0:T(8,128)S(1)} collective-permute-done((f32[17,32,128]{2,1,0:T(8,128)S(1)}, f32[17,32,128]{2,1,0:T(8,128)S(1)}, u32[]{:S(2)}, u32[]{:S(2)}) %collective-permute-start.4) | collective-permute-done | bytes 278560 | tf_op jit(solution)/shard_map/ppermute | solution.py:32
  20.6 2.5 %forward.1 = (f32[18,40,128]{2,1,0:T(8,128)S(1)}, f32[3,18,40,128]{3,2,1,0:T(8,128)S(1)}, f32[3,18,40,128]{3,2,1,0:T(8,128)S(1)}, f32[3,18,40,128]{3,2,1,0:T(8,128)S(1)}) custom-call(s32[1]{0:T(128)S(6)} %copy.12.r_0_, s32[1]{0:T(128)S(6)} %copy.13.r_0_.r_1_, f32[768,128]{1,0:T(8,128)S(1)} %get-tuple-element.27.r_1_.r_2_, ...), custom_call_target="tpu_custom_call" | custom-call | tf_op jit(solution)/shard_map/forward/pallas_call | solution.py:477
  23.1 0.5 %collective-permute-done.8.r_7_ = f32[14,32,128]{2,1,0:T(8,128)S(1)} collective-permute-done((f32[14,32,128]{2,1,0:T(8,128)S(1)}, f32[14,32,128]{2,1,0:T(8,128)S(1)}, u32[]{:S(2)}, u32[]{:S(2)}) %collective-permute-start.8) | collective-permute-done | bytes 229408 | tf_op jit(solution)/shard_map/ppermute | solution.py:32
  23.6 1.9 %collective-permute-done.9.r_8_ = f32[14,32,128]{2,1,0:T(8,128)S(1)} collective-permute-done((f32[14,32,128]{2,1,0:T(8,128)S(1)}, f32[14,32,128]{2,1,0:T(8,128)S(1)}, u32[]{:S(2)}, u32[]{:S(2)}) %collective-permute-start.9) | collective-permute-done | bytes 229408 | tf_op jit(solution)/shard_map/ppermute | solution.py:32
  25.5 1.9 %adjoint.1 = (f32[3,18,40,128]{3,2,1,0:T(8,128)S(1)}, f32[32,128]{1,0:T(8,128)S(1)}) custom-call(s32[1]{0:T(128)S(6)} %copy.13.r_0_.r_1_, f32[768,128]{1,0:T(8,128)S(1)} %get-tuple-element.29.r_3_.r_1_, f32[768,128]{1,0:T(8,128)S(1)} %get-tuple-element.30.r_4_.r_2_, f32[18,40,128]{2,1,0:T(8,128)S(1)} %get-tuple-element.42.r_3_, ...), custom_call_target="tpu_custom_call" | custom-call | tf_op jit(solution)/shard_map/adjoint/pallas_call | solution.py:482
  27.4 3.5 %collective-permute-start.12 = (f32[32,128]{1,0:T(8,128)S(1)}, f32[32,128]{1,0:T(8,128)S(1)}, u32[]{:S(2)}, u32[]{:S(2)}) collective-permute-start(f32[32,128]{1,0:T(8,128)S(1)} %get-tuple-element.50.r_0_), channel_id=1, source_target_pairs={{0,24},{8,16},{16,8},{24,0},{1,25},{9,17},{17,9},{25,1},{2,26},{10... | collective-permute-start | bytes 49160 | tf_op jit(solution)/shard_map/ppermute | solution.py:450
  30.8 0.4 %collective-permute-start.11 = (f32[32,128]{1,0:T(8,128)S(1)}, f32[32,128]{1,0:T(8,128)S(1)}, u32[]{:S(2)}, u32[]{:S(2)}) collective-permute-start(f32[32,128]{1,0:T(8,128)S(1)} %get-tuple-element.50.r_0_), channel_id=1, source_target_pairs={{0,16},{8,24},{16,0},{24,8},{1,17},{9,25},{17,1},{25,9},{2,18},{10... | collective-permute-start | bytes 49160 | tf_op jit(solution)/shard_map/ppermute | solution.py:450
  31.2 0.1 collective-permute-start.10
  31.3 1.0 %store.1 = (f32[768,128]{1,0:T(8,128)}, f32[768,128]{1,0:T(8,128)}) custom-call(f32[3,18,40,128]{3,2,1,0:T(8,128)S(1)} %get-tuple-element.41.r_6_.r_0_, f32[3,18,40,128]{3,2,1,0:T(8,128)S(1)} %get-tuple-element.47.r_1_), custom_call_target="tpu_custom_call" | custom-call | tf_op jit(solution)/shard_map/store/pallas_call | solution.py:487
  32.3 0.3 %collective-permute-done.12.r_3_ = f32[32,128]{1,0:T(8,128)S(1)} collective-permute-done((f32[32,128]{1,0:T(8,128)S(1)}, f32[32,128]{1,0:T(8,128)S(1)}, u32[]{:S(2)}, u32[]{:S(2)}) %collective-permute-start.12) | collective-permute-done | bytes 16416 | tf_op jit(solution)/shard_map/ppermute | solution.py:450
  32.7 0.8 %collective-permute-done.11.r_2_ = f32[32,128]{1,0:T(8,128)S(1)} collective-permute-done((f32[32,128]{1,0:T(8,128)S(1)}, f32[32,128]{1,0:T(8,128)S(1)}, u32[]{:S(2)}, u32[]{:S(2)}) %collective-permute-start.11) | collective-permute-done | bytes 16416 | tf_op jit(solution)/shard_map/ppermute | solution.py:450
  33.4 0.0 collective-permute-done.10.r_1_
  33.4 0.7 %gather_sum.1 = f32[2,8,32]{2,1,0:T(8,128)} custom-call(f32[32,128]{1,0:T(8,128)S(1)} %get-tuple-element.50.r_0_, f32[32,128]{1,0:T(8,128)S(1)} %collective-permute-done.10.r_1_, f32[32,128]{1,0:T(8,128)S(1)} %collective-permute-done.11.r_2_, f32[32,128]{1,0:T(8,128)S(1)} %collective-permute-done.12.r_3_), custom_call_target="tpu_custom_call" | custom-call | tf_op jit(solution)/shard_map/gather_sum/pallas_call | solution.py:489
  (4 shorter events, 0.0 us)
Async XLA Ops:
  0.6 4.6 %copy-start = (f32[2,32,8]{1,2,0:T(8,128)S(1)}, f32[2,32,8]{1,2,0:T(8,128)}, u32[]{:S(2)}) copy-start(f32[2,32,8]{1,2,0:T(8,128)} %param.14) | copy-start | bytes 6148
  0.6 4.6 %copy-start.1 = (f32[1,32,8]{1,2,0:T(8,128)S(1)}, f32[1,32,8]{1,2,0:T(8,128)}, u32[]{:S(2)}) copy-start(f32[1,32,8]{1,2,0:T(8,128)} %param.15) | copy-start | bytes 3076
  0.7 4.5 %collective-permute-start.2 = (f32[2,8,32]{2,1,0:T(8,128)}, f32[2,8,32]{2,1,0:T(8,128)S(1)}, u32[]{:S(2)}, u32[]{:S(2)}) collective-permute-start(f32[2,8,32]{2,1,0:T(8,128)} %bitcast.12), channel_id=1, source_target_pairs={{0,24},{8,16},{16,8},{24,0},{1,25},{9,17},{17,9},{25,1},{2,26},{10... | collective-permute-start | bytes 6152 | tf_op jit(solution)/shard_map/ppermute | solution.py:450
  2.5 2.7 %collective-permute-start.1 = (f32[2,8,32]{2,1,0:T(8,128)}, f32[2,8,32]{2,1,0:T(8,128)S(1)}, u32[]{:S(2)}, u32[]{:S(2)}) collective-permute-start(f32[2,8,32]{2,1,0:T(8,128)} %bitcast.13), channel_id=1, source_target_pairs={{0,16},{8,24},{16,0},{24,8},{1,17},{9,25},{17,1},{25,9},{2,18},{10... | collective-permute-start | bytes 6152 | tf_op jit(solution)/shard_map/ppermute | solution.py:450
  2.7 2.5 %collective-permute-start = (f32[2,8,32]{2,1,0:T(8,128)}, f32[2,8,32]{2,1,0:T(8,128)S(1)}, u32[]{:S(2)}, u32[]{:S(2)}) collective-permute-start(f32[2,8,32]{2,1,0:T(8,128)} %bitcast.14), channel_id=1, source_target_pairs={{0,8},{8,0},{16,24},{24,16},{1,9},{9,1},{17,25},{25,17},{2,10},{10... | collective-permute-start | bytes 6152 | tf_op jit(solution)/shard_map/ppermute | solution.py:450
  6.5 8.8 %collective-permute-start.6 = (f32[18,8,128]{2,1,0:T(8,128)S(1)}, f32[18,8,128]{2,1,0:T(8,128)S(1)}, u32[]{:S(2)}, u32[]{:S(2)}) collective-permute-start(f32[18,8,128]{2,1,0:T(8,128)S(1)} %get-tuple-element.39), channel_id=1, source_target_pairs={{0,5},{1,4},{2,7},{3,6},{4,1},{5,0},{6,3},{7,2},{8,13},{9,12},{10,... | collective-permute-start | bytes 221192 | tf_op jit(solution)/shard_map/ppermute | solution.py:32
  7.7 7.8 %collective-permute-start.7 = (f32[18,8,128]{2,1,0:T(8,128)S(1)}, f32[18,8,128]{2,1,0:T(8,128)S(1)}, u32[]{:S(2)}, u32[]{:S(2)}) collective-permute-start(f32[18,8,128]{2,1,0:T(8,128)S(1)} %get-tuple-element.40), channel_id=1, source_target_pairs={{1,6},{2,5},{5,2},{6,1},{9,14},{10,13},{13,10},{14,9},{17,22},{18,... | collective-permute-start | bytes 221192 | tf_op jit(solution)/shard_map/ppermute | solution.py:32
  12.0 7.8 %collective-permute-start.3 = (f32[17,32,128]{2,1,0:T(8,128)S(1)}, f32[17,32,128]{2,1,0:T(8,128)S(1)}, u32[]{:S(2)}, u32[]{:S(2)}) collective-permute-start(f32[17,32,128]{2,1,0:T(8,128)S(1)} %get-tuple-element.36), channel_id=1, source_target_pairs={{0,1},{1,0},{2,3},{3,2},{4,5},{5,4},{6,7},{7,6},{8,9},{9,8},{10,11... | collective-permute-start | bytes 835592 | tf_op jit(solution)/shard_map/ppermute | solution.py:32
  12.1 8.5 %collective-permute-start.4 = (f32[17,32,128]{2,1,0:T(8,128)S(1)}, f32[17,32,128]{2,1,0:T(8,128)S(1)}, u32[]{:S(2)}, u32[]{:S(2)}) collective-permute-start(f32[17,32,128]{2,1,0:T(8,128)S(1)} %get-tuple-element.37), channel_id=1, source_target_pairs={{1,2},{2,1},{5,6},{6,5},{9,10},{10,9},{13,14},{14,13},{17,18},{18,... | collective-permute-start | bytes 835592 | tf_op jit(solution)/shard_map/ppermute | solution.py:32
  14.1 5.7 %collective-permute-start.5 = (f32[57,8,128]{2,1,0:T(8,128)S(1)}, f32[57,8,128]{2,1,0:T(8,128)S(1)}, u32[]{:S(2)}, u32[]{:S(2)}) collective-permute-start(f32[57,8,128]{2,1,0:T(8,128)S(1)} %get-tuple-element.38), channel_id=1, source_target_pairs={{0,4},{1,5},{2,6},{3,7},{4,0},{5,1},{6,2},{7,3},{8,12},{9,13},{10,... | collective-permute-start | bytes 700424 | tf_op jit(solution)/shard_map/ppermute | solution.py:32
  15.3 8.3 %collective-permute-start.8 = (f32[14,32,128]{2,1,0:T(8,128)S(1)}, f32[14,32,128]{2,1,0:T(8,128)S(1)}, u32[]{:S(2)}, u32[]{:S(2)}) collective-permute-start(f32[14,32,128]{2,1,0:T(8,128)S(1)} %get-tuple-element.45), channel_id=1, source_target_pairs={{0,1},{1,0},{2,3},{3,2},{4,5},{5,4},{6,7},{7,6},{8,9},{9,8},{10,11... | collective-permute-start | bytes 688136 | tf_op jit(solution)/shard_map/ppermute | solution.py:32
  15.5 10.0 %collective-permute-start.9 = (f32[14,32,128]{2,1,0:T(8,128)S(1)}, f32[14,32,128]{2,1,0:T(8,128)S(1)}, u32[]{:S(2)}, u32[]{:S(2)}) collective-permute-start(f32[14,32,128]{2,1,0:T(8,128)S(1)} %get-tuple-element.46), channel_id=1, source_target_pairs={{1,2},{2,1},{5,6},{6,5},{9,10},{10,9},{13,14},{14,13},{17,18},{18,... | collective-permute-start | bytes 688136 | tf_op jit(solution)/shard_map/ppermute | solution.py:32
  27.4 5.3 %collective-permute-start.12 = (f32[32,128]{1,0:T(8,128)S(1)}, f32[32,128]{1,0:T(8,128)S(1)}, u32[]{:S(2)}, u32[]{:S(2)}) collective-permute-start(f32[32,128]{1,0:T(8,128)S(1)} %get-tuple-element.50.r_0_), channel_id=1, source_target_pairs={{0,24},{8,16},{16,8},{24,0},{1,25},{9,17},{17,9},{25,1},{2,26},{10... | collective-permute-start | bytes 49160 | tf_op jit(solution)/shard_map/ppermute | solution.py:450
  30.8 2.6 %collective-permute-start.11 = (f32[32,128]{1,0:T(8,128)S(1)}, f32[32,128]{1,0:T(8,128)S(1)}, u32[]{:S(2)}, u32[]{:S(2)}) collective-permute-start(f32[32,128]{1,0:T(8,128)S(1)} %get-tuple-element.50.r_0_), channel_id=1, source_target_pairs={{0,16},{8,24},{16,0},{24,8},{1,17},{9,25},{17,1},{25,9},{2,18},{10... | collective-permute-start | bytes 49160 | tf_op jit(solution)/shard_map/ppermute | solution.py:450
  31.2 2.2 %collective-permute-start.10 = (f32[32,128]{1,0:T(8,128)S(1)}, f32[32,128]{1,0:T(8,128)S(1)}, u32[]{:S(2)}, u32[]{:S(2)}) collective-permute-start(f32[32,128]{1,0:T(8,128)S(1)} %get-tuple-element.50.r_0_), channel_id=1, source_target_pairs={{0,8},{8,0},{16,24},{24,16},{1,9},{9,1},{17,25},{25,17},{2,10},{10... | collective-permute-start | bytes 49160 | tf_op jit(solution)/shard_map/ppermute | solution.py:450

commit v8 on v7

--- a/solution.py
+++ b/solution.py
@@ -84,11 +84,14 @@
     return jnp.where(up, flat(h, yl - 1 - i), h1[c, i, pl.ds(x, count), :])
 
 
-def fetch_body(ae, ah, fe, fh, bg, *rest, xl, yl):
-    outs, (h1, fh1, aa, ab, sems) = rest[:5], rest[5:]
+def fetch_body(ae, ah, fe, fh, bg, sp, *rest, xl, yl):
+    outs, (h1, fh1, aa, ab, prof_t, turn, sems) = rest[:5], rest[5:]
     copies = [pltpu.make_async_copy(s, d, sems.at[i]) for i, (s, d) in enumerate(zip((ae, ah, fe, fh, bg), outs))]
     for c in copies:
         c.start()
+    turn[...] = jnp.zeros((128, 128), F32)
+    turn[0:yl, 0:xl] = sp[...]
+    prof_t[...] = jnp.transpose(turn[...])[0:xl]
     copies[0].wait()
     copies[1].wait()
     e, h = outs[0], outs[1]
@@ -103,8 +106,8 @@
     copies[4].wait()
 
 
-def send_body(mon, fe, fh, ae, ah, bg, fh1, ah1, sp, *rest, xl, yl, nw, owned):
-    parts, (co, prof_t, fa, fb, px, da, db, turn) = rest[:nw], rest[nw:]
+def send_body(mon, fe, fh, ae, ah, bg, fh1, ah1, prof_t, *rest, xl, yl, nw, owned):
+    parts, (co, fa, fb, px, da, db, turn) = rest[:nw], rest[nw:]
     gx, gy, w = lax.axis_index("gx"), lax.axis_index("gy"), lax.axis_index("wl")
     plane = xl * yl
     depth = nw * owned
@@ -121,8 +124,6 @@
         moved = pltpu.roll(layers, (Z0 - depth * y) % 128, 1)
         perm = jnp.where((lane >= Z0) & (lane < Z0 + depth), moved, bg[pl.ds(y, xl, stride=yl), :])
         co[y] = DT / perm
-    turn[0:yl, 0:xl] = sp[...]
-    prof_t[...] = jnp.transpose(turn[...])[0:xl]
     low_x = gx == 0
     x8 = pl.multiple_of(jnp.where(low_x, xl - 8, 0), 8)
 
@@ -458,16 +459,17 @@
     layers = over_wl(jnp.transpose(design, (0, 2, 1)))
     fe, fh, ae, ah, bg = flat
     h1 = (3, yl, xl, nz)
-    ae, ah, fe, fh, bg, ah1, fh1, aa, ab = call(
+    ae, ah, fe, fh, bg, ah1, fh1, aa, ab, prof_t = call(
         lambda *r: fetch_body(*r, xl=xl, yl=yl), "fetch",
-        [ae.shape] * 4 + [bg.shape, h1, h1, a_side, a_side], [hbm] * 5, [pltpu.SemaphoreType.DMA((5,))],
-    )(*[pltpu.with_memory_space_constraint(v, pltpu.HBM) for v in (ae, ah, fe, fh, bg)])
+        [ae.shape] * 4 + [bg.shape, h1, h1, a_side, a_side, (xl, nz)], [hbm] * 5 + [vmem],
+        [ext(128, 128), pltpu.SemaphoreType.DMA((5,))],
+    )(*[pltpu.with_memory_space_constraint(v, pltpu.HBM) for v in (ae, ah, fe, fh, bg)], sp)
     raa, rab = swap(aa, False, 0), swap(ab, False, 1)
-    co, prof_t, fa, fb, px, da, db = call(
+    co, fa, fb, px, da, db = call(
         lambda *r: send_body(*r, xl=xl, yl=yl, nw=nw, owned=owned), "send",
-        [(yl, xl, nz), (xl, nz), f_side, f_side, beside, corner, corner],
+        [(yl, xl, nz), f_side, f_side, beside, corner, corner],
         [smem] + [vmem] * (8 + nw), [ext(128, 128)],
-    )(monitor_layer, fe, fh, ae, ah, bg, fh1, ah1, sp, *layers)
+    )(monitor_layer, fe, fh, ae, ah, bg, fh1, ah1, prof_t, *layers)
     rfa, rfb = swap(fa, False, 0), swap(fb, False, 1)
     rx = swap(px, True, None)
     rda, rdb = swap(da, True, 0), swap(db, True, 1)

time: 34.3 us -> 35 us (1.020)
  starting transfers between devices: 18.4 us -> 17.7 us
  waiting for transfers between devices: 4.77 us -> 5.45 us
  local copies, waits for them, and re-layouts: 0.01 us -> 0.68 us
    ppermute x6, starting transfers between devices: 6.26 us -> 5.56 us  [over_wl(): lax.ppermute(v, 'wl', [(i, i ^ k) for i in range(nw)])]
    ppermute x7, waiting for transfers between devices: 3.64 us -> 4.34 us  [swap(): return lax.ppermute(block, ('gx', 'gy'), route)]
    unnamed x4, local copies, waits for them, and re-layouts: 0.01 us -> 0.68 us
where the time goes in v8:
time: 35 us; the launch traced here: 34.8 us
  starting transfers between devices  17.7 us (51%)
  Pallas kernels  8.93 us (26%)
  waiting for transfers between devices  5.45 us (16%)
  between operations  2.04 us (6%)
  local copies, waits for them, and re-layouts  0.68 us (2%)
    ppermute x7, starting transfers between devices, swap(): return lax.ppermute(block, ('gx', 'gy'), route)  12.1 us
    ppermute x6, starting transfers between devices, over_wl(): lax.ppermute(v, 'wl', [(i, i ^ k) for i in range(nw)])  5.56 us
    ppermute x7, waiting for transfers between devices, swap(): return lax.ppermute(block, ('gx', 'gy'), route)  4.34 us
    pallas_call x1, Pallas kernels, per_device(): call(lambda *r: forward_body(*r, xl=xl, yl=yl, signals=signals), 'forward...  2.53 us
    pallas_call x1, Pallas kernels, per_device(): call(lambda *r: adjoint_body(*r, xl=xl, yl=yl, omegas=omegas), 'adjoint',...  1.86 us
    pallas_call x1, Pallas kernels, per_device(): call(lambda *r: fetch_body(*r, xl=xl, yl=yl), 'fetch', [ae.shape] * 4 + [...  1.54 us
    pallas_call x1, Pallas kernels, per_device(): call(lambda *r: send_body(*r, xl=xl, yl=yl, nw=nw, owned=owned), 'send',...  1.29 us
    ppermute x6, waiting for transfers between devices, over_wl(): lax.ppermute(v, 'wl', [(i, i ^ k) for i in range(nw)])  1.11 us
  transfers between devices with their start and end apart: 13, of which 6 were waited for; matrix products, arithmetic and copies ran while one was open for 0% of the time, Pallas kernels for 15%

profile of v8, /device:TPU:9, one launch (start us, length us, event | category | flops | bytes accessed | tf_op | source)
XLA Modules:
  0.0 34.8 jit_solution(6229547667886237491)
XLA Ops:
  0.6 1.8 %collective-permute-start.2 = (f32[2,8,32]{2,1,0:T(8,128)}, f32[2,8,32]{2,1,0:T(8,128)S(1)}, u32[]{:S(2)}, u32[]{:S(2)}) collective-permute-start(f32[2,8,32]{2,1,0:T(8,128)} %bitcast.12), channel_id=1, source_target_pairs={{0,24},{8,16},{16,8},{24,0},{1,25},{9,17},{17,9},{25,1},{2,26},{10... | collective-permute-start | bytes 6152 | tf_op jit(solution)/shard_map/ppermute | solution.py:451
  2.5 0.3 collective-permute-start.1
  2.7 0.2 collective-permute-start
  3.6 0.7 %copy-done.1 = f32[1,32,8]{1,2,0:T(8,128)S(1)} copy-done((f32[1,32,8]{1,2,0:T(8,128)S(1)}, f32[1,32,8]{1,2,0:T(8,128)}, u32[]{:S(2)}) %copy-start.1) | copy-done | bytes 1048
  4.3 1.5 %fetch.1 = (f32[768,128]{1,0:T(8,128)S(1)}, f32[768,128]{1,0:T(8,128)S(1)}, f32[768,128]{1,0:T(8,128)S(1)}, f32[768,128]{1,0:T(8,128)S(1)}, f32[256,128]{1,0:T(8...) custom-call(f32[768,128]{1,0:T(8,128)} %bitcast.17, ...), custom_call_target="tpu_custom_call" | custom-call | tf_op jit(solution)/shard_map/fetch/pallas_call | solution.py:462
  5.8 0.0 collective-permute-done.2.r_12_
  5.9 0.0 collective-permute-done.1.r_11_
  5.9 0.0 collective-permute-done.r_10_
  5.9 1.3 %send.1 = (f32[8,32,128]{2,1,0:T(8,128)S(1)}, f32[17,32,128]{2,1,0:T(8,128)S(1)}, f32[17,32,128]{2,1,0:T(8,128)S(1)}, f32[57,8,128]{2,1,0:T(8,128)S(1)}, f32[18,...) custom-call(s32[1]{0:T(128)S(6)} %copy.13.r_0_.r_1_, f32[768,128]{1,0:T(8,128)S(1)} %get-tuple-element.27.r_1_.r_2_, ...), custom_call_target="tpu_custom_call" | custom-call | tf_op jit(solution)/shard_map/send/pallas_call | solution.py:468
  7.2 1.2 %collective-permute-start.6 = (f32[18,8,128]{2,1,0:T(8,128)S(1)}, f32[18,8,128]{2,1,0:T(8,128)S(1)}, u32[]{:S(2)}, u32[]{:S(2)}) collective-permute-start(f32[18,8,128]{2,1,0:T(8,128)S(1)} %get-tuple-element.39), channel_id=1, source_target_pairs={{0,5},{1,4},{2,7},{3,6},{4,1},{5,0},{6,3},{7,2},{8,13},{9,12},{10,... | collective-permute-start | bytes 221192 | tf_op jit(solution)/shard_map/ppermute | solution.py:32
  8.4 4.3 %collective-permute-start.7 = (f32[18,8,128]{2,1,0:T(8,128)S(1)}, f32[18,8,128]{2,1,0:T(8,128)S(1)}, u32[]{:S(2)}, u32[]{:S(2)}) collective-permute-start(f32[18,8,128]{2,1,0:T(8,128)S(1)} %get-tuple-element.40), channel_id=1, source_target_pairs={{1,6},{2,5},{5,2},{6,1},{9,14},{10,13},{13,10},{14,9},{17,22},{18,... | collective-permute-start | bytes 221192 | tf_op jit(solution)/shard_map/ppermute | solution.py:32
  12.6 0.1 collective-permute-start.3
  12.7 2.0 %collective-permute-start.4 = (f32[17,32,128]{2,1,0:T(8,128)S(1)}, f32[17,32,128]{2,1,0:T(8,128)S(1)}, u32[]{:S(2)}, u32[]{:S(2)}) collective-permute-start(f32[17,32,128]{2,1,0:T(8,128)S(1)} %get-tuple-element.37), channel_id=1, source_target_pairs={{1,2},{2,1},{5,6},{6,5},{9,10},{10,9},{13,14},{14,13},{17,18},{18,... | collective-permute-start | bytes 835592 | tf_op jit(solution)/shard_map/ppermute | solution.py:32
  14.7 1.2 %collective-permute-start.5 = (f32[57,8,128]{2,1,0:T(8,128)S(1)}, f32[57,8,128]{2,1,0:T(8,128)S(1)}, u32[]{:S(2)}, u32[]{:S(2)}) collective-permute-start(f32[57,8,128]{2,1,0:T(8,128)S(1)} %get-tuple-element.38), channel_id=1, source_target_pairs={{0,4},{1,5},{2,6},{3,7},{4,0},{5,1},{6,2},{7,3},{8,12},{9,13},{10,... | collective-permute-start | bytes 700424 | tf_op jit(solution)/shard_map/ppermute | solution.py:32
  15.9 0.0 collective-permute-done.6.r_9_.r_10_
  16.0 0.2 collective-permute-start.8
  16.2 0.0 collective-permute-done.7.r_10_.r_11_
  16.2 3.2 %collective-permute-start.9 = (f32[14,32,128]{2,1,0:T(8,128)S(1)}, f32[14,32,128]{2,1,0:T(8,128)S(1)}, u32[]{:S(2)}, u32[]{:S(2)}) collective-permute-start(f32[14,32,128]{2,1,0:T(8,128)S(1)} %get-tuple-element.46), channel_id=1, source_target_pairs={{1,2},{2,1},{5,6},{6,5},{9,10},{10,9},{13,14},{14,13},{17,18},{18,... | collective-permute-start | bytes 688136 | tf_op jit(solution)/shard_map/ppermute | solution.py:32
  20.0 1.1 %collective-permute-done.5.r_8_.r_9_ = f32[57,8,128]{2,1,0:T(8,128)S(1)} collective-permute-done((f32[57,8,128]{2,1,0:T(8,128)S(1)}, f32[57,8,128]{2,1,0:T(8,128)S(1)}, u32[]{:S(2)}, u32[]{:S(2)}) %collective-permute-start.5) | collective-permute-done | bytes 233504 | tf_op jit(solution)/shard_map/ppermute | solution.py:32
  21.1 0.0 collective-permute-done.3.r_6_
  21.1 0.8 %collective-permute-done.4.r_7_ = f32[17,32,128]{2,1,0:T(8,128)S(1)} collective-permute-done((f32[17,32,128]{2,1,0:T(8,128)S(1)}, f32[17,32,128]{2,1,0:T(8,128)S(1)}, u32[]{:S(2)}, u32[]{:S(2)}) %collective-permute-start.4) | collective-permute-done | bytes 278560 | tf_op jit(solution)/shard_map/ppermute | solution.py:32
  21.9 2.5 %forward.1 = (f32[18,40,128]{2,1,0:T(8,128)S(1)}, f32[3,18,40,128]{3,2,1,0:T(8,128)S(1)}, f32[3,18,40,128]{3,2,1,0:T(8,128)S(1)}, f32[3,18,40,128]{3,2,1,0:T(8,128)S(1)}) custom-call(s32[1]{0:T(128)S(6)} %copy.12.r_0_, s32[1]{0:T(128)S(6)} %copy.13.r_0_.r_1_, f32[768,128]{1,0:T(8,128)S(1)} %get-tuple-element.27.r_1_.r_2_, ...), custom_call_target="tpu_custom_call" | custom-call | tf_op jit(solution)/shard_map/forward/pallas_call | solution.py:479
  24.5 0.5 %collective-permute-done.8.r_7_ = f32[14,32,128]{2,1,0:T(8,128)S(1)} collective-permute-done((f32[14,32,128]{2,1,0:T(8,128)S(1)}, f32[14,32,128]{2,1,0:T(8,128)S(1)}, u32[]{:S(2)}, u32[]{:S(2)}) %collective-permute-start.8) | collective-permute-done | bytes 229408 | tf_op jit(solution)/shard_map/ppermute | solution.py:32
  24.9 1.9 %collective-permute-done.9.r_8_ = f32[14,32,128]{2,1,0:T(8,128)S(1)} collective-permute-done((f32[14,32,128]{2,1,0:T(8,128)S(1)}, f32[14,32,128]{2,1,0:T(8,128)S(1)}, u32[]{:S(2)}, u32[]{:S(2)}) %collective-permute-start.9) | collective-permute-done | bytes 229408 | tf_op jit(solution)/shard_map/ppermute | solution.py:32
  26.8 1.9 %adjoint.1 = (f32[3,18,40,128]{3,2,1,0:T(8,128)S(1)}, f32[32,128]{1,0:T(8,128)S(1)}) custom-call(s32[1]{0:T(128)S(6)} %copy.13.r_0_.r_1_, f32[768,128]{1,0:T(8,128)S(1)} %get-tuple-element.29.r_3_.r_1_, f32[768,128]{1,0:T(8,128)S(1)} %get-tuple-element.30.r_4_.r_2_, f32[18,40,128]{2,1,0:T(8,128)S(1)} %get-tuple-element.42.r_3_, ...), custom_call_target="tpu_custom_call" | custom-call | tf_op jit(solution)/shard_map/adjoint/pallas_call | solution.py:484
  28.7 2.8 %collective-permute-start.12 = (f32[32,128]{1,0:T(8,128)S(1)}, f32[32,128]{1,0:T(8,128)S(1)}, u32[]{:S(2)}, u32[]{:S(2)}) collective-permute-start(f32[32,128]{1,0:T(8,128)S(1)} %get-tuple-element.50.r_0_), channel_id=1, source_target_pairs={{0,24},{8,16},{16,8},{24,0},{1,25},{9,17},{17,9},{25,1},{2,26},{10... | collective-permute-start | bytes 49160 | tf_op jit(solution)/shard_map/ppermute | solution.py:451
  31.5 0.4 %collective-permute-start.11 = (f32[32,128]{1,0:T(8,128)S(1)}, f32[32,128]{1,0:T(8,128)S(1)}, u32[]{:S(2)}, u32[]{:S(2)}) collective-permute-start(f32[32,128]{1,0:T(8,128)S(1)} %get-tuple-element.50.r_0_), channel_id=1, source_target_pairs={{0,16},{8,24},{16,0},{24,8},{1,17},{9,25},{17,1},{25,9},{2,18},{10... | collective-permute-start | bytes 49160 | tf_op jit(solution)/shard_map/ppermute | solution.py:451
  31.8 0.1 collective-permute-start.10
  31.9 1.0 %store.1 = (f32[768,128]{1,0:T(8,128)}, f32[768,128]{1,0:T(8,128)}) custom-call(f32[3,18,40,128]{3,2,1,0:T(8,128)S(1)} %get-tuple-element.41.r_6_.r_0_, f32[3,18,40,128]{3,2,1,0:T(8,128)S(1)} %get-tuple-element.47.r_1_), custom_call_target="tpu_custom_call" | custom-call | tf_op jit(solution)/shard_map/store/pallas_call | solution.py:489
  33.0 0.3 %collective-permute-done.12.r_3_ = f32[32,128]{1,0:T(8,128)S(1)} collective-permute-done((f32[32,128]{1,0:T(8,128)S(1)}, f32[32,128]{1,0:T(8,128)S(1)}, u32[]{:S(2)}, u32[]{:S(2)}) %collective-permute-start.12) | collective-permute-done | bytes 16416 | tf_op jit(solution)/shard_map/ppermute | solution.py:451
  33.3 0.8 %collective-permute-done.11.r_2_ = f32[32,128]{1,0:T(8,128)S(1)} collective-permute-done((f32[32,128]{1,0:T(8,128)S(1)}, f32[32,128]{1,0:T(8,128)S(1)}, u32[]{:S(2)}, u32[]{:S(2)}) %collective-permute-start.11) | collective-permute-done | bytes 16416 | tf_op jit(solution)/shard_map/ppermute | solution.py:451
  34.1 0.7 %gather_sum.1 = f32[2,8,32]{2,1,0:T(8,128)} custom-call(f32[32,128]{1,0:T(8,128)S(1)} %get-tuple-element.50.r_0_, f32[32,128]{1,0:T(8,128)S(1)} %collective-permute-done.10.r_1_, f32[32,128]{1,0:T(8,128)S(1)} %collective-permute-done.11.r_2_, f32[32,128]{1,0:T(8,128)S(1)} %collective-permute-done.12.r_3_), custom_call_target="tpu_custom_call" | custom-call | tf_op jit(solution)/shard_map/gather_sum/pallas_call | solution.py:491
  (4 shorter events, 0.0 us)
Async XLA Ops:
  0.6 5.2 %copy-start = (f32[2,32,8]{1,2,0:T(8,128)S(1)}, f32[2,32,8]{1,2,0:T(8,128)}, u32[]{:S(2)}) copy-start(f32[2,32,8]{1,2,0:T(8,128)} %param.14) | copy-start | bytes 6148
  0.6 5.2 %collective-permute-start.2 = (f32[2,8,32]{2,1,0:T(8,128)}, f32[2,8,32]{2,1,0:T(8,128)S(1)}, u32[]{:S(2)}, u32[]{:S(2)}) collective-permute-start(f32[2,8,32]{2,1,0:T(8,128)} %bitcast.12), channel_id=1, source_target_pairs={{0,24},{8,16},{16,8},{24,0},{1,25},{9,17},{17,9},{25,1},{2,26},{10... | collective-permute-start | bytes 6152 | tf_op jit(solution)/shard_map/ppermute | solution.py:451
  2.5 3.4 %collective-permute-start.1 = (f32[2,8,32]{2,1,0:T(8,128)}, f32[2,8,32]{2,1,0:T(8,128)S(1)}, u32[]{:S(2)}, u32[]{:S(2)}) collective-permute-start(f32[2,8,32]{2,1,0:T(8,128)} %bitcast.13), channel_id=1, source_target_pairs={{0,16},{8,24},{16,0},{24,8},{1,17},{9,25},{17,1},{25,9},{2,18},{10... | collective-permute-start | bytes 6152 | tf_op jit(solution)/shard_map/ppermute | solution.py:451
  2.7 3.1 %collective-permute-start = (f32[2,8,32]{2,1,0:T(8,128)}, f32[2,8,32]{2,1,0:T(8,128)S(1)}, u32[]{:S(2)}, u32[]{:S(2)}) collective-permute-start(f32[2,8,32]{2,1,0:T(8,128)} %bitcast.14), channel_id=1, source_target_pairs={{0,8},{8,0},{16,24},{24,16},{1,9},{9,1},{17,25},{25,17},{2,10},{10... | collective-permute-start | bytes 6152 | tf_op jit(solution)/shard_map/ppermute | solution.py:451
  3.6 0.7 %copy-start.1 = (f32[1,32,8]{1,2,0:T(8,128)S(1)}, f32[1,32,8]{1,2,0:T(8,128)}, u32[]{:S(2)}) copy-start(f32[1,32,8]{1,2,0:T(8,128)} %param.15) | copy-start | bytes 3076
  7.2 8.8 %collective-permute-start.6 = (f32[18,8,128]{2,1,0:T(8,128)S(1)}, f32[18,8,128]{2,1,0:T(8,128)S(1)}, u32[]{:S(2)}, u32[]{:S(2)}) collective-permute-start(f32[18,8,128]{2,1,0:T(8,128)S(1)} %get-tuple-element.39), channel_id=1, source_target_pairs={{0,5},{1,4},{2,7},{3,6},{4,1},{5,0},{6,3},{7,2},{8,13},{9,12},{10,... | collective-permute-start | bytes 221192 | tf_op jit(solution)/shard_map/ppermute | solution.py:32
  8.4 7.8 %collective-permute-start.7 = (f32[18,8,128]{2,1,0:T(8,128)S(1)}, f32[18,8,128]{2,1,0:T(8,128)S(1)}, u32[]{:S(2)}, u32[]{:S(2)}) collective-permute-start(f32[18,8,128]{2,1,0:T(8,128)S(1)} %get-tuple-element.40), channel_id=1, source_target_pairs={{1,6},{2,5},{5,2},{6,1},{9,14},{10,13},{13,10},{14,9},{17,22},{18,... | collective-permute-start | bytes 221192 | tf_op jit(solution)/shard_map/ppermute | solution.py:32
  12.6 8.5 %collective-permute-start.3 = (f32[17,32,128]{2,1,0:T(8,128)S(1)}, f32[17,32,128]{2,1,0:T(8,128)S(1)}, u32[]{:S(2)}, u32[]{:S(2)}) collective-permute-start(f32[17,32,128]{2,1,0:T(8,128)S(1)} %get-tuple-element.36), channel_id=1, source_target_pairs={{0,1},{1,0},{2,3},{3,2},{4,5},{5,4},{6,7},{7,6},{8,9},{9,8},{10,11... | collective-permute-start | bytes 835592 | tf_op jit(solution)/shard_map/ppermute | solution.py:32
  12.7 9.2 %collective-permute-start.4 = (f32[17,32,128]{2,1,0:T(8,128)S(1)}, f32[17,32,128]{2,1,0:T(8,128)S(1)}, u32[]{:S(2)}, u32[]{:S(2)}) collective-permute-start(f32[17,32,128]{2,1,0:T(8,128)S(1)} %get-tuple-element.37), channel_id=1, source_target_pairs={{1,2},{2,1},{5,6},{6,5},{9,10},{10,9},{13,14},{14,13},{17,18},{18,... | collective-permute-start | bytes 835592 | tf_op jit(solution)/shard_map/ppermute | solution.py:32
  14.7 6.4 %collective-permute-start.5 = (f32[57,8,128]{2,1,0:T(8,128)S(1)}, f32[57,8,128]{2,1,0:T(8,128)S(1)}, u32[]{:S(2)}, u32[]{:S(2)}) collective-permute-start(f32[57,8,128]{2,1,0:T(8,128)S(1)} %get-tuple-element.38), channel_id=1, source_target_pairs={{0,4},{1,5},{2,6},{3,7},{4,0},{5,1},{6,2},{7,3},{8,12},{9,13},{10,... | collective-permute-start | bytes 700424 | tf_op jit(solution)/shard_map/ppermute | solution.py:32
  16.0 9.0 %collective-permute-start.8 = (f32[14,32,128]{2,1,0:T(8,128)S(1)}, f32[14,32,128]{2,1,0:T(8,128)S(1)}, u32[]{:S(2)}, u32[]{:S(2)}) collective-permute-start(f32[14,32,128]{2,1,0:T(8,128)S(1)} %get-tuple-element.45), channel_id=1, source_target_pairs={{0,1},{1,0},{2,3},{3,2},{4,5},{5,4},{6,7},{7,6},{8,9},{9,8},{10,11... | collective-permute-start | bytes 688136 | tf_op jit(solution)/shard_map/ppermute | solution.py:32
  16.2 10.7 %collective-permute-start.9 = (f32[14,32,128]{2,1,0:T(8,128)S(1)}, f32[14,32,128]{2,1,0:T(8,128)S(1)}, u32[]{:S(2)}, u32[]{:S(2)}) collective-permute-start(f32[14,32,128]{2,1,0:T(8,128)S(1)} %get-tuple-element.46), channel_id=1, source_target_pairs={{1,2},{2,1},{5,6},{6,5},{9,10},{10,9},{13,14},{14,13},{17,18},{18,... | collective-permute-start | bytes 688136 | tf_op jit(solution)/shard_map/ppermute | solution.py:32
  28.7 4.6 %collective-permute-start.12 = (f32[32,128]{1,0:T(8,128)S(1)}, f32[32,128]{1,0:T(8,128)S(1)}, u32[]{:S(2)}, u32[]{:S(2)}) collective-permute-start(f32[32,128]{1,0:T(8,128)S(1)} %get-tuple-element.50.r_0_), channel_id=1, source_target_pairs={{0,24},{8,16},{16,8},{24,0},{1,25},{9,17},{17,9},{25,1},{2,26},{10... | collective-permute-start | bytes 49160 | tf_op jit(solution)/shard_map/ppermute | solution.py:451
  31.5 2.6 %collective-permute-start.11 = (f32[32,128]{1,0:T(8,128)S(1)}, f32[32,128]{1,0:T(8,128)S(1)}, u32[]{:S(2)}, u32[]{:S(2)}) collective-permute-start(f32[32,128]{1,0:T(8,128)S(1)} %get-tuple-element.50.r_0_), channel_id=1, source_target_pairs={{0,16},{8,24},{16,0},{24,8},{1,17},{9,25},{17,1},{25,9},{2,18},{10... | collective-permute-start | bytes 49160 | tf_op jit(solution)/shard_map/ppermute | solution.py:451
  31.8 2.2 %collective-permute-start.10 = (f32[32,128]{1,0:T(8,128)S(1)}, f32[32,128]{1,0:T(8,128)S(1)}, u32[]{:S(2)}, u32[]{:S(2)}) collective-permute-start(f32[32,128]{1,0:T(8,128)S(1)} %get-tuple-element.50.r_0_), channel_id=1, source_target_pairs={{0,8},{8,0},{16,24},{24,16},{1,9},{9,1},{17,25},{25,17},{2,10},{10... | collective-permute-start | bytes 49160 | tf_op jit(solution)/shard_map/ppermute | solution.py:451
